TPU v7x, 128 devices: a whole 4x4x4 slice. The times are simulated.
128 devices in a mesh: grp: 32 (over y, x, core), mem: 4 (over z).
Axes of the slice: x: 4, y: 4, z: 4, core: 2. Of those that a mesh axis runs over, the one named last changes fastest.
Arguments:
- incident: bfloat16 [2, 256, 65536], P(None, None, ('grp', 'mem')), may hold values from -6 to 6
- near_blocks: bfloat16 [256, 3, 2, 256, 256], P(('grp', 'mem')), may hold values from -0.15625 to 0.15625
- near_mask: int32 [256, 3], P(('grp', 'mem')), may hold values 0 or 1
- far_source: int32 [32, 14], replicated, may hold values from 0 to 31
- far_rank: int32 [32, 14], P('grp'), may hold values from 32 to 128
- basis_in: bfloat16 [32, 4, 14, 2, 128, 512], P('grp', 'mem'), may hold values from -0.1875 to 0.1875
- section_one: bfloat16 [32, 4, 14, 2, 128, 256], P('grp', 'mem'), may hold values from -0.25 to 0.25
- section_two: bfloat16 [32, 4, 14, 2, 128, 256], P('grp', 'mem'), may hold values from -0.25 to 0.25
- basis_out: bfloat16 [32, 4, 14, 2, 2048, 128], P('grp', 'mem'), may hold values from -0.0625 to 0.0625
Outputs:
- product: bfloat16 [2, 256, 65536], P(None, None, ('grp', 'mem'))
Inputs may be any that keep to these rules, and one draw needn't show every extreme that they name: far_source names the cluster whose coefficients feed each far-field block; clusters may repeat. far_rank gives the number of live rank components of each block. `near_mask`: 1 marks a present near-field block.
All inputs are finite; a program needn't handle non-finite values.
Results may differ from a plain program's by a relative error of at most 0.0053.
Values may be sent and summed in bfloat16 or wider, within the bound.
No kernel may reach another device: no remote copies, remote signals or barrier semaphores. Data moves between devices by JAX's collectives and lax.ppermute only.
A program may use at most 128 MiB of HBM per device.

v0:
```python
import functools

import jax
import jax.numpy as jnp
from jax import lax
from jax.experimental import pallas as pl
from jax.experimental.pallas import tpu as pltpu
from jax.sharding import PartitionSpec as P


F32 = jnp.float32
BF16 = jnp.bfloat16
SIDE = 4
SHIFT = {"x": 1, "y": 3}


def swap(value, axis, mask):
    return lax.ppermute(value, axis, [(i, i ^ mask) for i in range(lax.axis_size(axis))])


def ring(value, axis, by):
    at = SHIFT[axis]
    perm = []
    for i in range(lax.axis_size("grp")):
        v = (i >> at) & (SIDE - 1)
        perm.append((i, i + ((((v + by) % SIDE) - v) << at)))
    return lax.ppermute(value, "grp", perm)


def nt(left, right):
    return lax.dot_general(left, right, (((1,), (1,)), ((), ())), preferred_element_type=F32)


VMEM = pl.BlockSpec(memory_space=pltpu.VMEM)
SMEM = pl.BlockSpec(memory_space=pltpu.SMEM)


def size(v):
    return v.size * v.dtype.itemsize


def call(body, scalars, arrays, out_shape, flops, nbytes, scratch=(), space=None, room=0):
    space = space or [pltpu.VMEM] * len(arrays)
    inside = [v for v, at in zip(arrays, space) if at == pltpu.VMEM]
    room += sum(size(v) for v in jax.tree.leaves(out_shape) + inside) + (2 << 20)
    return pl.pallas_call(
        body,
        in_specs=[SMEM] * len(scalars) + [pl.BlockSpec(memory_space=at) for at in space],
        out_specs=jax.tree.map(lambda _: VMEM, out_shape),
        out_shape=out_shape,
        scratch_shapes=scratch,
        compiler_params=pltpu.CompilerParams(vmem_limit_bytes=room),
        cost_estimate=pl.CostEstimate(flops=flops, bytes_accessed=nbytes, transcendentals=0),
    )(
        *scalars,
        *(
            pltpu.with_memory_space_constraint(v, at) if at == pltpu.HBM else v
            for v, at in zip(arrays, space)
        ),
    )


def near_body(mask, x, low, high, blocks, out):
    nrhs = x.shape[1]
    leaf = blocks.shape[-1]
    rows = nrhs // 4

    def step(t, carry):
        at = pl.ds(pl.multiple_of(t * rows, rows), rows)
        seq = [low[:, at, :]]
        seq += [x[:, at, i * leaf : (i + 1) * leaf] for i in range(2)]
        seq += [high[:, at, :]]
        seq = [v.reshape(2 * rows, leaf) for v in seq]
        for i in range(2):
            real = jnp.zeros((rows, leaf), F32)
            imag = jnp.zeros((rows, leaf), F32)
            for j in range(3):
                p = nt(seq[i + j], blocks[i, j].reshape(2 * leaf, leaf))
                w = mask[i, j].astype(F32)
                real += w * (p[:rows, :leaf] - p[rows:, leaf:])
                imag += w * (p[rows:, :leaf] + p[:rows, leaf:])
            out[0, at, i * leaf : (i + 1) * leaf] = real
            out[1, at, i * leaf : (i + 1) * leaf] = imag
        return carry

    lax.fori_loop(0, 4, step, 0)


def near_field(mask, x, low, high, blocks):
    _, nrhs, rows = x.shape
    leaf = blocks.shape[-1]
    return call(
        near_body, [mask], [x, low, high, blocks],
        jax.ShapeDtypeStruct((2, nrhs, rows), F32),
        8 * nrhs * 6 * leaf * leaf, 4 << 20,
    )


def level0_body(color, base, count, src, gidx, rank, *refs):
    bufs, w, out = refs[:16], refs[16], refs[17]
    xs, ws, sems = refs[18:]
    me = gidx[0]
    k = w.shape[-2]
    n = xs.shape[2]

    def fetch(i, carry):
        f = i + base
        s = src[me, f]
        dx = (((s >> 1) & 3) - ((me >> 1) & 3)) & 3
        dy = (((s >> 3) & 3) - ((me >> 3) & 3)) & 3
        dx, dy = (jnp.where(v == 0, 0, jnp.where(v == 3, 1, v + 1)) for v in (dx, dy))
        first, second = (dx, dy) if color == 0 else (dy, dx)
        which = 2 * second + (first >> 1) + 8 * ((s ^ me) & 1)
        for t in range(16):

            @pl.when(which == t)
            def _():
                pltpu.make_async_copy(bufs[t].at[first & 1], xs.at[i], sems.at[0, i]).start()

        pltpu.make_async_copy(w.at[0, 0, f], ws.at[i], sems.at[1, i]).start()
        return carry

    lax.fori_loop(0, count, fetch, 0)
    for i in range(count):
        pltpu.make_async_copy(bufs[0].at[0], xs.at[i], sems.at[0, i]).wait()
        pltpu.make_async_copy(w.at[0, 0, 0], ws.at[i], sems.at[1, i]).wait()
        p = nt(xs[i].reshape(2 * n, xs.shape[3]), ws[i].reshape(2 * k, ws.shape[3]))
        live = lax.broadcasted_iota(jnp.int32, (n, k), 1) < rank[0, base + i]
        out[i, 0], out[i, 1] = combine(p, n, k, live)


def level0(color, base, count, src, gidx, rank, bufs, w):
    _, _, n, rows = bufs[0].shape
    k = w.shape[-2]
    return call(
        functools.partial(level0_body, color, base, count),
        [src, gidx, rank], [*bufs, w],
        jax.ShapeDtypeStruct((count, 2, n, k), BF16),
        8 * count * n * k * rows, 4 << 20,
        [
            pltpu.VMEM((count, 2, n, rows), BF16),
            pltpu.VMEM((count, 2, k, rows), BF16),
            pltpu.SemaphoreType.DMA((2, count)),
        ],
        space=[pltpu.HBM] * 17,
        room=count * 2 * rows * (n + k) * 2,
    )


def combine(p, n, k, live):
    zero = jnp.zeros((n, k), F32)
    real = jnp.where(live, p[:n, :k] - p[n:, k:], zero).astype(BF16)
    imag = jnp.where(live, p[n:, :k] + p[:n, k:], zero).astype(BF16)
    return real, imag


def section_body(base, bit, rank, own, other, *refs):
    half = len(refs) // 2
    ws, outs = refs[:half], refs[half:]
    count, _, n, k = own.shape
    upper = bit[0] == 1
    for i in range(count):
        a = own[i].reshape(2 * n, k)
        b = other[i].reshape(2 * n, k)
        x = jnp.concatenate([jnp.where(upper, b, a), jnp.where(upper, a, b)], axis=1)
        live = lax.broadcasted_iota(jnp.int32, (n, k), 1) < rank[0, base + i]
        for w, out in zip(ws, outs):
            p = nt(x, w[0, 0, base + i].reshape(2 * k, 2 * k))
            out[i, 0], out[i, 1] = combine(p, n, k, live)


def section(base, bit, rank, own, other, ws):
    count, _, n, k = own.shape
    shape = jax.ShapeDtypeStruct(own.shape, BF16)
    return call(
        functools.partial(section_body, base),
        [bit, rank], [own, other, *ws], [shape] * len(ws),
        16 * count * n * k * k * len(ws), 2 << 20,
    )


def outward_body(dtype, order, *refs):
    levels, w, out, xs, ws, sems = refs[:-5], refs[-5], refs[-4], refs[-3], refs[-2], refs[-1]
    n = xs.shape[1] // 2
    blocks, step = ws.shape[0], ws.shape[3]
    piece = out.shape[3]
    per = piece // step

    def copy(b):
        start = pl.multiple_of(order[b // per] * piece + (b % per) * step, step)
        return pltpu.make_async_copy(w.at[0, 0, :, :, pl.ds(start, step)], ws.at[b], sems.at[b])

    copy(0).start()
    copy(1).start()
    f = 0
    for level in levels:
        for i in range(level.shape[0]):
            real, imag = level[i, 0], level[i, 1]
            xs[f, :n] = jnp.concatenate([real, -imag], 1)
            xs[f, n:] = jnp.concatenate([imag, real], 1)
            f += 1

    def body(b, carry):
        copy(b).wait()

        @pl.when(b + 2 < blocks)
        def _():
            copy(b + 2).start()

        acc = jnp.zeros((2 * n, step), F32)
        for f in range(xs.shape[0]):
            acc += nt(xs[f], jnp.concatenate([ws[b, f, 0], ws[b, f, 1]], 1))
        to = pl.ds(pl.multiple_of((b % per) * step, step), step)
        out[b // per, 0, :, to] = acc[:n].astype(dtype)
        out[b // per, 1, :, to] = acc[n:].astype(dtype)
        return carry

    lax.fori_loop(0, blocks, body, 0)


def outward(dtype, order, levels, w, step=256):
    _, _, n, k = levels[0].shape
    far = w.shape[2]
    piece = w.shape[4] // 4
    count = order.shape[0]
    blocks = count * piece // step
    return call(
        functools.partial(outward_body, dtype),
        [order], [*levels, w],
        jax.ShapeDtypeStruct((count, 2, n, piece), dtype),
        8 * far * n * k * piece * count, 4 << 20,
        [
            pltpu.VMEM((far, 2 * n, 2 * k), BF16),
            pltpu.VMEM((blocks, far, 2, step, k), BF16),
            pltpu.SemaphoreType.DMA((blocks,)),
        ],
        space=[pltpu.VMEM] * len(levels) + [pltpu.HBM],
        room=far * n * k * 8 + blocks * far * step * k * 4,
    )


def gather(color, block):
    one, two = ("x", "y") if color == 0 else ("y", "x")
    below = ring(block, one, 1)
    above = ring(block, one, -1)
    far_r = ring(below[:, :1], one, 1)
    far_i = ring(above[:, 1:], one, -1)
    lo = jnp.concatenate([block, below], 0)
    hi = jnp.concatenate([above, jnp.concatenate([far_r, far_i], 1)], 0)
    below_lo = ring(lo, two, 1)
    above_hi = ring(hi, two, -1)
    below_hi = ring(hi, two, 1)
    above_lo = ring(lo, two, -1)
    far_lo = ring(below_lo, two, 1)
    far_hi = ring(above_hi, two, -1)
    mine = [lo, hi, below_lo, below_hi, above_lo, above_hi, far_lo, far_hi]
    return mine + [swap(v, "grp", 1) for v in mine]


def on_device(
    incident,
    near_blocks,
    near_mask,
    far_source,
    far_rank,
    basis_in,
    section_one,
    section_two,
    basis_out,
):
    _, nrhs, rows = incident.shape
    leaf = near_blocks.shape[3]
    far = basis_in.shape[2]
    q = nrhs // 4
    member = lax.axis_index("mem")
    gidx = lax.axis_index("grp").reshape(1).astype(jnp.int32)

    bufs = [gather(c, incident[None, :, 2 * c * q : 2 * (c + 1) * q]) for c in range(2)]
    section_pair = swap(section_one, "mem", 1)

    axes = ("grp", "mem")
    total = lax.axis_size("grp") * lax.axis_size("mem")
    forward = [(i, i + 1) for i in range(total - 1)]
    backward = [(i + 1, i) for i in range(total - 1)]
    low = lax.ppermute(incident[:, :, rows - leaf :], axes, forward)
    high = lax.ppermute(incident[:, :, :leaf], axes, backward)
    near = near_field(near_mask, incident, low, high, near_blocks)

    bit0 = (member & 1).reshape(1).astype(jnp.int32)
    bit1 = (member >> 1).reshape(1).astype(jnp.int32)
    far_near = jnp.array([2, 1, 3, 0], jnp.int32)
    cut = far // 2
    spans = ((0, cut), (cut, far - cut))

    pieces = []
    for h in range(2):
        two = []
        for base, count in spans:
            lev0 = level0(h, base, count, far_source, gidx, far_rank, bufs[h], basis_in)
            lev0_pair = swap(lev0, "mem", 1)
            lev1, lev1_pair = section(
                base, bit0, far_rank, lev0, lev0_pair, [section_one, section_pair]
            )
            lev1_other = swap(lev1_pair, "mem", 3)
            two += section(base, bit1, far_rank, lev1, lev1_other, [section_two])
        if h == 0:
            sent = outward(BF16, member ^ far_near[:2], two, basis_out)
            sent = swap(sent, "mem", 1)
            sent = (sent[0], sent[1])
        else:
            sent = []
            for i in range(2):
                part = outward(BF16, member ^ far_near[i : i + 1], two, basis_out)
                sent.append(swap(part, "mem", 1)[0])
        other = outward(F32, member ^ far_near[2:3], two, basis_out)[0]
        last = swap((other + sent[0].astype(F32)).astype(BF16), "mem", 3)
        kept = outward(F32, member ^ far_near[3:], two, basis_out)[0]
        at = slice(2 * h * q, 2 * (h + 1) * q)
        pieces.append((kept + sent[1].astype(F32) + last.astype(F32) + near[:, at]).astype(BF16))
    return jnp.concatenate(pieces, 1)


def solution(mesh):
    placed = (
        P(None, None, ("grp", "mem")),
        P(("grp", "mem"), None, None, None, None),
        P(("grp", "mem"), None),
        P(),
        P("grp", None),
        P("grp", "mem", None, None, None, None),
        P("grp", "mem", None, None, None, None),
        P("grp", "mem", None, None, None, None),
        P("grp", "mem", None, None, None, None),
    )

    return jax.shard_map(
        on_device,
        mesh=mesh,
        in_specs=placed,
        out_specs=P(None, None, ("grp", "mem")),
        check_vma=False,
    )
```

profile of v0, /device:TPU:7, one launch (start us, length us, event | category | flops | bytes accessed | tf_op | source)
XLA Modules:
  0.0 195.6 jit_solution(767290451735932051)
XLA Ops:
  5.1 4.6 %collective-permute-done.27 = bf16[1,2,128,512]{3,2,1,0:T(8,128)(2,1)S(1)} collective-permute-done((bf16[1,2,128,512]{3,2,1,0:T(8,128)(2,1)S(1)}, bf16[1,2,128,512]{3,2,1,0:T(8,128)(2,1)S(1)}, u32[]{:S(2)}, u32[]{:S(2)}) %collective-permute-start.27) | collective-permute-done | bytes 262176 | tf_op jit(solution)/shard_map/ppermute | solution.py:27
  15.6 3.4 %collective-permute-done.28 = bf16[1,2,128,512]{3,2,1,0:T(8,128)(2,1)S(1)} collective-permute-done((bf16[1,2,128,512]{3,2,1,0:T(8,128)(2,1)S(1)}, bf16[1,2,128,512]{3,2,1,0:T(8,128)(2,1)S(1)}, u32[]{:S(2)}, u32[]{:S(2)}) %collective-permute-start.28) | collective-permute-done | bytes 262176 | tf_op jit(solution)/shard_map/ppermute | solution.py:27
  29.8 2.9 %collective-permute-start.38 = (bf16[2,2,128,512]{3,2,1,0:T(8,128)(2,1)S(1)}, bf16[2,2,128,512]{3,2,1,0:T(8,128)(2,1)S(1)}, u32[]{:S(2)}, u32[]{:S(2)}) collective-permute-start(bf16[2,2,128,512]{3,2,1,0:T(8,128)(2,1)S(1)} %maximum_maximum_fusion.1.refs_1_), channel_id=1, source_target_pairs={{0,4},{4,0},{8,12},{12,8},{16,20},{20,16},{24,28},{28,24},{32,36},... | collective-permute-start | bytes 1572872 | tf_op jit(solution)/shard_map/ppermute | solution.py:18
  46.9 2.9 %collective-permute-start.41 = (bf16[2,2,128,512]{3,2,1,0:T(8,128)(2,1)S(1)}, bf16[2,2,128,512]{3,2,1,0:T(8,128)(2,1)S(1)}, u32[]{:S(2)}, u32[]{:S(2)}) collective-permute-start(bf16[2,2,128,512]{3,2,1,0:T(8,128)(2,1)S(1)} %collective-permute-done.33.refs_4_), channel_id=1, source_target_pairs={{0,4},{4,0},{8,12},{12,8},{16,20},{20,16},{24,28},{28,24},{32,36},... | collective-permute-start | bytes 1572872 | tf_op jit(solution)/shard_map/ppermute | solution.py:18
  50.0 3.3 %collective-permute-start.35 = (bf16[2,2,128,512]{3,2,1,0:T(8,128)(2,1)S(1)}, bf16[2,2,128,512]{3,2,1,0:T(8,128)(2,1)}, u32[]{:S(2)}, u32[]{:S(2)}) collective-permute-start(bf16[2,2,128,512]{3,2,1,0:T(8,128)(2,1)S(1)} %collective-permute-done.31.refs_2_), channel_id=1, source_target_pairs={{0,8},{4,12},{8,16},{12,20},{16,24},{20,28},{24,0},{28,4},{32,40},... | collective-permute-start | bytes 1572872 | tf_op jit(solution)/shard_map/ppermute | solution.py:27
  66.4 8.4 %collective-permute-done.8.refs_6_ = bf16[2,2,128,512]{3,2,1,0:T(8,128)(2,1)S(1)} collective-permute-done((bf16[2,2,128,512]{3,2,1,0:T(8,128)(2,1)S(1)}, bf16[2,2,128,512]{3,2,1,0:T(8,128)(2,1)S(1)}, u32[]{:S(2)}, u32[]{:S(2)}) %collective-permute-start.8) | collective-permute-done | bytes 524320 | tf_op jit(solution)/shard_map/ppermute | solution.py:27
  75.6 4.1 %collective-permute-done.36.refs_7_ = bf16[2,2,128,512]{3,2,1,0:T(8,128)(2,1)} collective-permute-done((bf16[2,2,128,512]{3,2,1,0:T(8,128)(2,1)}, bf16[2,2,128,512]{3,2,1,0:T(8,128)(2,1)}, u32[]{:S(2)}, u32[]{:S(2)}) %collective-permute-start.36) | collective-permute-done | bytes 524320 | tf_op jit(solution)/shard_map/ppermute | solution.py:27
  84.4 4.2 %shard_map.103.own = bf16[7,2,128,128]{3,2,1,0:T(8,128)(2,1)S(1)} custom-call(s32[32,14]{1,0:T(8,128)S(1)} %copy.11.src, s32[1]{0:T(128)} %bitcast.3.gidx, s32[1,14]{1,0:T(1,128)S(1)} %copy-done.8, bf16[2,2,128,512]{3,2,1,0:T(8,128)(2,1)} %copy-done.12, bf16[2,2,128,512]{3,2,1,0:T(8,128)(2,1)} %copy-done.13, bf16[2,2,128,512]{3,2,1,0:T(8,128)(2,1)} %copy-done.20, ...), custom_call_target="tpu_custom_call" | custom-call | flops 469762048 | bytes 4194304 | tf_op jit(solution)/shard_map/pallas_call | solution.py:46
  90.4 4.2 %shard_map.100.own = bf16[7,2,128,128]{3,2,1,0:T(8,128)(2,1)S(1)} custom-call(s32[32,14]{1,0:T(8,128)S(1)} %copy.11.src, s32[1]{0:T(128)} %bitcast.3.gidx, s32[1,14]{1,0:T(1,128)S(1)} %copy-done.8, bf16[2,2,128,512]{3,2,1,0:T(8,128)(2,1)} %copy-done.12, bf16[2,2,128,512]{3,2,1,0:T(8,128)(2,1)} %copy-done.13, bf16[2,2,128,512]{3,2,1,0:T(8,128)(2,1)} %copy-done.20, ...), custom_call_target="tpu_custom_call" | custom-call | flops 469762048 | bytes 4194304 | tf_op jit(solution)/shard_map/pallas_call | solution.py:46
  94.7 5.0 %shard_map.110.own = bf16[7,2,128,128]{3,2,1,0:T(8,128)(2,1)} custom-call(s32[32,14]{1,0:T(8,128)S(1)} %copy.11.src, s32[1]{0:T(128)} %bitcast.3.gidx, s32[1,14]{1,0:T(1,128)S(1)} %copy-done.8, bf16[2,2,128,512]{3,2,1,0:T(8,128)(2,1)} %copy-done.10, bf16[2,2,128,512]{3,2,1,0:T(8,128)(2,1)} %copy-done.11, bf16[2,2,128,512]{3,2,1,0:T(8,128)(2,1)} %copy-done.16, ...), custom_call_target="tpu_custom_call" | custom-call | flops 469762048 | bytes 4194304 | tf_op jit(solution)/shard_map/pallas_call | solution.py:46
  101.2 4.2 %shard_map.113.own = bf16[7,2,128,128]{3,2,1,0:T(8,128)(2,1)S(1)} custom-call(s32[32,14]{1,0:T(8,128)S(1)} %copy.11.src, s32[1]{0:T(128)} %bitcast.3.gidx, s32[1,14]{1,0:T(1,128)S(1)} %copy-done.8, bf16[2,2,128,512]{3,2,1,0:T(8,128)(2,1)} %copy-done.10, bf16[2,2,128,512]{3,2,1,0:T(8,128)(2,1)} %copy-done.11, bf16[2,2,128,512]{3,2,1,0:T(8,128)(2,1)} %copy-done.16, ...), custom_call_target="tpu_custom_call" | custom-call | flops 469762048 | bytes 4194304 | tf_op jit(solution)/shard_map/pallas_call | solution.py:46
  105.5 6.5 %collective-permute-done.21.other = bf16[7,2,128,128]{3,2,1,0:T(8,128)(2,1)} collective-permute-done((bf16[7,2,128,128]{3,2,1,0:T(8,128)(2,1)S(1)}, bf16[7,2,128,128]{3,2,1,0:T(8,128)(2,1)}, u32[]{:S(2)}, u32[]{:S(2)}) %collective-permute-start.21) | collective-permute-done | bytes 458784 | tf_op jit(solution)/shard_map/ppermute | solution.py:18
  112.0 3.1 %shard_map.104 = (bf16[7,2,128,128]{3,2,1,0:T(8,128)(2,1)S(1)}, bf16[7,2,128,128]{3,2,1,0:T(8,128)(2,1)}) custom-call(s32[1]{0:T(128)} %bitcast.2.bit, s32[1,14]{1,0:T(1,128)S(1)} %copy-done.8, bf16[7,2,128,128]{3,2,1,0:T(8,128)(2,1)S(1)} %shard_map.103.own, bf16[7,2,128,128]{3,2,1,0:T(8,128)(2,1)} %collective-permute-done.21.other, ...), custom_call_target="tpu_custom_call" | custom-call | flops 469762048 | bytes 2097152 | tf_op jit(solution)/shard_map/pallas_call | solution.py:46
  115.9 3.4 %collective-permute-start.22 = (bf16[7,2,128,128]{3,2,1,0:T(8,128)(2,1)}, bf16[7,2,128,128]{3,2,1,0:T(8,128)(2,1)}, u32[]{:S(2)}, u32[]{:S(2)}) collective-permute-start(bf16[7,2,128,128]{3,2,1,0:T(8,128)(2,1)} %get-tuple-element.16), channel_id=1, source_target_pairs={{0,3},{1,2},{2,1},{3,0},{4,7},{5,6},{6,5},{7,4},{8,11},{9,10},{10,... | collective-permute-start | bytes 1376264 | tf_op jit(solution)/shard_map/ppermute | solution.py:18
  121.8 3.1 %shard_map.101 = (bf16[7,2,128,128]{3,2,1,0:T(8,128)(2,1)S(1)}, bf16[7,2,128,128]{3,2,1,0:T(8,128)(2,1)}) custom-call(s32[1]{0:T(128)} %bitcast.2.bit, s32[1,14]{1,0:T(1,128)S(1)} %copy-done.8, bf16[7,2,128,128]{3,2,1,0:T(8,128)(2,1)S(1)} %shard_map.100.own, bf16[7,2,128,128]{3,2,1,0:T(8,128)(2,1)} %collective-permute-done.18.other, ...), custom_call_target="tpu_custom_call" | custom-call | flops 469762048 | bytes 2097152 | tf_op jit(solution)/shard_map/pallas_call | solution.py:46
  125.7 3.4 %collective-permute-start.20 = (bf16[7,2,128,128]{3,2,1,0:T(8,128)(2,1)}, bf16[7,2,128,128]{3,2,1,0:T(8,128)(2,1)S(1)}, u32[]{:S(2)}, u32[]{:S(2)}) collective-permute-start(bf16[7,2,128,128]{3,2,1,0:T(8,128)(2,1)} %get-tuple-element.14), channel_id=1, source_target_pairs={{0,3},{1,2},{2,1},{3,0},{4,7},{5,6},{6,5},{7,4},{8,11},{9,10},{10,... | collective-permute-start | bytes 1376264 | tf_op jit(solution)/shard_map/ppermute | solution.py:18
  129.9 3.3 %collective-permute-start.26 = (bf16[2,256,256]{2,1,0:T(8,128)(2,1)}, bf16[2,256,256]{2,1,0:T(8,128)(2,1)S(1)}, u32[]{:S(2)}, u32[]{:S(2)}) collective-permute-start(bf16[2,256,256]{2,1,0:T(8,128)(2,1)} %get-tuple-element.25), channel_id=1, source_target_pairs={{1,0},{2,1},{3,2},{4,3},{5,4},{6,5},{7,6},{8,7},{9,8},{10,9},{11,1... | collective-permute-start | bytes 786440 | tf_op jit(solution)/shard_map/ppermute | solution.py:286
  137.6 3.8 %collective-permute-done.47.other = bf16[7,2,128,128]{3,2,1,0:T(8,128)(2,1)} collective-permute-done((bf16[7,2,128,128]{3,2,1,0:T(8,128)(2,1)S(1)}, bf16[7,2,128,128]{3,2,1,0:T(8,128)(2,1)}, u32[]{:S(2)}, u32[]{:S(2)}) %collective-permute-start.47) | collective-permute-done | bytes 458784 | tf_op jit(solution)/shard_map/ppermute | solution.py:18
  143.8 3.5 %collective-permute-start.48 = (bf16[7,2,128,128]{3,2,1,0:T(8,128)(2,1)S(1)}, bf16[7,2,128,128]{3,2,1,0:T(8,128)(2,1)S(1)}, u32[]{:S(2)}, u32[]{:S(2)}) collective-permute-start(bf16[7,2,128,128]{3,2,1,0:T(8,128)(2,1)S(1)} %get-tuple-element.20), channel_id=1, source_target_pairs={{0,3},{1,2},{2,1},{3,0},{4,7},{5,6},{6,5},{7,4},{8,11},{9,10},{10,... | collective-permute-start | bytes 1376264 | tf_op jit(solution)/shard_map/ppermute | solution.py:18
  151.8 5.1 %shard_map.107 = bf16[2,2,128,512]{3,2,1,0:T(8,128)(2,1)S(1)} custom-call(s32[2]{0:T(128)S(1)} %broadcast_xor_fusion.order, bf16[7,2,128,128]{3,2,1,0:T(8,128)(2,1)S(1)} %shard_map.102.refs_0_, bf16[7,2,128,128]{3,2,1,0:T(8,128)(2,1)S(1)} %shard_map.105.refs_1_, bf16[1,1,14,2,2048,128]{5,4,3,2,1,0:T(8,128)(2,1)} %refs_2_.13), custom_call_target="tpu_custom_call" | custom-call | flops 1879048192 | bytes 4194304 | tf_op jit(solution)/shard_map/pallas_call | solution.py:46
  158.2 6.8 %collective-permute-done.48.other = bf16[7,2,128,128]{3,2,1,0:T(8,128)(2,1)S(1)} collective-permute-done((bf16[7,2,128,128]{3,2,1,0:T(8,128)(2,1)S(1)}, bf16[7,2,128,128]{3,2,1,0:T(8,128)(2,1)S(1)}, u32[]{:S(2)}, u32[]{:S(2)}) %collective-permute-start.48) | collective-permute-done | bytes 458784 | tf_op jit(solution)/shard_map/ppermute | solution.py:18
  165.9 2.9 %shard_map.119 = bf16[1,2,128,512]{3,2,1,0:T(8,128)(2,1)S(1)} custom-call(s32[1]{0:T(128)} %bitcast.11.order, bf16[7,2,128,128]{3,2,1,0:T(8,128)(2,1)S(1)} %shard_map.112.refs_0_, bf16[7,2,128,128]{3,2,1,0:T(8,128)(2,1)S(1)} %shard_map.115.refs_1_, bf16[1,1,14,2,2048,128]{5,4,3,2,1,0:T(8,128)(2,1)} %refs_2_.13), custom_call_target="tpu_custom_call" | custom-call | flops 939524096 | bytes 4194304 | tf_op jit(solution)/shard_map/pallas_call | solution.py:46
  179.3 3.2 %collective-permute-start.51 = (bf16[2,128,512]{2,1,0:T(8,128)(2,1)S(1)}, bf16[2,128,512]{2,1,0:T(8,128)(2,1)S(1)}, u32[]{:S(2)}, u32[]{:S(2)}) collective-permute-start(bf16[2,128,512]{2,1,0:T(8,128)(2,1)S(1)} %fusion.3), channel_id=1, source_target_pairs={{0,3},{1,2},{2,1},{3,0},{4,7},{5,6},{6,5},{7,4},{8,11},{9,10},{10,... | collective-permute-start | bytes 786440 | tf_op jit(solution)/shard_map/ppermute | solution.py:18
  182.7 3.2 %shard_map.109 = f32[2,256,512]{2,1,0:T(8,128)S(1)} custom-call(s32[2,3]{1,0:T(2,128)S(1)} %copy-done.9, bf16[2,256,512]{2,1,0:T(8,128)(2,1)S(1)} %copy-done.2, bf16[2,256,256]{2,1,0:T(8,128)(2,1)S(1)} %collective-permute-done.25.low, bf16[2,256,256]{2,1,0:T(8,128)(2,1)S(1)} %collective-permute-done.26.high, bf16[2,3,2,256,256]{4,3,2,1,0:T(8,128)(2,1)S(1)} %copy-done.3), custom_call_target="tpu_custom_call" | custom-call | flops 805306368 | bytes 4194304 | tf_op jit(solution)/shard_map/pallas_call | solution.py:46
  (190 shorter events, 96.6 us)
Async XLA Ops:
  9.7 19.2 %collective-permute-start.37 = (bf16[2,2,128,512]{3,2,1,0:T(8,128)(2,1)S(1)}, bf16[2,2,128,512]{3,2,1,0:T(8,128)(2,1)S(1)}, u32[]{:S(2)}, u32[]{:S(2)}) collective-permute-start(bf16[2,2,128,512]{3,2,1,0:T(8,128)(2,1)S(1)} %pad_maximum_fusion.1.refs_0_), channel_id=1, source_target_pairs={{0,4},{4,0},{8,12},{12,8},{16,20},{20,16},{24,28},{28,24},{32,36},... | collective-permute-start | bytes 1572872 | tf_op jit(solution)/shard_map/ppermute | solution.py:18
  15.6 14.2 %collective-permute-start.33 = (bf16[2,2,128,512]{3,2,1,0:T(8,128)(2,1)S(1)}, bf16[2,2,128,512]{3,2,1,0:T(8,128)(2,1)S(1)}, u32[]{:S(2)}, u32[]{:S(2)}) collective-permute-start(bf16[2,2,128,512]{3,2,1,0:T(8,128)(2,1)S(1)} %pad_maximum_fusion.1.refs_0_), channel_id=1, source_target_pairs={{0,24},{4,28},{8,0},{12,4},{16,8},{20,12},{24,16},{28,20},{32,56},... | collective-permute-start | bytes 1572872 | tf_op jit(solution)/shard_map/ppermute | solution.py:27
  29.7 13.9 %collective-permute-start.4 = (bf16[2,2,128,512]{3,2,1,0:T(8,128)(2,1)S(1)}, bf16[2,2,128,512]{3,2,1,0:T(8,128)(2,1)S(1)}, u32[]{:S(2)}, u32[]{:S(2)}) collective-permute-start(bf16[2,2,128,512]{3,2,1,0:T(8,128)(2,1)S(1)} %pad_maximum_fusion.refs_0_), channel_id=1, source_target_pairs={{0,32},{4,36},{8,40},{12,44},{16,48},{20,52},{24,56},{28,60},{32,6... | collective-permute-start | bytes 1572872 | tf_op jit(solution)/shard_map/ppermute | solution.py:27
  29.8 14.7 %collective-permute-start.38 = (bf16[2,2,128,512]{3,2,1,0:T(8,128)(2,1)S(1)}, bf16[2,2,128,512]{3,2,1,0:T(8,128)(2,1)S(1)}, u32[]{:S(2)}, u32[]{:S(2)}) collective-permute-start(bf16[2,2,128,512]{3,2,1,0:T(8,128)(2,1)S(1)} %maximum_maximum_fusion.1.refs_1_), channel_id=1, source_target_pairs={{0,4},{4,0},{8,12},{12,8},{16,20},{20,16},{24,28},{28,24},{32,36},... | collective-permute-start | bytes 1572872 | tf_op jit(solution)/shard_map/ppermute | solution.py:18
  35.5 14.3 %collective-permute-start.32 = (bf16[2,2,128,512]{3,2,1,0:T(8,128)(2,1)S(1)}, bf16[2,2,128,512]{3,2,1,0:T(8,128)(2,1)}, u32[]{:S(2)}, u32[]{:S(2)}) collective-permute-start(bf16[2,2,128,512]{3,2,1,0:T(8,128)(2,1)S(1)} %maximum_maximum_fusion.1.refs_1_), channel_id=1, source_target_pairs={{0,8},{4,12},{8,16},{12,20},{16,24},{20,28},{24,0},{28,4},{32,40},... | collective-permute-start | bytes 1572872 | tf_op jit(solution)/shard_map/ppermute | solution.py:27
  44.5 13.8 %collective-permute-start.5 = (bf16[2,2,128,512]{3,2,1,0:T(8,128)(2,1)S(1)}, bf16[2,2,128,512]{3,2,1,0:T(8,128)(2,1)S(1)}, u32[]{:S(2)}, u32[]{:S(2)}) collective-permute-start(bf16[2,2,128,512]{3,2,1,0:T(8,128)(2,1)S(1)} %maximum_maximum_fusion.refs_1_), channel_id=1, source_target_pairs={{0,32},{4,36},{8,40},{12,44},{16,48},{20,52},{24,56},{28,60},{32,6... | collective-permute-start | bytes 1572872 | tf_op jit(solution)/shard_map/ppermute | solution.py:27
  50.0 14.5 %collective-permute-start.35 = (bf16[2,2,128,512]{3,2,1,0:T(8,128)(2,1)S(1)}, bf16[2,2,128,512]{3,2,1,0:T(8,128)(2,1)}, u32[]{:S(2)}, u32[]{:S(2)}) collective-permute-start(bf16[2,2,128,512]{3,2,1,0:T(8,128)(2,1)S(1)} %collective-permute-done.31.refs_2_), channel_id=1, source_target_pairs={{0,8},{4,12},{8,16},{12,20},{16,24},{20,28},{24,0},{28,4},{32,40},... | collective-permute-start | bytes 1572872 | tf_op jit(solution)/shard_map/ppermute | solution.py:27
  60.1 14.7 %collective-permute-start.8 = (bf16[2,2,128,512]{3,2,1,0:T(8,128)(2,1)S(1)}, bf16[2,2,128,512]{3,2,1,0:T(8,128)(2,1)S(1)}, u32[]{:S(2)}, u32[]{:S(2)}) collective-permute-start(bf16[2,2,128,512]{3,2,1,0:T(8,128)(2,1)S(1)} %collective-permute-done.4.refs_2_), channel_id=1, source_target_pairs={{0,32},{4,36},{8,40},{12,44},{16,48},{20,52},{24,56},{28,60},{32,6... | collective-permute-start | bytes 1572872 | tf_op jit(solution)/shard_map/ppermute | solution.py:27
  60.1 45.4 %collective-permute-start.19 = (bf16[1,1,14,2,128,256]{5,4,3,2,1,0:T(8,128)(2,1)S(1)}, bf16[1,1,14,2,128,256]{5,4,3,2,1,0:T(8,128)(2,1)}, u32[]{:S(2)}, u32[]{:S(2)}) collective-permute-start(bf16[1,1,14,2,128,256]{5,4,3,2,1,0:T(8,128)(2,1)S(1)} %copy-done), channel_id=1, source_target_pairs={{0,1},{1,0},{2,3},{3,2},{4,5},{5,4},{6,7},{7,6},{8,9},{9,8},{10,11... | collective-permute-start | bytes 5505032 | tf_op jit(solution)/shard_map/ppermute | solution.py:18
  64.5 15.2 %collective-permute-start.36 = (bf16[2,2,128,512]{3,2,1,0:T(8,128)(2,1)}, bf16[2,2,128,512]{3,2,1,0:T(8,128)(2,1)}, u32[]{:S(2)}, u32[]{:S(2)}) collective-permute-start(bf16[2,2,128,512]{3,2,1,0:T(8,128)(2,1)} %collective-permute-done.34.refs_5_), channel_id=1, source_target_pairs={{0,24},{4,28},{8,0},{12,4},{16,8},{20,12},{24,16},{28,20},{32,56},... | collective-permute-start | bytes 1572872 | tf_op jit(solution)/shard_map/ppermute | solution.py:27
  64.6 16.7 %collective-permute-start.9 = (bf16[2,2,128,512]{3,2,1,0:T(8,128)(2,1)S(1)}, bf16[2,2,128,512]{3,2,1,0:T(8,128)(2,1)S(1)}, u32[]{:S(2)}, u32[]{:S(2)}) collective-permute-start(bf16[2,2,128,512]{3,2,1,0:T(8,128)(2,1)S(1)} %collective-permute-done.7.refs_5_), channel_id=1, source_target_pairs={{0,96},{4,100},{8,104},{12,108},{16,112},{20,116},{24,120},{28,124... | collective-permute-start | bytes 1572872 | tf_op jit(solution)/shard_map/ppermute | solution.py:27
  65.2 16.1 %collective-permute-start.15 = (bf16[2,2,128,512]{3,2,1,0:T(8,128)(2,1)S(1)}, bf16[2,2,128,512]{3,2,1,0:T(8,128)(2,1)S(1)}, u32[]{:S(2)}, u32[]{:S(2)}) collective-permute-start(bf16[2,2,128,512]{3,2,1,0:T(8,128)(2,1)S(1)} %collective-permute-done.7.refs_5_), channel_id=1, source_target_pairs={{0,4},{4,0},{8,12},{12,8},{16,20},{20,16},{24,28},{28,24},{32,36},... | collective-permute-start | bytes 1572872 | tf_op jit(solution)/shard_map/ppermute | solution.py:18
  88.7 23.3 %collective-permute-start.21 = (bf16[7,2,128,128]{3,2,1,0:T(8,128)(2,1)S(1)}, bf16[7,2,128,128]{3,2,1,0:T(8,128)(2,1)}, u32[]{:S(2)}, u32[]{:S(2)}) collective-permute-start(bf16[7,2,128,128]{3,2,1,0:T(8,128)(2,1)S(1)} %shard_map.103.own), channel_id=1, source_target_pairs={{0,1},{1,0},{2,3},{3,2},{4,5},{5,4},{6,7},{7,6},{8,9},{9,8},{10,11... | collective-permute-start | bytes 1376264 | tf_op jit(solution)/shard_map/ppermute | solution.py:18
  94.6 27.2 %collective-permute-start.18 = (bf16[7,2,128,128]{3,2,1,0:T(8,128)(2,1)S(1)}, bf16[7,2,128,128]{3,2,1,0:T(8,128)(2,1)}, u32[]{:S(2)}, u32[]{:S(2)}) collective-permute-start(bf16[7,2,128,128]{3,2,1,0:T(8,128)(2,1)S(1)} %shard_map.100.own), channel_id=1, source_target_pairs={{0,1},{1,0},{2,3},{3,2},{4,5},{5,4},{6,7},{7,6},{8,9},{9,8},{10,11... | collective-permute-start | bytes 1376264 | tf_op jit(solution)/shard_map/ppermute | solution.py:18
  99.7 33.6 %collective-permute-start.45 = (bf16[7,2,128,128]{3,2,1,0:T(8,128)(2,1)}, bf16[7,2,128,128]{3,2,1,0:T(8,128)(2,1)}, u32[]{:S(2)}, u32[]{:S(2)}) collective-permute-start(bf16[7,2,128,128]{3,2,1,0:T(8,128)(2,1)} %shard_map.110.own), channel_id=1, source_target_pairs={{0,1},{1,0},{2,3},{3,2},{4,5},{5,4},{6,7},{7,6},{8,9},{9,8},{10,11... | collective-permute-start | bytes 1376264 | tf_op jit(solution)/shard_map/ppermute | solution.py:18
  105.3 36.1 %collective-permute-start.47 = (bf16[7,2,128,128]{3,2,1,0:T(8,128)(2,1)S(1)}, bf16[7,2,128,128]{3,2,1,0:T(8,128)(2,1)}, u32[]{:S(2)}, u32[]{:S(2)}) collective-permute-start(bf16[7,2,128,128]{3,2,1,0:T(8,128)(2,1)S(1)} %shard_map.113.own), channel_id=1, source_target_pairs={{0,1},{1,0},{2,3},{3,2},{4,5},{5,4},{6,7},{7,6},{8,9},{9,8},{10,11... | collective-permute-start | bytes 1376264 | tf_op jit(solution)/shard_map/ppermute | solution.py:18
  115.9 31.4 %collective-permute-start.22 = (bf16[7,2,128,128]{3,2,1,0:T(8,128)(2,1)}, bf16[7,2,128,128]{3,2,1,0:T(8,128)(2,1)}, u32[]{:S(2)}, u32[]{:S(2)}) collective-permute-start(bf16[7,2,128,128]{3,2,1,0:T(8,128)(2,1)} %get-tuple-element.16), channel_id=1, source_target_pairs={{0,3},{1,2},{2,1},{3,0},{4,7},{5,6},{6,5},{7,4},{8,11},{9,10},{10,... | collective-permute-start | bytes 1376264 | tf_op jit(solution)/shard_map/ppermute | solution.py:18
  125.7 25.1 %collective-permute-start.20 = (bf16[7,2,128,128]{3,2,1,0:T(8,128)(2,1)}, bf16[7,2,128,128]{3,2,1,0:T(8,128)(2,1)S(1)}, u32[]{:S(2)}, u32[]{:S(2)}) collective-permute-start(bf16[7,2,128,128]{3,2,1,0:T(8,128)(2,1)} %get-tuple-element.14), channel_id=1, source_target_pairs={{0,3},{1,2},{2,1},{3,0},{4,7},{5,6},{6,5},{7,4},{8,11},{9,10},{10,... | collective-permute-start | bytes 1376264 | tf_op jit(solution)/shard_map/ppermute | solution.py:18
  129.9 52.7 %collective-permute-start.26 = (bf16[2,256,256]{2,1,0:T(8,128)(2,1)}, bf16[2,256,256]{2,1,0:T(8,128)(2,1)S(1)}, u32[]{:S(2)}, u32[]{:S(2)}) collective-permute-start(bf16[2,256,256]{2,1,0:T(8,128)(2,1)} %get-tuple-element.25), channel_id=1, source_target_pairs={{1,0},{2,1},{3,2},{4,3},{5,4},{6,5},{7,6},{8,7},{9,8},{10,9},{11,1... | collective-permute-start | bytes 786440 | tf_op jit(solution)/shard_map/ppermute | solution.py:286
  135.8 21.4 %collective-permute-start.46 = (bf16[7,2,128,128]{3,2,1,0:T(8,128)(2,1)S(1)}, bf16[7,2,128,128]{3,2,1,0:T(8,128)(2,1)S(1)}, u32[]{:S(2)}, u32[]{:S(2)}) collective-permute-start(bf16[7,2,128,128]{3,2,1,0:T(8,128)(2,1)S(1)} %get-tuple-element.18), channel_id=1, source_target_pairs={{0,3},{1,2},{2,1},{3,0},{4,7},{5,6},{6,5},{7,4},{8,11},{9,10},{10,... | collective-permute-start | bytes 1376264 | tf_op jit(solution)/shard_map/ppermute | solution.py:18
  143.8 21.1 %collective-permute-start.48 = (bf16[7,2,128,128]{3,2,1,0:T(8,128)(2,1)S(1)}, bf16[7,2,128,128]{3,2,1,0:T(8,128)(2,1)S(1)}, u32[]{:S(2)}, u32[]{:S(2)}) collective-permute-start(bf16[7,2,128,128]{3,2,1,0:T(8,128)(2,1)S(1)} %get-tuple-element.20), channel_id=1, source_target_pairs={{0,3},{1,2},{2,1},{3,0},{4,7},{5,6},{6,5},{7,4},{8,11},{9,10},{10,... | collective-permute-start | bytes 1376264 | tf_op jit(solution)/shard_map/ppermute | solution.py:18
  147.3 35.3 %collective-permute-start.25 = (bf16[2,256,256]{2,1,0:T(8,128)(2,1)S(1)}, bf16[2,256,256]{2,1,0:T(8,128)(2,1)S(1)}, u32[]{:S(2)}, u32[]{:S(2)}) collective-permute-start(bf16[2,256,256]{2,1,0:T(8,128)(2,1)S(1)} %copy-done.34), channel_id=1, source_target_pairs={{0,1},{1,2},{2,3},{3,4},{4,5},{5,6},{6,7},{7,8},{8,9},{9,10},{10,1... | collective-permute-start | bytes 786440 | tf_op jit(solution)/shard_map/ppermute | solution.py:285
  156.9 25.6 %collective-permute-start.23 = (bf16[2,2,128,512]{3,2,1,0:T(8,128)(2,1)S(1)}, bf16[2,2,128,512]{3,2,1,0:T(8,128)(2,1)S(1)}, u32[]{:S(2)}, u32[]{:S(2)}) collective-permute-start(bf16[2,2,128,512]{3,2,1,0:T(8,128)(2,1)S(1)} %shard_map.107), channel_id=1, source_target_pairs={{0,1},{1,0},{2,3},{3,2},{4,5},{5,4},{6,7},{7,6},{8,9},{9,8},{10,11... | collective-permute-start | bytes 1572872 | tf_op jit(solution)/shard_map/ppermute | solution.py:18
  171.8 19.8 %collective-permute-start.49 = (bf16[1,2,128,512]{3,2,1,0:T(8,128)(2,1)S(1)}, bf16[1,2,128,512]{3,2,1,0:T(8,128)(2,1)S(1)}, u32[]{:S(2)}, u32[]{:S(2)}) collective-permute-start(bf16[1,2,128,512]{3,2,1,0:T(8,128)(2,1)S(1)} %shard_map.117), channel_id=1, source_target_pairs={{0,1},{1,0},{2,3},{3,2},{4,5},{5,4},{6,7},{7,6},{8,9},{9,8},{10,11... | collective-permute-start | bytes 786440 | tf_op jit(solution)/shard_map/ppermute | solution.py:18
  (65 other events, 991.0 us)
where the time goes:
time: 197 us; the launch traced here: 196 us
  starting transfers between devices  69.5 us (35%)
  waiting for transfers between devices  59.5 us (30%)
  Pallas kernels  58.6 us (30%)
  local copies, waits for them, and re-layouts  5.79 us (3%)
    pallas_call x20, Pallas kernels, call(): pl.pallas_call(body, in_specs=[SMEM] * len(scalars) + [pl.BlockSpec(memor...  58.6 us
    ppermute x30, starting transfers between devices, swap(): lax.ppermute(value, axis, [(i, i ^ mask) for i in range(lax.axis_size(axi...  43.3 us
    ppermute x20, waiting for transfers between devices, ring(): return lax.ppermute(value, 'grp', perm)  36.2 us
    ppermute x30, waiting for transfers between devices, swap(): lax.ppermute(value, axis, [(i, i ^ mask) for i in range(lax.axis_size(axi...  23.3 us
    ppermute x20, starting transfers between devices, ring(): return lax.ppermute(value, 'grp', perm)  21 us
  transfers between devices with their start and end apart: 52, of which 20 were waited for; matrix products, arithmetic and copies ran while one was open for 1% of the time, Pallas kernels for 30%

commit v1 on v0

--- a/solution.py
+++ b/solution.py
@@ -154,33 +154,67 @@
     return real, imag
 
 
-def section_body(base, bit, rank, own, other, *refs):
-    half = len(refs) // 2
-    ws, outs = refs[:half], refs[half:]
-    count, _, n, k = own.shape
-    upper = bit[0] == 1
+def section_copies(base, own, other, ws, levels, weights, sems):
+    def copies(i):
+        pairs = [(own.at[i], levels.at[0, i]), (other.at[i], levels.at[1, i])]
+        pairs += [(w.at[0, 0, base + i], weights.at[j, i]) for j, w in enumerate(ws)]
+        return [pltpu.make_async_copy(a, b, sems.at[j, i]) for j, (a, b) in enumerate(pairs)]
+
+    return copies
+
+
+def section_apply(i, f, upper, rank, levels, weights):
+    _, _, _, n, k = levels.shape
+    a = levels[0, i].reshape(2 * n, k)
+    b = levels[1, i].reshape(2 * n, k)
+    x = jnp.concatenate([jnp.where(upper, b, a), jnp.where(upper, a, b)], axis=1)
+    live = lax.broadcasted_iota(jnp.int32, (n, k), 1) < rank[0, f]
+    for j in range(weights.shape[0]):
+        yield combine(nt(x, weights[j, i].reshape(2 * k, 2 * k)), n, k, live)
+
+
+def section_scratch(count, n, k, parts):
+    return [
+        pltpu.VMEM((2, count, 2, n, k), BF16),
+        pltpu.VMEM((parts, count, 2, k, 2 * k), BF16),
+        pltpu.SemaphoreType.DMA((2 + parts, count)),
+    ], 8 * count * n * k + 8 * parts * count * k * k
+
+
+def section_body(base, parts, bit, rank, own, other, *refs):
+    ws, outs, (levels, weights, sems) = refs[:parts], refs[parts : 2 * parts], refs[2 * parts :]
+    count = own.shape[0]
+    copies = section_copies(base, own, other, ws, levels, weights, sems)
     for i in range(count):
-        a = own[i].reshape(2 * n, k)
-        b = other[i].reshape(2 * n, k)
-        x = jnp.concatenate([jnp.where(upper, b, a), jnp.where(upper, a, b)], axis=1)
-        live = lax.broadcasted_iota(jnp.int32, (n, k), 1) < rank[0, base + i]
-        for w, out in zip(ws, outs):
-            p = nt(x, w[0, 0, base + i].reshape(2 * k, 2 * k))
-            out[i, 0], out[i, 1] = combine(p, n, k, live)
+        for c in copies(i):
+            c.start()
+    for i in range(count):
+        for c in copies(i):
+            c.wait()
+        got = section_apply(i, base + i, bit[0] == 1, rank, levels, weights)
+        for out, (real, imag) in zip(outs, got):
+            out[i, 0], out[i, 1] = real, imag
 
 
 def section(base, bit, rank, own, other, ws):
     count, _, n, k = own.shape
     shape = jax.ShapeDtypeStruct(own.shape, BF16)
-    return call(
-        functools.partial(section_body, base),
+    scratch, room = section_scratch(count, n, k, len(ws))
+    return call(
+        functools.partial(section_body, base, len(ws)),
         [bit, rank], [own, other, *ws], [shape] * len(ws),
-        16 * count * n * k * k * len(ws), 2 << 20,
-    )
-
-
-def outward_body(dtype, order, *refs):
-    levels, w, out, xs, ws, sems = refs[:-5], refs[-5], refs[-4], refs[-3], refs[-2], refs[-1]
+        16 * count * n * k * k * len(ws), 3 << 20,
+        scratch, space=[pltpu.HBM] * (2 + len(ws)), room=room,
+    )
+
+
+def fill(xs, f, real, imag):
+    n = real.shape[0]
+    xs[f, :n] = jnp.concatenate([real, -imag], 1)
+    xs[f, n:] = jnp.concatenate([imag, real], 1)
+
+
+def outward_blocks(dtype, order, xs, w, out, ws, sems):
     n = xs.shape[1] // 2
     blocks, step = ws.shape[0], ws.shape[3]
     piece = out.shape[3]
@@ -190,15 +224,9 @@
         start = pl.multiple_of(order[b // per] * piece + (b % per) * step, step)
         return pltpu.make_async_copy(w.at[0, 0, :, :, pl.ds(start, step)], ws.at[b], sems.at[b])
 
-    copy(0).start()
-    copy(1).start()
-    f = 0
-    for level in levels:
-        for i in range(level.shape[0]):
-            real, imag = level[i, 0], level[i, 1]
-            xs[f, :n] = jnp.concatenate([real, -imag], 1)
-            xs[f, n:] = jnp.concatenate([imag, real], 1)
-            f += 1
+    def begin():
+        copy(0).start()
+        copy(1).start()
 
     def body(b, carry):
         copy(b).wait()
@@ -215,27 +243,81 @@
         out[b // per, 1, :, to] = acc[n:].astype(dtype)
         return carry
 
-    lax.fori_loop(0, blocks, body, 0)
-
-
-def outward(dtype, order, levels, w, step=256):
-    _, _, n, k = levels[0].shape
-    far = w.shape[2]
-    piece = w.shape[4] // 4
-    count = order.shape[0]
+    return begin, lambda: lax.fori_loop(0, blocks, body, 0)
+
+
+def outward_body(dtype, order, xs, w, out, ws, sems):
+    begin, rest = outward_blocks(dtype, order, xs, w, out, ws, sems)
+    begin()
+    rest()
+
+
+def outward_scratch(count, n, w, step=256):
+    _, _, far, _, size_out, k = w.shape
+    piece = size_out // 4
     blocks = count * piece // step
+    return (
+        (count, 2, n, piece),
+        [pltpu.VMEM((blocks, far, 2, step, k), BF16), pltpu.SemaphoreType.DMA((blocks,))],
+        blocks * far * step * k * 4,
+        8 * far * n * k * piece * count,
+    )
+
+
+def outward(dtype, order, xs, w):
+    shape, scratch, room, flops = outward_scratch(order.shape[0], xs.shape[1] // 2, w)
     return call(
         functools.partial(outward_body, dtype),
-        [order], [*levels, w],
-        jax.ShapeDtypeStruct((count, 2, n, piece), dtype),
-        8 * far * n * k * piece * count, 4 << 20,
-        [
-            pltpu.VMEM((far, 2 * n, 2 * k), BF16),
-            pltpu.VMEM((blocks, far, 2, step, k), BF16),
-            pltpu.SemaphoreType.DMA((blocks,)),
-        ],
-        space=[pltpu.VMEM] * len(levels) + [pltpu.HBM],
-        room=far * n * k * 8 + blocks * far * step * k * 4,
+        [order], [xs, w], jax.ShapeDtypeStruct(shape, dtype), flops, 4 << 20,
+        scratch, space=[pltpu.VMEM, pltpu.HBM], room=room,
+    )
+
+
+def level2_outward_body(base, order, bit, rank, ready, own, other, s2, w, xs, out, *scratch):
+    levels, weights, sems, ws, wsems = scratch
+    copies = section_copies(base, own, other, [s2], levels, weights, sems)
+    count = own.shape[0]
+    for i in range(count):
+        for c in copies(i):
+            c.start()
+    begin, rest = outward_blocks(BF16, order, xs, w, out, ws, wsems)
+    begin()
+    for i in range(base):
+        fill(xs, i, ready[i, 0], ready[i, 1])
+    for i in range(count):
+        for c in copies(i):
+            c.wait()
+        for real, imag in section_apply(i, base + i, bit[0] == 1, rank, levels, weights):
+            fill(xs, base + i, real, imag)
+    rest()
+
+
+def level2_outward(order, bit, rank, ready, own, other, s2, w):
+    count, _, n, k = own.shape
+    base = ready.shape[0]
+    far = base + count
+    scratch, room = section_scratch(count, n, k, 1)
+    shape, more, more_room, flops = outward_scratch(order.shape[0], n, w)
+    return call(
+        functools.partial(level2_outward_body, base),
+        [order, bit, rank], [ready, own, other, s2, w],
+        [jax.ShapeDtypeStruct((far, 2 * n, 2 * k), BF16), jax.ShapeDtypeStruct(shape, BF16)],
+        flops, 6 << 20,
+        scratch + more, space=[pltpu.VMEM] + [pltpu.HBM] * 4, room=room + more_room,
+    )
+
+
+def final_body(first, base, last, out):
+    n = first.shape[1]
+    out[:, :n] = first[...]
+    out[:, n:] = (base[...] + last[...].astype(F32)).astype(BF16)
+
+
+def final(first, base, last):
+    parts, n, rows = first.shape
+    return call(
+        final_body, [], [first, base, last],
+        jax.ShapeDtypeStruct((parts, 2 * n, rows), BF16), 1 << 18, 1 << 20,
     )
 
 
@@ -243,10 +325,9 @@
     one, two = ("x", "y") if color == 0 else ("y", "x")
     below = ring(block, one, 1)
     above = ring(block, one, -1)
-    far_r = ring(below[:, :1], one, 1)
-    far_i = ring(above[:, 1:], one, -1)
+    opposite = ring(block, one, 2)
     lo = jnp.concatenate([block, below], 0)
-    hi = jnp.concatenate([above, jnp.concatenate([far_r, far_i], 1)], 0)
+    hi = jnp.concatenate([above, opposite], 0)
     below_lo = ring(lo, two, 1)
     above_hi = ring(hi, two, -1)
     below_hi = ring(hi, two, 1)
@@ -294,30 +375,33 @@
 
     pieces = []
     for h in range(2):
-        two = []
+        at = slice(2 * h * q, 2 * (h + 1) * q)
+        level1 = []
         for base, count in spans:
             lev0 = level0(h, base, count, far_source, gidx, far_rank, bufs[h], basis_in)
             lev0_pair = swap(lev0, "mem", 1)
             lev1, lev1_pair = section(
                 base, bit0, far_rank, lev0, lev0_pair, [section_one, section_pair]
             )
-            lev1_other = swap(lev1_pair, "mem", 3)
-            two += section(base, bit1, far_rank, lev1, lev1_other, [section_two])
+            level1.append((lev1, swap(lev1_pair, "mem", 3)))
+        (ready,) = section(0, bit1, far_rank, *level1[0], [section_two])
+        early = 2 - h
+        xs, sent = level2_outward(
+            member ^ far_near[:early], bit1, far_rank, ready, *level1[1],
+            section_two, basis_out,
+        )
+        sent = swap(sent, "mem", 1)
         if h == 0:
-            sent = outward(BF16, member ^ far_near[:2], two, basis_out)
-            sent = swap(sent, "mem", 1)
             sent = (sent[0], sent[1])
         else:
-            sent = []
-            for i in range(2):
-                part = outward(BF16, member ^ far_near[i : i + 1], two, basis_out)
-                sent.append(swap(part, "mem", 1)[0])
-        other = outward(F32, member ^ far_near[2:3], two, basis_out)[0]
+            part = outward(BF16, member ^ far_near[1:2], xs, basis_out)
+            sent = (sent[0], swap(part, "mem", 1)[0])
+        other = outward(F32, member ^ far_near[2:3], xs, basis_out)[0]
         last = swap((other + sent[0].astype(F32)).astype(BF16), "mem", 3)
-        kept = outward(F32, member ^ far_near[3:], two, basis_out)[0]
-        at = slice(2 * h * q, 2 * (h + 1) * q)
-        pieces.append((kept + sent[1].astype(F32) + last.astype(F32) + near[:, at]).astype(BF16))
-    return jnp.concatenate(pieces, 1)
+        kept = outward(F32, member ^ far_near[3:], xs, basis_out)[0]
+        pieces.append((kept + sent[1].astype(F32) + near[:, at], last))
+    base, last = pieces[0]
+    return final((base + last.astype(F32)).astype(BF16), *pieces[1])
 
 
 def solution(mesh):

time: 197 us -> 208 us (1.056)
  Pallas kernels: 58.6 us -> 68.6 us
  starting transfers between devices: 69.5 us -> 76.9 us
  waiting for transfers between devices: 59.5 us -> 52.4 us
    ppermute x30, waiting for transfers between devices: 23.3 us -> 10.5 us  [swap(): lax.ppermute(value, axis, [(i, i ^ mask) for i in range(lax.axis_size(axi...]
    pallas_call x20 -> x19, Pallas kernels: 58.6 us -> 68.6 us  [call(): pl.pallas_call(body, in_specs=[SMEM] * len(scalars) + [pl.BlockSpec(memor...]
    ppermute x30, starting transfers between devices: 43.3 us -> 50.2 us  [swap(): lax.ppermute(value, axis, [(i, i ^ mask) for i in range(lax.axis_size(axi...]
    ppermute x20 -> x18, waiting for transfers between devices: 36.2 us -> 41.9 us  [ring(): return lax.ppermute(value, 'grp', perm)]
    unnamed x75 -> x89, local copies, waits for them, and re-layouts: 3.85 us -> 5.72 us
    ppermute x20 -> x18, starting transfers between devices: 21 us -> 20.7 us  [ring(): return lax.ppermute(value, 'grp', perm)]
  transfers between devices with their start and end apart: 52 -> 50, of which waited for: 20 -> 13; matrix products, arithmetic and copies ran while one was open for 1% -> 1% of each run, Pallas kernels for 30% -> 33%
where the time goes in v1:
time: 208 us; the launch traced here: 207 us
  starting transfers between devices  76.9 us (37%)
  Pallas kernels  68.6 us (33%)
  waiting for transfers between devices  52.4 us (25%)
  local copies, waits for them, and re-layouts  7.66 us (4%)
    pallas_call x19, Pallas kernels, call(): pl.pallas_call(body, in_specs=[SMEM] * len(scalars) + [pl.BlockSpec(memor...  68.6 us
    ppermute x30, starting transfers between devices, swap(): lax.ppermute(value, axis, [(i, i ^ mask) for i in range(lax.axis_size(axi...  50.2 us
    ppermute x18, waiting for transfers between devices, ring(): return lax.ppermute(value, 'grp', perm)  41.9 us
    ppermute x18, starting transfers between devices, ring(): return lax.ppermute(value, 'grp', perm)  20.7 us
    ppermute x30, waiting for transfers between devices, swap(): lax.ppermute(value, axis, [(i, i ^ mask) for i in range(lax.axis_size(axi...  10.5 us
    unnamed x89, local copies, waits for them, and re-layouts  5.72 us
  transfers between devices with their start and end apart: 50, of which 13 were waited for; matrix products, arithmetic and copies ran while one was open for 1% of the time, Pallas kernels for 33%

profile of v1, /device:TPU:7, one launch (start us, length us, event | category | flops | bytes accessed | tf_op | source)
XLA Modules:
  0.0 206.9 jit_solution(15348680615808774655)
XLA Ops:
  21.0 3.4 %collective-permute-start.6 = (bf16[2,2,128,512]{3,2,1,0:T(8,128)(2,1)S(1)}, bf16[2,2,128,512]{3,2,1,0:T(8,128)(2,1)S(1)}, u32[]{:S(2)}, u32[]{:S(2)}) collective-permute-start(bf16[2,2,128,512]{3,2,1,0:T(8,128)(2,1)S(1)} %constant_dynamic-update-slice_fusion.refs_1_), channel_id=1, source_target_pairs={{0,96},{4,100},{8,104},{12,108},{16,112},{20,116},{24,120},{28,124... | collective-permute-start | bytes 1572872 | tf_op jit(solution)/shard_map/ppermute | solution.py:27
  25.2 5.4 %collective-permute-done.5.refs_4_ = bf16[2,2,128,512]{3,2,1,0:T(8,128)(2,1)S(1)} collective-permute-done((bf16[2,2,128,512]{3,2,1,0:T(8,128)(2,1)S(1)}, bf16[2,2,128,512]{3,2,1,0:T(8,128)(2,1)S(1)}, u32[]{:S(2)}, u32[]{:S(2)}) %collective-permute-start.5) | collective-permute-done | bytes 524320 | tf_op jit(solution)/shard_map/ppermute | solution.py:27
  36.1 5.8 %collective-permute-done.6.refs_5_ = bf16[2,2,128,512]{3,2,1,0:T(8,128)(2,1)S(1)} collective-permute-done((bf16[2,2,128,512]{3,2,1,0:T(8,128)(2,1)S(1)}, bf16[2,2,128,512]{3,2,1,0:T(8,128)(2,1)S(1)}, u32[]{:S(2)}, u32[]{:S(2)}) %collective-permute-start.6) | collective-permute-done | bytes 524320 | tf_op jit(solution)/shard_map/ppermute | solution.py:27
  47.3 7.0 %collective-permute-start.13 = (bf16[2,2,128,512]{3,2,1,0:T(8,128)(2,1)S(1)}, bf16[2,2,128,512]{3,2,1,0:T(8,128)(2,1)S(1)}, u32[]{:S(2)}, u32[]{:S(2)}) collective-permute-start(bf16[2,2,128,512]{3,2,1,0:T(8,128)(2,1)S(1)} %collective-permute-done.5.refs_4_), channel_id=1, source_target_pairs={{0,4},{4,0},{8,12},{12,8},{16,20},{20,16},{24,28},{28,24},{32,36},... | collective-permute-start | bytes 1572872 | tf_op jit(solution)/shard_map/ppermute | solution.py:18
  54.4 5.5 %collective-permute-done.32.refs_5_ = bf16[2,2,128,512]{3,2,1,0:T(8,128)(2,1)} collective-permute-done((bf16[2,2,128,512]{3,2,1,0:T(8,128)(2,1)S(1)}, bf16[2,2,128,512]{3,2,1,0:T(8,128)(2,1)}, u32[]{:S(2)}, u32[]{:S(2)}) %collective-permute-start.32) | collective-permute-done | bytes 524320 | tf_op jit(solution)/shard_map/ppermute | solution.py:27
  64.8 3.8 %collective-permute-done.7.refs_6_ = bf16[2,2,128,512]{3,2,1,0:T(8,128)(2,1)S(1)} collective-permute-done((bf16[2,2,128,512]{3,2,1,0:T(8,128)(2,1)S(1)}, bf16[2,2,128,512]{3,2,1,0:T(8,128)(2,1)S(1)}, u32[]{:S(2)}, u32[]{:S(2)}) %collective-permute-start.7) | collective-permute-done | bytes 524320 | tf_op jit(solution)/shard_map/ppermute | solution.py:27
  70.1 6.5 %collective-permute-done.8.refs_7_ = bf16[2,2,128,512]{3,2,1,0:T(8,128)(2,1)S(1)} collective-permute-done((bf16[2,2,128,512]{3,2,1,0:T(8,128)(2,1)S(1)}, bf16[2,2,128,512]{3,2,1,0:T(8,128)(2,1)S(1)}, u32[]{:S(2)}, u32[]{:S(2)}) %collective-permute-start.8) | collective-permute-done | bytes 524320 | tf_op jit(solution)/shard_map/ppermute | solution.py:27
  79.6 9.8 %collective-permute-done.33.refs_6_ = bf16[2,2,128,512]{3,2,1,0:T(8,128)(2,1)} collective-permute-done((bf16[2,2,128,512]{3,2,1,0:T(8,128)(2,1)S(1)}, bf16[2,2,128,512]{3,2,1,0:T(8,128)(2,1)}, u32[]{:S(2)}, u32[]{:S(2)}) %collective-permute-start.33) | collective-permute-done | bytes 524320 | tf_op jit(solution)/shard_map/ppermute | solution.py:27
  93.6 4.2 %shard_map.100.own = bf16[7,2,128,128]{3,2,1,0:T(8,128)(2,1)S(1)} custom-call(s32[32,14]{1,0:T(8,128)S(1)} %copy.11.src, s32[1]{0:T(128)} %bitcast.3.gidx, s32[1,14]{1,0:T(1,128)S(1)} %copy-done.10, bf16[2,2,128,512]{3,2,1,0:T(8,128)(2,1)} %copy-done.13, bf16[2,2,128,512]{3,2,1,0:T(8,128)(2,1)} %copy-done.15, bf16[2,2,128,512]{3,2,1,0:T(8,128)(2,1)} %copy-done.20, ...), custom_call_target="tpu_custom_call" | custom-call | flops 469762048 | bytes 4194304 | tf_op jit(solution)/shard_map/pallas_call | solution.py:46
  99.6 4.2 %shard_map.103.own = bf16[7,2,128,128]{3,2,1,0:T(8,128)(2,1)S(1)} custom-call(s32[32,14]{1,0:T(8,128)S(1)} %copy.11.src, s32[1]{0:T(128)} %bitcast.3.gidx, s32[1,14]{1,0:T(1,128)S(1)} %copy-done.10, bf16[2,2,128,512]{3,2,1,0:T(8,128)(2,1)} %copy-done.13, bf16[2,2,128,512]{3,2,1,0:T(8,128)(2,1)} %copy-done.15, bf16[2,2,128,512]{3,2,1,0:T(8,128)(2,1)} %copy-done.20, ...), custom_call_target="tpu_custom_call" | custom-call | flops 469762048 | bytes 4194304 | tf_op jit(solution)/shard_map/pallas_call | solution.py:46
  103.9 4.2 %shard_map.109.own = bf16[7,2,128,128]{3,2,1,0:T(8,128)(2,1)S(1)} custom-call(s32[32,14]{1,0:T(8,128)S(1)} %copy.11.src, s32[1]{0:T(128)} %bitcast.3.gidx, s32[1,14]{1,0:T(1,128)S(1)} %copy-done.10, bf16[2,2,128,512]{3,2,1,0:T(8,128)(2,1)} %copy-done.14, bf16[2,2,128,512]{3,2,1,0:T(8,128)(2,1)} %copy-done.16, bf16[2,2,128,512]{3,2,1,0:T(8,128)(2,1)} %copy-done.22, ...), custom_call_target="tpu_custom_call" | custom-call | flops 469762048 | bytes 4194304 | tf_op jit(solution)/shard_map/pallas_call | solution.py:46
  109.6 4.2 %shard_map.112.own = bf16[7,2,128,128]{3,2,1,0:T(8,128)(2,1)S(1)} custom-call(s32[32,14]{1,0:T(8,128)S(1)} %copy.11.src, s32[1]{0:T(128)} %bitcast.3.gidx, s32[1,14]{1,0:T(1,128)S(1)} %copy-done.10, bf16[2,2,128,512]{3,2,1,0:T(8,128)(2,1)} %copy-done.14, bf16[2,2,128,512]{3,2,1,0:T(8,128)(2,1)} %copy-done.16, bf16[2,2,128,512]{3,2,1,0:T(8,128)(2,1)} %copy-done.22, ...), custom_call_target="tpu_custom_call" | custom-call | flops 469762048 | bytes 4194304 | tf_op jit(solution)/shard_map/pallas_call | solution.py:46
  115.3 3.7 %shard_map.101 = (bf16[7,2,128,128]{3,2,1,0:T(8,128)(2,1)S(1)}, bf16[7,2,128,128]{3,2,1,0:T(8,128)(2,1)S(1)}) custom-call(s32[1]{0:T(128)} %bitcast.2.bit, s32[1,14]{1,0:T(1,128)S(1)} %copy-done.10, bf16[7,2,128,128]{3,2,1,0:T(8,128)(2,1)} %copy-done.3, bf16[7,2,128,128]{3,2,1,0:T(8,128)(2,1)} %copy-done.36, bf16[1,1,14,2,128,256]{5,4,3,2,1,0:T(8,128)(2,1)} %refs_0_.11, ...), custom_call_target="tpu_custom_call" | custom-call | flops 469762048 | bytes 3145728 | tf_op jit(solution)/shard_map/pallas_call | solution.py:46
  119.8 3.4 %collective-permute-start.19 = (bf16[7,2,128,128]{3,2,1,0:T(8,128)(2,1)S(1)}, bf16[7,2,128,128]{3,2,1,0:T(8,128)(2,1)S(1)}, u32[]{:S(2)}, u32[]{:S(2)}) collective-permute-start(bf16[7,2,128,128]{3,2,1,0:T(8,128)(2,1)S(1)} %get-tuple-element.18), channel_id=1, source_target_pairs={{0,3},{1,2},{2,1},{3,0},{4,7},{5,6},{6,5},{7,4},{8,11},{9,10},{10,... | collective-permute-start | bytes 1376264 | tf_op jit(solution)/shard_map/ppermute | solution.py:18
  124.4 3.7 %shard_map.104 = (bf16[7,2,128,128]{3,2,1,0:T(8,128)(2,1)S(1)}, bf16[7,2,128,128]{3,2,1,0:T(8,128)(2,1)S(1)}) custom-call(s32[1]{0:T(128)} %bitcast.2.bit, s32[1,14]{1,0:T(1,128)S(1)} %copy-done.10, bf16[7,2,128,128]{3,2,1,0:T(8,128)(2,1)} %copy-done.1, bf16[7,2,128,128]{3,2,1,0:T(8,128)(2,1)} %collective-permute-done.20.other, ...), custom_call_target="tpu_custom_call" | custom-call | flops 469762048 | bytes 3145728 | tf_op jit(solution)/shard_map/pallas_call | solution.py:46
  133.2 4.0 %collective-permute-start.24 = (bf16[2,256,256]{2,1,0:T(8,128)(2,1)}, bf16[2,256,256]{2,1,0:T(8,128)(2,1)S(1)}, u32[]{:S(2)}, u32[]{:S(2)}) collective-permute-start(bf16[2,256,256]{2,1,0:T(8,128)(2,1)} %get-tuple-element.33), channel_id=1, source_target_pairs={{1,0},{2,1},{3,2},{4,3},{5,4},{6,5},{7,6},{8,7},{9,8},{10,9},{11,1... | collective-permute-start | bytes 786440 | tf_op jit(solution)/shard_map/ppermute | solution.py:367
  139.2 3.7 %shard_map.110 = (bf16[7,2,128,128]{3,2,1,0:T(8,128)(2,1)S(1)}, bf16[7,2,128,128]{3,2,1,0:T(8,128)(2,1)S(1)}) custom-call(s32[1]{0:T(128)} %bitcast.2.bit, s32[1,14]{1,0:T(1,128)S(1)} %copy-done.10, bf16[7,2,128,128]{3,2,1,0:T(8,128)(2,1)} %copy-done.4, bf16[7,2,128,128]{3,2,1,0:T(8,128)(2,1)} %copy-done.37, bf16[1,1,14,2,128,256]{5,4,3,2,1,0:T(8,128)(2,1)} %refs_0_.11, ...), custom_call_target="tpu_custom_call" | custom-call | flops 469762048 | bytes 3145728 | tf_op jit(solution)/shard_map/pallas_call | solution.py:46
  144.0 6.2 %collective-permute-start.44 = (bf16[7,2,128,128]{3,2,1,0:T(8,128)(2,1)S(1)}, bf16[7,2,128,128]{3,2,1,0:T(8,128)(2,1)}, u32[]{:S(2)}, u32[]{:S(2)}) collective-permute-start(bf16[7,2,128,128]{3,2,1,0:T(8,128)(2,1)S(1)} %get-tuple-element.24), channel_id=1, source_target_pairs={{0,3},{1,2},{2,1},{3,0},{4,7},{5,6},{6,5},{7,4},{8,11},{9,10},{10,... | collective-permute-start | bytes 1376264 | tf_op jit(solution)/shard_map/ppermute | solution.py:18
  150.2 3.7 %shard_map.113 = (bf16[7,2,128,128]{3,2,1,0:T(8,128)(2,1)S(1)}, bf16[7,2,128,128]{3,2,1,0:T(8,128)(2,1)S(1)}) custom-call(s32[1]{0:T(128)} %bitcast.2.bit, s32[1,14]{1,0:T(1,128)S(1)} %copy-done.10, bf16[7,2,128,128]{3,2,1,0:T(8,128)(2,1)} %copy-done.2, bf16[7,2,128,128]{3,2,1,0:T(8,128)(2,1)} %copy-done.38, bf16[1,1,14,2,128,256]{5,4,3,2,1,0:T(8,128)(2,1)} %refs_0_.11, ...), custom_call_target="tpu_custom_call" | custom-call | flops 469762048 | bytes 3145728 | tf_op jit(solution)/shard_map/pallas_call | solution.py:46
  155.5 3.5 %shard_map.102.ready = bf16[7,2,128,128]{3,2,1,0:T(8,128)(2,1)S(1)} custom-call(s32[1]{0:T(128)} %bitcast.1.bit, s32[1,14]{1,0:T(1,128)S(1)} %copy-done.10, bf16[7,2,128,128]{3,2,1,0:T(8,128)(2,1)} %copy-done.6, bf16[7,2,128,128]{3,2,1,0:T(8,128)(2,1)} %copy-done.39, bf16[1,1,14,2,128,256]{5,4,3,2,1,0:T(8,128)(2,1)} %s2_.3), custom_call_target="tpu_custom_call" | custom-call | flops 234881024 | bytes 3145728 | tf_op jit(solution)/shard_map/pallas_call | solution.py:46
  159.8 6.6 %shard_map.105 = (bf16[14,256,256]{2,1,0:T(8,128)(2,1)S(1)}, bf16[2,2,128,512]{3,2,1,0:T(8,128)(2,1)S(1)}) custom-call(s32[2]{0:T(128)S(1)} %broadcast_xor_fusion.order, s32[1]{0:T(128)} %bitcast.1.bit, s32[1,14]{1,0:T(1,128)S(1)} %copy-done.10, bf16[7,2,128,128]{3,2,1,0:T(8,128)(2,1)S(1)} %shard_map.102.ready, bf16[7,2,128,128]{3,2,1,0:T(8,128)(2,1)} %copy-done.8, ...), custom_call_target="tpu_custom_call" | custom-call | flops 1879048192 | bytes 6291456 | tf_op jit(solution)/shard_map/pallas_call | solution.py:46
  169.7 3.5 %shard_map.111.ready = bf16[7,2,128,128]{3,2,1,0:T(8,128)(2,1)S(1)} custom-call(s32[1]{0:T(128)} %bitcast.1.bit, s32[1,14]{1,0:T(1,128)S(1)} %copy-done.10, bf16[7,2,128,128]{3,2,1,0:T(8,128)(2,1)} %copy-done.7, bf16[7,2,128,128]{3,2,1,0:T(8,128)(2,1)} %collective-permute-done.44.other, bf16[1,1,14,2,128,256]{5,4,3,2,1,0:T(8,128)(2,1)} %s2_.3), custom_call_target="tpu_custom_call" | custom-call | flops 234881024 | bytes 3145728 | tf_op jit(solution)/shard_map/pallas_call | solution.py:46
  173.1 4.9 %shard_map.114 = (bf16[14,256,256]{2,1,0:T(8,128)(2,1)S(1)}, bf16[1,2,128,512]{3,2,1,0:T(8,128)(2,1)S(1)}) custom-call(s32[1]{0:T(128)} %bitcast.8.order, s32[1]{0:T(128)} %bitcast.1.bit, s32[1,14]{1,0:T(1,128)S(1)} %copy-done.10, bf16[7,2,128,128]{3,2,1,0:T(8,128)(2,1)S(1)} %shard_map.111.ready, bf16[7,2,128,128]{3,2,1,0:T(8,128)(2,1)} %copy-done.9, ...), custom_call_target="tpu_custom_call" | custom-call | flops 939524096 | bytes 6291456 | tf_op jit(solution)/shard_map/pallas_call | solution.py:46
  200.6 5.4 %collective-permute-done.49.last = bf16[2,128,512]{2,1,0:T(8,128)(2,1)S(1)} collective-permute-done((bf16[2,128,512]{2,1,0:T(8,128)(2,1)S(1)}, bf16[2,128,512]{2,1,0:T(8,128)(2,1)S(1)}, u32[]{:S(2)}, u32[]{:S(2)}) %collective-permute-start.49) | collective-permute-done | bytes 262176 | tf_op jit(solution)/shard_map/ppermute | solution.py:18
  (194 shorter events, 89.9 us)
Async XLA Ops:
  8.4 16.0 %collective-permute-start.9 = (bf16[2,2,128,512]{3,2,1,0:T(8,128)(2,1)S(1)}, bf16[2,2,128,512]{3,2,1,0:T(8,128)(2,1)S(1)}, u32[]{:S(2)}, u32[]{:S(2)}) collective-permute-start(bf16[2,2,128,512]{3,2,1,0:T(8,128)(2,1)S(1)} %pad_maximum_fusion.refs_0_), channel_id=1, source_target_pairs={{0,4},{4,0},{8,12},{12,8},{16,20},{20,16},{24,28},{28,24},{32,36},... | collective-permute-start | bytes 1572872 | tf_op jit(solution)/shard_map/ppermute | solution.py:18
  13.9 16.8 %collective-permute-start.5 = (bf16[2,2,128,512]{3,2,1,0:T(8,128)(2,1)S(1)}, bf16[2,2,128,512]{3,2,1,0:T(8,128)(2,1)S(1)}, u32[]{:S(2)}, u32[]{:S(2)}) collective-permute-start(bf16[2,2,128,512]{3,2,1,0:T(8,128)(2,1)S(1)} %pad_maximum_fusion.refs_0_), channel_id=1, source_target_pairs={{0,96},{4,100},{8,104},{12,108},{16,112},{20,116},{24,120},{28,124... | collective-permute-start | bytes 1572872 | tf_op jit(solution)/shard_map/ppermute | solution.py:27
  15.5 17.9 %collective-permute-start.3 = (bf16[2,2,128,512]{3,2,1,0:T(8,128)(2,1)S(1)}, bf16[2,2,128,512]{3,2,1,0:T(8,128)(2,1)S(1)}, u32[]{:S(2)}, u32[]{:S(2)}) collective-permute-start(bf16[2,2,128,512]{3,2,1,0:T(8,128)(2,1)S(1)} %pad_maximum_fusion.refs_0_), channel_id=1, source_target_pairs={{0,32},{4,36},{8,40},{12,44},{16,48},{20,52},{24,56},{28,60},{32,6... | collective-permute-start | bytes 1572872 | tf_op jit(solution)/shard_map/ppermute | solution.py:27
  19.5 15.0 %collective-permute-start.10 = (bf16[2,2,128,512]{3,2,1,0:T(8,128)(2,1)S(1)}, bf16[2,2,128,512]{3,2,1,0:T(8,128)(2,1)}, u32[]{:S(2)}, u32[]{:S(2)}) collective-permute-start(bf16[2,2,128,512]{3,2,1,0:T(8,128)(2,1)S(1)} %constant_dynamic-update-slice_fusion.refs_1_), channel_id=1, source_target_pairs={{0,4},{4,0},{8,12},{12,8},{16,20},{20,16},{24,28},{28,24},{32,36},... | collective-permute-start | bytes 1572872 | tf_op jit(solution)/shard_map/ppermute | solution.py:18
  21.0 21.0 %collective-permute-start.6 = (bf16[2,2,128,512]{3,2,1,0:T(8,128)(2,1)S(1)}, bf16[2,2,128,512]{3,2,1,0:T(8,128)(2,1)S(1)}, u32[]{:S(2)}, u32[]{:S(2)}) collective-permute-start(bf16[2,2,128,512]{3,2,1,0:T(8,128)(2,1)S(1)} %constant_dynamic-update-slice_fusion.refs_1_), channel_id=1, source_target_pairs={{0,96},{4,100},{8,104},{12,108},{16,112},{20,116},{24,120},{28,124... | collective-permute-start | bytes 1572872 | tf_op jit(solution)/shard_map/ppermute | solution.py:27
  25.2 19.5 %collective-permute-start.4 = (bf16[2,2,128,512]{3,2,1,0:T(8,128)(2,1)S(1)}, bf16[2,2,128,512]{3,2,1,0:T(8,128)(2,1)S(1)}, u32[]{:S(2)}, u32[]{:S(2)}) collective-permute-start(bf16[2,2,128,512]{3,2,1,0:T(8,128)(2,1)S(1)} %constant_dynamic-update-slice_fusion.refs_1_), channel_id=1, source_target_pairs={{0,32},{4,36},{8,40},{12,44},{16,48},{20,52},{24,56},{28,60},{32,6... | collective-permute-start | bytes 1572872 | tf_op jit(solution)/shard_map/ppermute | solution.py:27
  30.7 15.1 %collective-permute-start.35 = (bf16[2,2,128,512]{3,2,1,0:T(8,128)(2,1)S(1)}, bf16[2,2,128,512]{3,2,1,0:T(8,128)(2,1)S(1)}, u32[]{:S(2)}, u32[]{:S(2)}) collective-permute-start(bf16[2,2,128,512]{3,2,1,0:T(8,128)(2,1)S(1)} %pad_maximum_fusion.1.refs_0_), channel_id=1, source_target_pairs={{0,4},{4,0},{8,12},{12,8},{16,20},{20,16},{24,28},{28,24},{32,36},... | collective-permute-start | bytes 1572872 | tf_op jit(solution)/shard_map/ppermute | solution.py:18
  34.5 19.8 %collective-permute-start.29 = (bf16[2,2,128,512]{3,2,1,0:T(8,128)(2,1)S(1)}, bf16[2,2,128,512]{3,2,1,0:T(8,128)(2,1)S(1)}, u32[]{:S(2)}, u32[]{:S(2)}) collective-permute-start(bf16[2,2,128,512]{3,2,1,0:T(8,128)(2,1)S(1)} %pad_maximum_fusion.1.refs_0_), channel_id=1, source_target_pairs={{0,8},{4,12},{8,16},{12,20},{16,24},{20,28},{24,0},{28,4},{32,40},... | collective-permute-start | bytes 1572872 | tf_op jit(solution)/shard_map/ppermute | solution.py:27
  44.7 15.3 %collective-permute-start.32 = (bf16[2,2,128,512]{3,2,1,0:T(8,128)(2,1)S(1)}, bf16[2,2,128,512]{3,2,1,0:T(8,128)(2,1)}, u32[]{:S(2)}, u32[]{:S(2)}) collective-permute-start(bf16[2,2,128,512]{3,2,1,0:T(8,128)(2,1)S(1)} %constant_dynamic-update-slice_fusion.2.refs_1_), channel_id=1, source_target_pairs={{0,24},{4,28},{8,0},{12,4},{16,8},{20,12},{24,16},{28,20},{32,56},... | collective-permute-start | bytes 1572872 | tf_op jit(solution)/shard_map/ppermute | solution.py:27
  45.7 17.2 %collective-permute-start.30 = (bf16[2,2,128,512]{3,2,1,0:T(8,128)(2,1)S(1)}, bf16[2,2,128,512]{3,2,1,0:T(8,128)(2,1)}, u32[]{:S(2)}, u32[]{:S(2)}) collective-permute-start(bf16[2,2,128,512]{3,2,1,0:T(8,128)(2,1)S(1)} %constant_dynamic-update-slice_fusion.2.refs_1_), channel_id=1, source_target_pairs={{0,8},{4,12},{8,16},{12,20},{16,24},{20,28},{24,0},{28,4},{32,40},... | collective-permute-start | bytes 1572872 | tf_op jit(solution)/shard_map/ppermute | solution.py:27
  47.3 15.6 %collective-permute-start.13 = (bf16[2,2,128,512]{3,2,1,0:T(8,128)(2,1)S(1)}, bf16[2,2,128,512]{3,2,1,0:T(8,128)(2,1)S(1)}, u32[]{:S(2)}, u32[]{:S(2)}) collective-permute-start(bf16[2,2,128,512]{3,2,1,0:T(8,128)(2,1)S(1)} %collective-permute-done.5.refs_4_), channel_id=1, source_target_pairs={{0,4},{4,0},{8,12},{12,8},{16,20},{20,16},{24,28},{28,24},{32,36},... | collective-permute-start | bytes 1572872 | tf_op jit(solution)/shard_map/ppermute | solution.py:18
  63.1 50.9 %collective-permute-start.18 = (bf16[1,1,14,2,128,256]{5,4,3,2,1,0:T(8,128)(2,1)S(1)}, bf16[1,1,14,2,128,256]{5,4,3,2,1,0:T(8,128)(2,1)}, u32[]{:S(2)}, u32[]{:S(2)}) collective-permute-start(bf16[1,1,14,2,128,256]{5,4,3,2,1,0:T(8,128)(2,1)S(1)} %copy-done.12), channel_id=1, source_target_pairs={{0,1},{1,0},{2,3},{3,2},{4,5},{5,4},{6,7},{7,6},{8,9},{9,8},{10,11... | collective-permute-start | bytes 5505032 | tf_op jit(solution)/shard_map/ppermute | solution.py:18
  97.8 16.6 %collective-permute-start.17 = (bf16[7,2,128,128]{3,2,1,0:T(8,128)(2,1)S(1)}, bf16[7,2,128,128]{3,2,1,0:T(8,128)(2,1)S(1)}, u32[]{:S(2)}, u32[]{:S(2)}) collective-permute-start(bf16[7,2,128,128]{3,2,1,0:T(8,128)(2,1)S(1)} %shard_map.100.own), channel_id=1, source_target_pairs={{0,1},{1,0},{2,3},{3,2},{4,5},{5,4},{6,7},{7,6},{8,9},{9,8},{10,11... | collective-permute-start | bytes 1376264 | tf_op jit(solution)/shard_map/ppermute | solution.py:18
  103.8 20.6 %collective-permute-start.20 = (bf16[7,2,128,128]{3,2,1,0:T(8,128)(2,1)S(1)}, bf16[7,2,128,128]{3,2,1,0:T(8,128)(2,1)}, u32[]{:S(2)}, u32[]{:S(2)}) collective-permute-start(bf16[7,2,128,128]{3,2,1,0:T(8,128)(2,1)S(1)} %shard_map.103.own), channel_id=1, source_target_pairs={{0,1},{1,0},{2,3},{3,2},{4,5},{5,4},{6,7},{7,6},{8,9},{9,8},{10,11... | collective-permute-start | bytes 1376264 | tf_op jit(solution)/shard_map/ppermute | solution.py:18
  108.1 29.1 %collective-permute-start.43 = (bf16[7,2,128,128]{3,2,1,0:T(8,128)(2,1)S(1)}, bf16[7,2,128,128]{3,2,1,0:T(8,128)(2,1)S(1)}, u32[]{:S(2)}, u32[]{:S(2)}) collective-permute-start(bf16[7,2,128,128]{3,2,1,0:T(8,128)(2,1)S(1)} %shard_map.109.own), channel_id=1, source_target_pairs={{0,1},{1,0},{2,3},{3,2},{4,5},{5,4},{6,7},{7,6},{8,9},{9,8},{10,11... | collective-permute-start | bytes 1376264 | tf_op jit(solution)/shard_map/ppermute | solution.py:18
  113.8 30.1 %collective-permute-start.45 = (bf16[7,2,128,128]{3,2,1,0:T(8,128)(2,1)S(1)}, bf16[7,2,128,128]{3,2,1,0:T(8,128)(2,1)S(1)}, u32[]{:S(2)}, u32[]{:S(2)}) collective-permute-start(bf16[7,2,128,128]{3,2,1,0:T(8,128)(2,1)S(1)} %shard_map.112.own), channel_id=1, source_target_pairs={{0,1},{1,0},{2,3},{3,2},{4,5},{5,4},{6,7},{7,6},{8,9},{9,8},{10,11... | collective-permute-start | bytes 1376264 | tf_op jit(solution)/shard_map/ppermute | solution.py:18
  119.8 34.9 %collective-permute-start.19 = (bf16[7,2,128,128]{3,2,1,0:T(8,128)(2,1)S(1)}, bf16[7,2,128,128]{3,2,1,0:T(8,128)(2,1)S(1)}, u32[]{:S(2)}, u32[]{:S(2)}) collective-permute-start(bf16[7,2,128,128]{3,2,1,0:T(8,128)(2,1)S(1)} %get-tuple-element.18), channel_id=1, source_target_pairs={{0,3},{1,2},{2,1},{3,0},{4,7},{5,6},{6,5},{7,4},{8,11},{9,10},{10,... | collective-permute-start | bytes 1376264 | tf_op jit(solution)/shard_map/ppermute | solution.py:18
  128.9 30.1 %collective-permute-start.21 = (bf16[7,2,128,128]{3,2,1,0:T(8,128)(2,1)S(1)}, bf16[7,2,128,128]{3,2,1,0:T(8,128)(2,1)S(1)}, u32[]{:S(2)}, u32[]{:S(2)}) collective-permute-start(bf16[7,2,128,128]{3,2,1,0:T(8,128)(2,1)S(1)} %get-tuple-element.20), channel_id=1, source_target_pairs={{0,3},{1,2},{2,1},{3,0},{4,7},{5,6},{6,5},{7,4},{8,11},{9,10},{10,... | collective-permute-start | bytes 1376264 | tf_op jit(solution)/shard_map/ppermute | solution.py:18
  133.2 33.3 %collective-permute-start.24 = (bf16[2,256,256]{2,1,0:T(8,128)(2,1)}, bf16[2,256,256]{2,1,0:T(8,128)(2,1)S(1)}, u32[]{:S(2)}, u32[]{:S(2)}) collective-permute-start(bf16[2,256,256]{2,1,0:T(8,128)(2,1)} %get-tuple-element.33), channel_id=1, source_target_pairs={{1,0},{2,1},{3,2},{4,3},{5,4},{6,5},{7,6},{8,7},{9,8},{10,9},{11,1... | collective-permute-start | bytes 786440 | tf_op jit(solution)/shard_map/ppermute | solution.py:367
  137.2 29.2 %collective-permute-start.23 = (bf16[2,256,256]{2,1,0:T(8,128)(2,1)}, bf16[2,256,256]{2,1,0:T(8,128)(2,1)S(1)}, u32[]{:S(2)}, u32[]{:S(2)}) collective-permute-start(bf16[2,256,256]{2,1,0:T(8,128)(2,1)} %get-tuple-element.34), channel_id=1, source_target_pairs={{0,1},{1,2},{2,3},{3,4},{4,5},{5,6},{6,7},{7,8},{8,9},{9,10},{10,1... | collective-permute-start | bytes 786440 | tf_op jit(solution)/shard_map/ppermute | solution.py:366
  144.0 25.7 %collective-permute-start.44 = (bf16[7,2,128,128]{3,2,1,0:T(8,128)(2,1)S(1)}, bf16[7,2,128,128]{3,2,1,0:T(8,128)(2,1)}, u32[]{:S(2)}, u32[]{:S(2)}) collective-permute-start(bf16[7,2,128,128]{3,2,1,0:T(8,128)(2,1)S(1)} %get-tuple-element.24), channel_id=1, source_target_pairs={{0,3},{1,2},{2,1},{3,0},{4,7},{5,6},{6,5},{7,4},{8,11},{9,10},{10,... | collective-permute-start | bytes 1376264 | tf_op jit(solution)/shard_map/ppermute | solution.py:18
  154.7 18.4 %collective-permute-start.46 = (bf16[7,2,128,128]{3,2,1,0:T(8,128)(2,1)S(1)}, bf16[7,2,128,128]{3,2,1,0:T(8,128)(2,1)}, u32[]{:S(2)}, u32[]{:S(2)}) collective-permute-start(bf16[7,2,128,128]{3,2,1,0:T(8,128)(2,1)S(1)} %get-tuple-element.26), channel_id=1, source_target_pairs={{0,3},{1,2},{2,1},{3,0},{4,7},{5,6},{6,5},{7,4},{8,11},{9,10},{10,... | collective-permute-start | bytes 1376264 | tf_op jit(solution)/shard_map/ppermute | solution.py:18
  166.3 25.0 %collective-permute-start.22 = (bf16[2,2,128,512]{3,2,1,0:T(8,128)(2,1)S(1)}, bf16[2,2,128,512]{3,2,1,0:T(8,128)(2,1)S(1)}, u32[]{:S(2)}, u32[]{:S(2)}) collective-permute-start(bf16[2,2,128,512]{3,2,1,0:T(8,128)(2,1)S(1)} %get-tuple-element.22), channel_id=1, source_target_pairs={{0,1},{1,0},{2,3},{3,2},{4,5},{5,4},{6,7},{7,6},{8,9},{9,8},{10,11... | collective-permute-start | bytes 1572872 | tf_op jit(solution)/shard_map/ppermute | solution.py:18
  181.0 16.3 %collective-permute-start.47 = (bf16[1,2,128,512]{3,2,1,0:T(8,128)(2,1)S(1)}, bf16[1,2,128,512]{3,2,1,0:T(8,128)(2,1)S(1)}, u32[]{:S(2)}, u32[]{:S(2)}) collective-permute-start(bf16[1,2,128,512]{3,2,1,0:T(8,128)(2,1)S(1)} %shard_map.116), channel_id=1, source_target_pairs={{0,1},{1,0},{2,3},{3,2},{4,5},{5,4},{6,7},{7,6},{8,9},{9,8},{10,11... | collective-permute-start | bytes 786440 | tf_op jit(solution)/shard_map/ppermute | solution.py:18
  (69 other events, 1286.7 us)

commit v2 on v0

v2 whole, which is shorter than its diff:
```python
import functools

import jax
import jax.numpy as jnp
from jax import lax
from jax.experimental import pallas as pl
from jax.experimental.pallas import tpu as pltpu
from jax.sharding import PartitionSpec as P


F32 = jnp.float32
BF16 = jnp.bfloat16
SIDE = 4
SHIFT = {"x": 1, "y": 3}


def swap(value, axis, mask):
    return lax.ppermute(value, axis, [(i, i ^ mask) for i in range(lax.axis_size(axis))])


def ring(value, axis, by):
    at = SHIFT[axis]
    perm = []
    for i in range(lax.axis_size("grp")):
        v = (i >> at) & (SIDE - 1)
        perm.append((i, i + ((((v + by) % SIDE) - v) << at)))
    return lax.ppermute(value, "grp", perm)


def nt(left, right):
    return lax.dot_general(left, right, (((1,), (1,)), ((), ())), preferred_element_type=F32)


VMEM = pl.BlockSpec(memory_space=pltpu.VMEM)
SMEM = pl.BlockSpec(memory_space=pltpu.SMEM)


def size(v):
    return v.size * v.dtype.itemsize


def call(body, scalars, arrays, out_shape, scratch=(), space=None, room=0):
    space = space or [pltpu.VMEM] * len(arrays)
    inside = [v for v, at in zip(arrays, space) if at == pltpu.VMEM]
    room += sum(size(v) for v in jax.tree.leaves(out_shape) + inside) + (2 << 20)
    return pl.pallas_call(
        body,
        in_specs=[SMEM] * len(scalars) + [pl.BlockSpec(memory_space=at) for at in space],
        out_specs=jax.tree.map(lambda _: VMEM, out_shape),
        out_shape=out_shape,
        scratch_shapes=scratch,
        compiler_params=pltpu.CompilerParams(vmem_limit_bytes=room),
        cost_estimate=pl.CostEstimate(flops=0, bytes_accessed=0, transcendentals=0),
    )(
        *scalars,
        *(
            pltpu.with_memory_space_constraint(v, at) if at == pltpu.HBM else v
            for v, at in zip(arrays, space)
        ),
    )


def near_body(mask, x, low, high, blocks, out):
    nrhs = x.shape[1]
    leaf = blocks.shape[-1]
    rows = nrhs // 4

    def step(t, carry):
        at = pl.ds(pl.multiple_of(t * rows, rows), rows)
        seq = [low[:, at, :]]
        seq += [x[:, at, i * leaf : (i + 1) * leaf] for i in range(2)]
        seq += [high[:, at, :]]
        seq = [v.reshape(2 * rows, leaf) for v in seq]
        for i in range(2):
            real = jnp.zeros((rows, leaf), F32)
            imag = jnp.zeros((rows, leaf), F32)
            for j in range(3):
                p = nt(seq[i + j], blocks[i, j].reshape(2 * leaf, leaf))
                w = mask[i, j].astype(F32)
                real += w * (p[:rows, :leaf] - p[rows:, leaf:])
                imag += w * (p[rows:, :leaf] + p[:rows, leaf:])
            out[0, at, i * leaf : (i + 1) * leaf] = real
            out[1, at, i * leaf : (i + 1) * leaf] = imag
        return carry

    lax.fori_loop(0, 4, step, 0)


def near_field(mask, x, low, high, blocks):
    _, nrhs, rows = x.shape
    return call(
        near_body, [mask], [x, low, high, blocks],
        jax.ShapeDtypeStruct((2, nrhs, rows), F32),
    )


def level0_body(color, base, count, src, rank, *refs):
    bufs, w, out = refs[:16], refs[16], refs[17]
    xs, sems = refs[18:]
    me = lax.axis_index("grp")
    k = w.shape[-2]
    n = xs.shape[2]

    def fetch(i, carry):
        f = i + base
        s = src[f, me]
        dx = (((s >> 1) & 3) - ((me >> 1) & 3)) & 3
        dy = (((s >> 3) & 3) - ((me >> 3) & 3)) & 3
        dx, dy = (jnp.where(v == 0, 0, jnp.where(v == 3, 1, v + 1)) for v in (dx, dy))
        first, second = (dx, dy) if color == 0 else (dy, dx)
        which = 2 * second + (first >> 1) + 8 * ((s ^ me) & 1)
        for t in range(16):

            @pl.when(which == t)
            def _():
                pltpu.make_async_copy(bufs[t].at[first & 1], xs.at[i], sems.at[i]).start()

        return carry

    lax.fori_loop(0, count, fetch, 0)
    for i in range(count):
        pltpu.make_async_copy(bufs[0].at[0], xs.at[i], sems.at[i]).wait()
        p = nt(xs[i].reshape(2 * n, xs.shape[3]), w[0, 0, base + i].reshape(2 * k, w.shape[-1]))
        live = lax.broadcasted_iota(jnp.int32, (n, k), 1) < rank[0, base + i]
        out[i, 0], out[i, 1] = combine(p, n, k, live)


def level0(color, base, count, src, rank, bufs, w):
    _, _, n, rows = bufs[0].shape
    k = w.shape[-2]
    return call(
        functools.partial(level0_body, color, base, count),
        [src, rank], [*bufs, w],
        jax.ShapeDtypeStruct((count, 2, n, k), BF16),
        [
            pltpu.VMEM((count, 2, n, rows), BF16),
            pltpu.SemaphoreType.DMA((count,)),
        ],
        space=[pl.ANY] * 16 + [pltpu.VMEM],
        room=count * 2 * rows * n * 2,
    )


def combine(p, n, k, live):
    zero = jnp.zeros((n, k), F32)
    real = jnp.where(live, p[:n, :k] - p[n:, k:], zero).astype(BF16)
    imag = jnp.where(live, p[n:, :k] + p[:n, k:], zero).astype(BF16)
    return real, imag


def section_body(base, bit, rank, own, other, *refs):
    upper = (lax.axis_index("mem") >> bit) & 1 == 1
    half = len(refs) // 2
    ws, outs = refs[:half], refs[half:]
    count, _, n, k = own.shape
    for i in range(count):
        a = own[i].reshape(2 * n, k)
        b = other[i].reshape(2 * n, k)
        x = jnp.concatenate([jnp.where(upper, b, a), jnp.where(upper, a, b)], axis=1)
        live = lax.broadcasted_iota(jnp.int32, (n, k), 1) < rank[0, base + i]
        for w, out in zip(ws, outs):
            p = nt(x, w[0, 0, base + i].reshape(2 * k, 2 * k))
            out[i, 0], out[i, 1] = combine(p, n, k, live)


def section(base, bit, rank, own, other, ws):
    shape = jax.ShapeDtypeStruct(own.shape, BF16)
    return call(
        functools.partial(section_body, base, bit),
        [rank], [own, other, *ws], [shape] * len(ws),
    )


def fill(xs, f, real, imag):
    n = real.shape[0]
    xs[f, :n] = jnp.concatenate([real, -imag], 1)
    xs[f, n:] = jnp.concatenate([imag, real], 1)


def outward_apply(dtype, order, xs, w, out):
    member = lax.axis_index("mem")
    n = xs.shape[1] // 2
    step = 256
    piece = out.shape[3]
    per = piece // step

    def body(b, carry):
        mask = order[0]
        for p in range(1, len(order)):
            mask = jnp.where(b // per == p, order[p], mask)
        start = pl.multiple_of((member ^ mask) * piece + (b % per) * step, step)
        rows = pl.ds(start, step)
        acc = jnp.zeros((2 * n, step), F32)
        for f in range(xs.shape[0]):
            acc += nt(xs[f], jnp.concatenate([w[0, 0, f, 0, rows], w[0, 0, f, 1, rows]], 1))
        to = pl.ds(pl.multiple_of((b % per) * step, step), step)
        out[b // per, 0, :, to] = acc[:n].astype(dtype)
        out[b // per, 1, :, to] = acc[n:].astype(dtype)
        return carry

    lax.fori_loop(0, out.shape[0] * per, body, 0)


def first_body(base, order, rank, ready, own, other, s2, w, xs, out):
    for i in range(base):
        fill(xs, i, ready[i, 0], ready[i, 1])
    count, _, n, k = own.shape
    upper = (lax.axis_index("mem") >> 1) & 1 == 1
    for i in range(count):
        a = own[i].reshape(2 * n, k)
        b = other[i].reshape(2 * n, k)
        x = jnp.concatenate([jnp.where(upper, b, a), jnp.where(upper, a, b)], axis=1)
        live = lax.broadcasted_iota(jnp.int32, (n, k), 1) < rank[0, base + i]
        p = nt(x, s2[0, 0, base + i].reshape(2 * k, 2 * k))
        fill(xs, base + i, *combine(p, n, k, live))
    outward_apply(BF16, order, xs, w, out)


def first_outward(order, rank, ready, own, other, s2, w):
    count, _, n, k = own.shape
    base = ready.shape[0]
    far = base + count
    return call(
        functools.partial(first_body, base, order),
        [rank], [ready, own, other, s2, w],
        [
            jax.ShapeDtypeStruct((far, 2 * n, 2 * k), BF16),
            jax.ShapeDtypeStruct((len(order), 2, n, w.shape[4] // 4), BF16),
        ],
    )


def outward(dtype, order, xs, w):
    shape = (len(order), 2, xs.shape[1] // 2, w.shape[4] // 4)
    return call(
        functools.partial(outward_apply, dtype, order),
        [], [xs, w], jax.ShapeDtypeStruct(shape, dtype),
    )


def final_body(first, base, last, out):
    n = first.shape[1]
    out[:, :n] = first[...]
    out[:, n:] = (base[...] + last[...].astype(F32)).astype(BF16)


def final(first, base, last):
    parts, n, rows = first.shape
    return call(
        final_body, [], [first, base, last],
        jax.ShapeDtypeStruct((parts, 2 * n, rows), BF16),
    )


def gather(color, block):
    one, two = ("x", "y") if color == 0 else ("y", "x")
    below = ring(block, one, 1)
    above = ring(block, one, -1)
    opposite = ring(block, one, 2)
    lo = jnp.concatenate([block, below], 0)
    hi = jnp.concatenate([above, opposite], 0)
    below_lo = ring(lo, two, 1)
    above_hi = ring(hi, two, -1)
    below_hi = ring(hi, two, 1)
    above_lo = ring(lo, two, -1)
    far_lo = ring(below_lo, two, 1)
    far_hi = ring(above_hi, two, -1)
    mine = [lo, hi, below_lo, below_hi, above_lo, above_hi, far_lo, far_hi]
    return mine + [swap(v, "grp", 1) for v in mine]


def on_device(
    incident,
    near_blocks,
    near_mask,
    far_source,
    far_rank,
    basis_in,
    section_one,
    section_two,
    basis_out,
):
    _, nrhs, rows = incident.shape
    leaf = near_blocks.shape[3]
    far = basis_in.shape[2]
    q = nrhs // 4

    bufs = [gather(c, incident[None, :, 2 * c * q : 2 * (c + 1) * q]) for c in range(2)]
    section_pair = swap(section_one, "mem", 1)

    axes = ("grp", "mem")
    total = lax.axis_size("grp") * lax.axis_size("mem")
    forward = [(i, i + 1) for i in range(total - 1)]
    backward = [(i + 1, i) for i in range(total - 1)]
    low = lax.ppermute(incident[:, :, rows - leaf :], axes, forward)
    high = lax.ppermute(incident[:, :, :leaf], axes, backward)
    near = near_field(near_mask, incident, low, high, near_blocks)

    cut = far // 2
    spans = ((0, cut), (cut, far - cut))

    pieces = []
    for h in range(2):
        at = slice(2 * h * q, 2 * (h + 1) * q)
        level1 = []
        for base, count in spans:
            lev0 = level0(h, base, count, far_source.T, far_rank, bufs[h], basis_in)
            lev0_pair = swap(lev0, "mem", 1)
            lev1, lev1_pair = section(
                base, 0, far_rank, lev0, lev0_pair, [section_one, section_pair]
            )
            level1.append((lev1, swap(lev1_pair, "mem", 3)))
        (ready,) = section(0, 1, far_rank, *level1[0], [section_two])
        early = 2 - h
        xs, sent = first_outward(
            (2, 1)[:early], far_rank, ready, *level1[1],
            section_two, basis_out,
        )
        sent = swap(sent, "mem", 1)
        if h == 0:
            sent = (sent[0], sent[1])
        else:
            part = outward(BF16, (1,), xs, basis_out)
            sent = (sent[0], swap(part, "mem", 1)[0])
        other = outward(F32, (3,), xs, basis_out)[0]
        last = swap((other + sent[0].astype(F32)).astype(BF16), "mem", 3)
        kept = outward(F32, (0,), xs, basis_out)[0]
        pieces.append((kept + sent[1].astype(F32) + near[:, at], last))
    base, last = pieces[0]
    return final((base + last.astype(F32)).astype(BF16), *pieces[1])


def solution(mesh):
    placed = (
        P(None, None, ("grp", "mem")),
        P(("grp", "mem"), None, None, None, None),
        P(("grp", "mem"), None),
        P(),
        P("grp", None),
        P("grp", "mem", None, None, None, None),
        P("grp", "mem", None, None, None, None),
        P("grp", "mem", None, None, None, None),
        P("grp", "mem", None, None, None, None),
    )

    return jax.shard_map(
        on_device,
        mesh=mesh,
        in_specs=placed,
        out_specs=P(None, None, ("grp", "mem")),
        check_vma=False,
    )
```

time: 197 us -> 202 us (1.025)
  the two profiles are of different devices: /device:TPU:7 before, /device:TPU:6 now
where the time goes in v2:
time: 202 us
  waiting for transfers between devices  101 us (50%)
  starting transfers between devices  58.9 us (29%)
  Pallas kernels  39.2 us (19%)
    ppermute x18, waiting for transfers between devices, ring(): return lax.ppermute(value, 'grp', perm)  59.1 us
    ppermute x30, waiting for transfers between devices, swap(): lax.ppermute(value, axis, [(i, i ^ mask) for i in range(lax.axis_size(axi...  42 us
    pallas_call x19, Pallas kernels, call(): pl.pallas_call(body, in_specs=[SMEM] * len(scalars) + [pl.BlockSpec(memor...  39.2 us
    ppermute x30, starting transfers between devices, swap(): lax.ppermute(value, axis, [(i, i ^ mask) for i in range(lax.axis_size(axi...  26.6 us
    ppermute x18, starting transfers between devices, ring(): return lax.ppermute(value, 'grp', perm)  26.3 us
    ppermute x1, starting transfers between devices, on_device(): low = lax.ppermute(incident[:, :, rows - leaf:], axes, forward)  4.14 us
  transfers between devices with their start and end apart: 50, of which 21 were waited for; matrix products, arithmetic and copies ran while one was open for 0% of the time, Pallas kernels for 19%

profile of v2, /device:TPU:6, one launch (start us, length us, event | category | flops | bytes accessed | tf_op | source)
XLA Modules:
  0.0 201.5 jit_solution(14074478440087511654)
XLA Ops:
  1.5 3.3 %collective-permute-start.28 = (bf16[1,2,128,512]{3,2,1,0:T(8,128)(2,1)S(1)}, bf16[1,2,128,512]{3,2,1,0:T(8,128)(2,1)S(1)}, u32[]{:S(2)}, u32[]{:S(2)}) collective-permute-start(bf16[1,2,128,512]{3,2,1,0:T(8,128)(2,1)S(1)} %get-tuple-element.31), channel_id=1, source_target_pairs={{0,64},{4,68},{8,72},{12,76},{16,80},{20,84},{24,88},{28,92},{32,9... | collective-permute-start | bytes 786440 | tf_op jit(solution)/shard_map/ppermute | solution.py:27
  10.8 4.5 %collective-permute-start.5 = (bf16[2,2,128,512]{3,2,1,0:T(8,128)(2,1)S(1)}, bf16[2,2,128,512]{3,2,1,0:T(8,128)(2,1)S(1)}, u32[]{:S(2)}, u32[]{:S(2)}) collective-permute-start(bf16[2,2,128,512]{3,2,1,0:T(8,128)(2,1)S(1)} %pad_maximum_fusion.refs_0_), channel_id=1, source_target_pairs={{0,96},{4,100},{8,104},{12,108},{16,112},{20,116},{24,120},{28,124... | collective-permute-start | bytes 1572872 | tf_op jit(solution)/shard_map/ppermute | solution.py:27
  15.3 3.8 %collective-permute-done.1 = bf16[1,2,128,512]{3,2,1,0:T(8,128)(2,1)S(1)} collective-permute-done((bf16[1,2,128,512]{3,2,1,0:T(8,128)(2,1)S(1)}, bf16[1,2,128,512]{3,2,1,0:T(8,128)(2,1)S(1)}, u32[]{:S(2)}, u32[]{:S(2)}) %collective-permute-start.1) | collective-permute-done | bytes 262176 | tf_op jit(solution)/shard_map/ppermute | solution.py:27
  20.0 16.6 %collective-permute-done.26 = bf16[1,2,128,512]{3,2,1,0:T(8,128)(2,1)S(1)} collective-permute-done((bf16[1,2,128,512]{3,2,1,0:T(8,128)(2,1)S(1)}, bf16[1,2,128,512]{3,2,1,0:T(8,128)(2,1)S(1)}, u32[]{:S(2)}, u32[]{:S(2)}) %collective-permute-start.26) | collective-permute-done | bytes 262176 | tf_op jit(solution)/shard_map/ppermute | solution.py:27
  42.2 3.7 %collective-permute-done.6.refs_5_ = bf16[2,2,128,512]{3,2,1,0:T(8,128)(2,1)S(1)} collective-permute-done((bf16[2,2,128,512]{3,2,1,0:T(8,128)(2,1)S(1)}, bf16[2,2,128,512]{3,2,1,0:T(8,128)(2,1)S(1)}, u32[]{:S(2)}, u32[]{:S(2)}) %collective-permute-start.6) | collective-permute-done | bytes 524320 | tf_op jit(solution)/shard_map/ppermute | solution.py:27
  47.9 3.2 %collective-permute-start.30 = (bf16[2,2,128,512]{3,2,1,0:T(8,128)(2,1)S(1)}, bf16[2,2,128,512]{3,2,1,0:T(8,128)(2,1)S(1)}, u32[]{:S(2)}, u32[]{:S(2)}) collective-permute-start(bf16[2,2,128,512]{3,2,1,0:T(8,128)(2,1)S(1)} %constant_dynamic-update-slice_fusion.2.refs_1_), channel_id=1, source_target_pairs={{0,8},{4,12},{8,16},{12,20},{16,24},{20,28},{24,0},{28,4},{32,40},... | collective-permute-start | bytes 1572872 | tf_op jit(solution)/shard_map/ppermute | solution.py:27
  51.1 3.8 %collective-permute-done.31.refs_4_ = bf16[2,2,128,512]{3,2,1,0:T(8,128)(2,1)S(1)} collective-permute-done((bf16[2,2,128,512]{3,2,1,0:T(8,128)(2,1)S(1)}, bf16[2,2,128,512]{3,2,1,0:T(8,128)(2,1)S(1)}, u32[]{:S(2)}, u32[]{:S(2)}) %collective-permute-start.31) | collective-permute-done | bytes 524320 | tf_op jit(solution)/shard_map/ppermute | solution.py:27
  57.1 8.5 %collective-permute-done.32.refs_5_ = bf16[2,2,128,512]{3,2,1,0:T(8,128)(2,1)S(1)} collective-permute-done((bf16[2,2,128,512]{3,2,1,0:T(8,128)(2,1)S(1)}, bf16[2,2,128,512]{3,2,1,0:T(8,128)(2,1)S(1)}, u32[]{:S(2)}, u32[]{:S(2)}) %collective-permute-start.32) | collective-permute-done | bytes 524320 | tf_op jit(solution)/shard_map/ppermute | solution.py:27
  69.4 10.9 %collective-permute-done.7.refs_6_ = bf16[2,2,128,512]{3,2,1,0:T(8,128)(2,1)S(1)} collective-permute-done((bf16[2,2,128,512]{3,2,1,0:T(8,128)(2,1)S(1)}, bf16[2,2,128,512]{3,2,1,0:T(8,128)(2,1)S(1)}, u32[]{:S(2)}, u32[]{:S(2)}) %collective-permute-start.7) | collective-permute-done | bytes 524320 | tf_op jit(solution)/shard_map/ppermute | solution.py:27
  84.2 3.8 %shard_map.91.own = bf16[7,2,128,128]{3,2,1,0:T(8,128)(2,1)S(1)} custom-call(s32[14,32]{1,0:T(8,128)S(1)} %bitcast.15, s32[1,14]{1,0:T(1,128)S(1)} %copy-done.6, bf16[2,2,128,512]{3,2,1,0:T(8,128)(2,1)S(1)} %pad_maximum_fusion.refs_0_, bf16[2,2,128,512]{3,2,1,0:T(8,128)(2,1)S(1)} %constant_dynamic-update-slice_fusion.refs_1_, ...), custom_call_target="tpu_custom_call" | custom-call | tf_op jit(solution)/shard_map/pallas_call | solution.py:46
  90.2 5.9 %collective-permute-done.33.refs_6_ = bf16[2,2,128,512]{3,2,1,0:T(8,128)(2,1)S(1)} collective-permute-done((bf16[2,2,128,512]{3,2,1,0:T(8,128)(2,1)S(1)}, bf16[2,2,128,512]{3,2,1,0:T(8,128)(2,1)S(1)}, u32[]{:S(2)}, u32[]{:S(2)}) %collective-permute-start.33) | collective-permute-done | bytes 524320 | tf_op jit(solution)/shard_map/ppermute | solution.py:27
  98.6 3.8 %shard_map.94.own = bf16[7,2,128,128]{3,2,1,0:T(8,128)(2,1)S(1)} custom-call(s32[14,32]{1,0:T(8,128)S(1)} %bitcast.16, s32[1,14]{1,0:T(1,128)S(1)} %copy-done.6, bf16[2,2,128,512]{3,2,1,0:T(8,128)(2,1)S(1)} %pad_maximum_fusion.refs_0_, bf16[2,2,128,512]{3,2,1,0:T(8,128)(2,1)S(1)} %constant_dynamic-update-slice_fusion.refs_1_, ...), custom_call_target="tpu_custom_call" | custom-call | tf_op jit(solution)/shard_map/pallas_call | solution.py:46
  102.4 5.2 %collective-permute-done.17.other = bf16[7,2,128,128]{3,2,1,0:T(8,128)(2,1)S(1)} collective-permute-done((bf16[7,2,128,128]{3,2,1,0:T(8,128)(2,1)S(1)}, bf16[7,2,128,128]{3,2,1,0:T(8,128)(2,1)S(1)}, u32[]{:S(2)}, u32[]{:S(2)}) %collective-permute-start.17) | collective-permute-done | bytes 458784 | tf_op jit(solution)/shard_map/ppermute | solution.py:18
  110.6 9.3 %collective-permute-done.20.other = bf16[7,2,128,128]{3,2,1,0:T(8,128)(2,1)S(1)} collective-permute-done((bf16[7,2,128,128]{3,2,1,0:T(8,128)(2,1)S(1)}, bf16[7,2,128,128]{3,2,1,0:T(8,128)(2,1)S(1)}, u32[]{:S(2)}, u32[]{:S(2)}) %collective-permute-start.20) | collective-permute-done | bytes 458784 | tf_op jit(solution)/shard_map/ppermute | solution.py:18
  119.8 3.7 %collective-permute-start.19 = (bf16[7,2,128,128]{3,2,1,0:T(8,128)(2,1)S(1)}, bf16[7,2,128,128]{3,2,1,0:T(8,128)(2,1)S(1)}, u32[]{:S(2)}, u32[]{:S(2)}) collective-permute-start(bf16[7,2,128,128]{3,2,1,0:T(8,128)(2,1)S(1)} %get-tuple-element.18), channel_id=1, source_target_pairs={{0,3},{1,2},{2,1},{3,0},{4,7},{5,6},{6,5},{7,4},{8,11},{9,10},{10,... | collective-permute-start | bytes 1376264 | tf_op jit(solution)/shard_map/ppermute | solution.py:18
  124.9 3.8 %shard_map.100.own = bf16[7,2,128,128]{3,2,1,0:T(8,128)(2,1)S(1)} custom-call(s32[14,32]{1,0:T(8,128)S(1)} %bitcast.17, s32[1,14]{1,0:T(1,128)S(1)} %copy-done.6, bf16[2,2,128,512]{3,2,1,0:T(8,128)(2,1)S(1)} %pad_maximum_fusion.1.refs_0_, bf16[2,2,128,512]{3,2,1,0:T(8,128)(2,1)S(1)} %constant_dynamic-update-slice_fusion.2.refs_1_, ...), custom_call_target="tpu_custom_call" | custom-call | tf_op jit(solution)/shard_map/pallas_call | solution.py:46
  128.9 3.8 %shard_map.103.own = bf16[7,2,128,128]{3,2,1,0:T(8,128)(2,1)S(1)} custom-call(s32[14,32]{1,0:T(8,128)S(1)} %bitcast.18, s32[1,14]{1,0:T(1,128)S(1)} %copy-done.6, bf16[2,2,128,512]{3,2,1,0:T(8,128)(2,1)S(1)} %pad_maximum_fusion.1.refs_0_, bf16[2,2,128,512]{3,2,1,0:T(8,128)(2,1)S(1)} %constant_dynamic-update-slice_fusion.2.refs_1_, ...), custom_call_target="tpu_custom_call" | custom-call | tf_op jit(solution)/shard_map/pallas_call | solution.py:46
  135.9 6.9 %collective-permute-done.21.other = bf16[7,2,128,128]{3,2,1,0:T(8,128)(2,1)S(1)} collective-permute-done((bf16[7,2,128,128]{3,2,1,0:T(8,128)(2,1)S(1)}, bf16[7,2,128,128]{3,2,1,0:T(8,128)(2,1)S(1)}, u32[]{:S(2)}, u32[]{:S(2)}) %collective-permute-start.21) | collective-permute-done | bytes 458784 | tf_op jit(solution)/shard_map/ppermute | solution.py:18
  142.9 3.9 %shard_map.96 = (bf16[14,256,256]{2,1,0:T(8,128)(2,1)S(1)}, bf16[2,2,128,512]{3,2,1,0:T(8,128)(2,1)S(1)}) custom-call(s32[1,14]{1,0:T(1,128)S(1)} %copy-done.6, bf16[7,2,128,128]{3,2,1,0:T(8,128)(2,1)S(1)} %shard_map.93.ready, bf16[7,2,128,128]{3,2,1,0:T(8,128)(2,1)S(1)} %get-tuple-element.19.own, ...), custom_call_target="tpu_custom_call" | custom-call | tf_op jit(solution)/shard_map/pallas_call | solution.py:46
  152.8 3.2 %collective-permute-start.46 = (bf16[7,2,128,128]{3,2,1,0:T(8,128)(2,1)S(1)}, bf16[7,2,128,128]{3,2,1,0:T(8,128)(2,1)S(1)}, u32[]{:S(2)}, u32[]{:S(2)}) collective-permute-start(bf16[7,2,128,128]{3,2,1,0:T(8,128)(2,1)S(1)} %get-tuple-element.26), channel_id=1, source_target_pairs={{0,3},{1,2},{2,1},{3,0},{4,7},{5,6},{6,5},{7,4},{8,11},{9,10},{10,... | collective-permute-start | bytes 1376264 | tf_op jit(solution)/shard_map/ppermute | solution.py:18
  158.1 4.1 %collective-permute-start.23 = (bf16[2,256,256]{2,1,0:T(8,128)(2,1)S(1)}, bf16[2,256,256]{2,1,0:T(8,128)(2,1)S(1)}, u32[]{:S(2)}, u32[]{:S(2)}) collective-permute-start(bf16[2,256,256]{2,1,0:T(8,128)(2,1)S(1)} %get-tuple-element.34), channel_id=1, source_target_pairs={{0,1},{1,2},{2,3},{3,4},{4,5},{5,6},{6,7},{7,8},{8,9},{9,10},{10,1... | collective-permute-start | bytes 786440 | tf_op jit(solution)/shard_map/ppermute | solution.py:295
  165.8 8.6 %collective-permute-done.46.other = bf16[7,2,128,128]{3,2,1,0:T(8,128)(2,1)S(1)} collective-permute-done((bf16[7,2,128,128]{3,2,1,0:T(8,128)(2,1)S(1)}, bf16[7,2,128,128]{3,2,1,0:T(8,128)(2,1)S(1)}, u32[]{:S(2)}, u32[]{:S(2)}) %collective-permute-start.46) | collective-permute-done | bytes 458784 | tf_op jit(solution)/shard_map/ppermute | solution.py:18
  181.8 3.8 %collective-permute-start.25 = (bf16[2,128,512]{2,1,0:T(8,128)(2,1)S(1)}, bf16[2,128,512]{2,1,0:T(8,128)(2,1)S(1)}, u32[]{:S(2)}, u32[]{:S(2)}) collective-permute-start(bf16[2,128,512]{2,1,0:T(8,128)(2,1)S(1)} %fusion.2), channel_id=1, source_target_pairs={{0,3},{1,2},{2,1},{3,0},{4,7},{5,6},{6,5},{7,4},{8,11},{9,10},{10,... | collective-permute-start | bytes 786440 | tf_op jit(solution)/shard_map/ppermute | solution.py:18
  193.4 7.2 %collective-permute-done.49.last = bf16[2,128,512]{2,1,0:T(8,128)(2,1)S(1)} collective-permute-done((bf16[2,128,512]{2,1,0:T(8,128)(2,1)S(1)}, bf16[2,128,512]{2,1,0:T(8,128)(2,1)S(1)}, u32[]{:S(2)}, u32[]{:S(2)}) %collective-permute-start.49) | collective-permute-done | bytes 262176 | tf_op jit(solution)/shard_map/ppermute | solution.py:18
  (131 shorter events, 65.7 us)
Async XLA Ops:
  10.0 27.5 %collective-permute-start.9 = (bf16[2,2,128,512]{3,2,1,0:T(8,128)(2,1)S(1)}, bf16[2,2,128,512]{3,2,1,0:T(8,128)(2,1)S(1)}, u32[]{:S(2)}, u32[]{:S(2)}) collective-permute-start(bf16[2,2,128,512]{3,2,1,0:T(8,128)(2,1)S(1)} %pad_maximum_fusion.refs_0_), channel_id=1, source_target_pairs={{0,4},{4,0},{8,12},{12,8},{16,20},{20,16},{24,28},{28,24},{32,36},... | collective-permute-start | bytes 1572872 | tf_op jit(solution)/shard_map/ppermute | solution.py:18
  10.8 28.0 %collective-permute-start.5 = (bf16[2,2,128,512]{3,2,1,0:T(8,128)(2,1)S(1)}, bf16[2,2,128,512]{3,2,1,0:T(8,128)(2,1)S(1)}, u32[]{:S(2)}, u32[]{:S(2)}) collective-permute-start(bf16[2,2,128,512]{3,2,1,0:T(8,128)(2,1)S(1)} %pad_maximum_fusion.refs_0_), channel_id=1, source_target_pairs={{0,96},{4,100},{8,104},{12,108},{16,112},{20,116},{24,120},{28,124... | collective-permute-start | bytes 1572872 | tf_op jit(solution)/shard_map/ppermute | solution.py:27
  19.1 19.7 %collective-permute-start.3 = (bf16[2,2,128,512]{3,2,1,0:T(8,128)(2,1)S(1)}, bf16[2,2,128,512]{3,2,1,0:T(8,128)(2,1)S(1)}, u32[]{:S(2)}, u32[]{:S(2)}) collective-permute-start(bf16[2,2,128,512]{3,2,1,0:T(8,128)(2,1)S(1)} %pad_maximum_fusion.refs_0_), channel_id=1, source_target_pairs={{0,32},{4,36},{8,40},{12,44},{16,48},{20,52},{24,56},{28,60},{32,6... | collective-permute-start | bytes 1572872 | tf_op jit(solution)/shard_map/ppermute | solution.py:27
  19.8 16.9 %collective-permute-start.26 = (bf16[1,2,128,512]{3,2,1,0:T(8,128)(2,1)S(1)}, bf16[1,2,128,512]{3,2,1,0:T(8,128)(2,1)S(1)}, u32[]{:S(2)}, u32[]{:S(2)}) collective-permute-start(bf16[1,2,128,512]{3,2,1,0:T(8,128)(2,1)S(1)} %get-tuple-element.31), channel_id=1, source_target_pairs={{0,32},{4,36},{8,40},{12,44},{16,48},{20,52},{24,56},{28,60},{32,6... | collective-permute-start | bytes 786440 | tf_op jit(solution)/shard_map/ppermute | solution.py:27
  20.0 19.0 %collective-permute-start.10 = (bf16[2,2,128,512]{3,2,1,0:T(8,128)(2,1)S(1)}, bf16[2,2,128,512]{3,2,1,0:T(8,128)(2,1)S(1)}, u32[]{:S(2)}, u32[]{:S(2)}) collective-permute-start(bf16[2,2,128,512]{3,2,1,0:T(8,128)(2,1)S(1)} %constant_dynamic-update-slice_fusion.refs_1_), channel_id=1, source_target_pairs={{0,4},{4,0},{8,12},{12,8},{16,20},{20,16},{24,28},{28,24},{32,36},... | collective-permute-start | bytes 1572872 | tf_op jit(solution)/shard_map/ppermute | solution.py:18
  38.9 16.1 %collective-permute-start.31 = (bf16[2,2,128,512]{3,2,1,0:T(8,128)(2,1)S(1)}, bf16[2,2,128,512]{3,2,1,0:T(8,128)(2,1)S(1)}, u32[]{:S(2)}, u32[]{:S(2)}) collective-permute-start(bf16[2,2,128,512]{3,2,1,0:T(8,128)(2,1)S(1)} %pad_maximum_fusion.1.refs_0_), channel_id=1, source_target_pairs={{0,24},{4,28},{8,0},{12,4},{16,8},{20,12},{24,16},{28,20},{32,56},... | collective-permute-start | bytes 1572872 | tf_op jit(solution)/shard_map/ppermute | solution.py:27
  39.0 16.0 %collective-permute-start.29 = (bf16[2,2,128,512]{3,2,1,0:T(8,128)(2,1)S(1)}, bf16[2,2,128,512]{3,2,1,0:T(8,128)(2,1)S(1)}, u32[]{:S(2)}, u32[]{:S(2)}) collective-permute-start(bf16[2,2,128,512]{3,2,1,0:T(8,128)(2,1)S(1)} %pad_maximum_fusion.1.refs_0_), channel_id=1, source_target_pairs={{0,8},{4,12},{8,16},{12,20},{16,24},{20,28},{24,0},{28,4},{32,40},... | collective-permute-start | bytes 1572872 | tf_op jit(solution)/shard_map/ppermute | solution.py:27
  47.9 17.8 %collective-permute-start.32 = (bf16[2,2,128,512]{3,2,1,0:T(8,128)(2,1)S(1)}, bf16[2,2,128,512]{3,2,1,0:T(8,128)(2,1)S(1)}, u32[]{:S(2)}, u32[]{:S(2)}) collective-permute-start(bf16[2,2,128,512]{3,2,1,0:T(8,128)(2,1)S(1)} %constant_dynamic-update-slice_fusion.2.refs_1_), channel_id=1, source_target_pairs={{0,24},{4,28},{8,0},{12,4},{16,8},{20,12},{24,16},{28,20},{32,56},... | collective-permute-start | bytes 1572872 | tf_op jit(solution)/shard_map/ppermute | solution.py:27
  47.9 17.9 %collective-permute-start.30 = (bf16[2,2,128,512]{3,2,1,0:T(8,128)(2,1)S(1)}, bf16[2,2,128,512]{3,2,1,0:T(8,128)(2,1)S(1)}, u32[]{:S(2)}, u32[]{:S(2)}) collective-permute-start(bf16[2,2,128,512]{3,2,1,0:T(8,128)(2,1)S(1)} %constant_dynamic-update-slice_fusion.2.refs_1_), channel_id=1, source_target_pairs={{0,8},{4,12},{8,16},{12,20},{16,24},{20,28},{24,0},{28,4},{32,40},... | collective-permute-start | bytes 1572872 | tf_op jit(solution)/shard_map/ppermute | solution.py:27
  55.0 43.2 %collective-permute-start.18 = (bf16[1,1,14,2,128,256]{5,4,3,2,1,0:T(8,128)(2,1)}, bf16[1,1,14,2,128,256]{5,4,3,2,1,0:T(8,128)(2,1)S(1)}, u32[]{:S(2)}, u32[]{:S(2)}) collective-permute-start(bf16[1,1,14,2,128,256]{5,4,3,2,1,0:T(8,128)(2,1)} %refs_0_.11), channel_id=1, source_target_pairs={{0,1},{1,0},{2,3},{3,2},{4,5},{5,4},{6,7},{7,6},{8,9},{9,8},{10,11... | collective-permute-start | bytes 5505032 | tf_op jit(solution)/shard_map/ppermute | solution.py:18
  82.9 15.2 %collective-permute-start.34 = (bf16[2,2,128,512]{3,2,1,0:T(8,128)(2,1)S(1)}, bf16[2,2,128,512]{3,2,1,0:T(8,128)(2,1)S(1)}, u32[]{:S(2)}, u32[]{:S(2)}) collective-permute-start(bf16[2,2,128,512]{3,2,1,0:T(8,128)(2,1)S(1)} %collective-permute-done.32.refs_5_), channel_id=1, source_target_pairs={{0,24},{4,28},{8,0},{12,4},{16,8},{20,12},{24,16},{28,20},{32,56},... | collective-permute-start | bytes 1572872 | tf_op jit(solution)/shard_map/ppermute | solution.py:27
  88.0 19.6 %collective-permute-start.17 = (bf16[7,2,128,128]{3,2,1,0:T(8,128)(2,1)S(1)}, bf16[7,2,128,128]{3,2,1,0:T(8,128)(2,1)S(1)}, u32[]{:S(2)}, u32[]{:S(2)}) collective-permute-start(bf16[7,2,128,128]{3,2,1,0:T(8,128)(2,1)S(1)} %shard_map.91.own), channel_id=1, source_target_pairs={{0,1},{1,0},{2,3},{3,2},{4,5},{5,4},{6,7},{7,6},{8,9},{9,8},{10,11... | collective-permute-start | bytes 1376264 | tf_op jit(solution)/shard_map/ppermute | solution.py:18
  90.2 34.6 %collective-permute-start.40 = (bf16[2,2,128,512]{3,2,1,0:T(8,128)(2,1)S(1)}, bf16[2,2,128,512]{3,2,1,0:T(8,128)(2,1)S(1)}, u32[]{:S(2)}, u32[]{:S(2)}) collective-permute-start(bf16[2,2,128,512]{3,2,1,0:T(8,128)(2,1)S(1)} %collective-permute-done.32.refs_5_), channel_id=1, source_target_pairs={{0,4},{4,0},{8,12},{12,8},{16,20},{20,16},{24,28},{28,24},{32,36},... | collective-permute-start | bytes 1572872 | tf_op jit(solution)/shard_map/ppermute | solution.py:18
  96.1 28.7 %collective-permute-start.38 = (bf16[2,2,128,512]{3,2,1,0:T(8,128)(2,1)S(1)}, bf16[2,2,128,512]{3,2,1,0:T(8,128)(2,1)S(1)}, u32[]{:S(2)}, u32[]{:S(2)}) collective-permute-start(bf16[2,2,128,512]{3,2,1,0:T(8,128)(2,1)S(1)} %collective-permute-done.30.refs_3_), channel_id=1, source_target_pairs={{0,4},{4,0},{8,12},{12,8},{16,20},{20,16},{24,28},{28,24},{32,36},... | collective-permute-start | bytes 1572872 | tf_op jit(solution)/shard_map/ppermute | solution.py:18
  98.1 26.8 %collective-permute-start.41 = (bf16[2,2,128,512]{3,2,1,0:T(8,128)(2,1)S(1)}, bf16[2,2,128,512]{3,2,1,0:T(8,128)(2,1)S(1)}, u32[]{:S(2)}, u32[]{:S(2)}) collective-permute-start(bf16[2,2,128,512]{3,2,1,0:T(8,128)(2,1)S(1)} %collective-permute-done.33.refs_6_), channel_id=1, source_target_pairs={{0,4},{4,0},{8,12},{12,8},{16,20},{20,16},{24,28},{28,24},{32,36},... | collective-permute-start | bytes 1572872 | tf_op jit(solution)/shard_map/ppermute | solution.py:18
  98.1 26.8 %collective-permute-start.42 = (bf16[2,2,128,512]{3,2,1,0:T(8,128)(2,1)S(1)}, bf16[2,2,128,512]{3,2,1,0:T(8,128)(2,1)S(1)}, u32[]{:S(2)}, u32[]{:S(2)}) collective-permute-start(bf16[2,2,128,512]{3,2,1,0:T(8,128)(2,1)S(1)} %collective-permute-done.34.refs_7_), channel_id=1, source_target_pairs={{0,4},{4,0},{8,12},{12,8},{16,20},{20,16},{24,28},{28,24},{32,36},... | collective-permute-start | bytes 1572872 | tf_op jit(solution)/shard_map/ppermute | solution.py:18
  124.8 18.1 %collective-permute-start.21 = (bf16[7,2,128,128]{3,2,1,0:T(8,128)(2,1)S(1)}, bf16[7,2,128,128]{3,2,1,0:T(8,128)(2,1)S(1)}, u32[]{:S(2)}, u32[]{:S(2)}) collective-permute-start(bf16[7,2,128,128]{3,2,1,0:T(8,128)(2,1)S(1)} %get-tuple-element.20), channel_id=1, source_target_pairs={{0,3},{1,2},{2,1},{3,0},{4,7},{5,6},{6,5},{7,4},{8,11},{9,10},{10,... | collective-permute-start | bytes 1376264 | tf_op jit(solution)/shard_map/ppermute | solution.py:18
  128.8 18.1 %collective-permute-start.43 = (bf16[7,2,128,128]{3,2,1,0:T(8,128)(2,1)S(1)}, bf16[7,2,128,128]{3,2,1,0:T(8,128)(2,1)S(1)}, u32[]{:S(2)}, u32[]{:S(2)}) collective-permute-start(bf16[7,2,128,128]{3,2,1,0:T(8,128)(2,1)S(1)} %shard_map.100.own), channel_id=1, source_target_pairs={{0,1},{1,0},{2,3},{3,2},{4,5},{5,4},{6,7},{7,6},{8,9},{9,8},{10,11... | collective-permute-start | bytes 1376264 | tf_op jit(solution)/shard_map/ppermute | solution.py:18
  132.7 19.0 %collective-permute-start.45 = (bf16[7,2,128,128]{3,2,1,0:T(8,128)(2,1)S(1)}, bf16[7,2,128,128]{3,2,1,0:T(8,128)(2,1)S(1)}, u32[]{:S(2)}, u32[]{:S(2)}) collective-permute-start(bf16[7,2,128,128]{3,2,1,0:T(8,128)(2,1)S(1)} %shard_map.103.own), channel_id=1, source_target_pairs={{0,1},{1,0},{2,3},{3,2},{4,5},{5,4},{6,7},{7,6},{8,9},{9,8},{10,11... | collective-permute-start | bytes 1376264 | tf_op jit(solution)/shard_map/ppermute | solution.py:18
  146.7 35.0 %collective-permute-start.22 = (bf16[2,2,128,512]{3,2,1,0:T(8,128)(2,1)S(1)}, bf16[2,2,128,512]{3,2,1,0:T(8,128)(2,1)S(1)}, u32[]{:S(2)}, u32[]{:S(2)}) collective-permute-start(bf16[2,2,128,512]{3,2,1,0:T(8,128)(2,1)S(1)} %get-tuple-element.22), channel_id=1, source_target_pairs={{0,1},{1,0},{2,3},{3,2},{4,5},{5,4},{6,7},{7,6},{8,9},{9,8},{10,11... | collective-permute-start | bytes 1572872 | tf_op jit(solution)/shard_map/ppermute | solution.py:18
  148.1 16.8 %collective-permute-start.44 = (bf16[7,2,128,128]{3,2,1,0:T(8,128)(2,1)S(1)}, bf16[7,2,128,128]{3,2,1,0:T(8,128)(2,1)S(1)}, u32[]{:S(2)}, u32[]{:S(2)}) collective-permute-start(bf16[7,2,128,128]{3,2,1,0:T(8,128)(2,1)S(1)} %get-tuple-element.24), channel_id=1, source_target_pairs={{0,3},{1,2},{2,1},{3,0},{4,7},{5,6},{6,5},{7,4},{8,11},{9,10},{10,... | collective-permute-start | bytes 1376264 | tf_op jit(solution)/shard_map/ppermute | solution.py:18
  152.8 21.6 %collective-permute-start.46 = (bf16[7,2,128,128]{3,2,1,0:T(8,128)(2,1)S(1)}, bf16[7,2,128,128]{3,2,1,0:T(8,128)(2,1)S(1)}, u32[]{:S(2)}, u32[]{:S(2)}) collective-permute-start(bf16[7,2,128,128]{3,2,1,0:T(8,128)(2,1)S(1)} %get-tuple-element.26), channel_id=1, source_target_pairs={{0,3},{1,2},{2,1},{3,0},{4,7},{5,6},{6,5},{7,4},{8,11},{9,10},{10,... | collective-permute-start | bytes 1376264 | tf_op jit(solution)/shard_map/ppermute | solution.py:18
  156.1 29.5 %collective-permute-start.24 = (bf16[2,256,256]{2,1,0:T(8,128)(2,1)S(1)}, bf16[2,256,256]{2,1,0:T(8,128)(2,1)S(1)}, u32[]{:S(2)}, u32[]{:S(2)}) collective-permute-start(bf16[2,256,256]{2,1,0:T(8,128)(2,1)S(1)} %get-tuple-element.33), channel_id=1, source_target_pairs={{1,0},{2,1},{3,2},{4,3},{5,4},{6,5},{7,6},{8,7},{9,8},{10,9},{11,1... | collective-permute-start | bytes 786440 | tf_op jit(solution)/shard_map/ppermute | solution.py:296
  158.1 27.6 %collective-permute-start.23 = (bf16[2,256,256]{2,1,0:T(8,128)(2,1)S(1)}, bf16[2,256,256]{2,1,0:T(8,128)(2,1)S(1)}, u32[]{:S(2)}, u32[]{:S(2)}) collective-permute-start(bf16[2,256,256]{2,1,0:T(8,128)(2,1)S(1)} %get-tuple-element.34), channel_id=1, source_target_pairs={{0,1},{1,2},{2,3},{3,4},{4,5},{5,6},{6,7},{7,8},{8,9},{9,10},{10,1... | collective-permute-start | bytes 786440 | tf_op jit(solution)/shard_map/ppermute | solution.py:295
  (38 other events, 620.5 us)

commit v3 on v2

--- a/solution.py
+++ b/solution.py
@@ -96,7 +96,7 @@
 
 def level0_body(color, base, count, src, rank, *refs):
     bufs, w, out = refs[:16], refs[16], refs[17]
-    xs, sems = refs[18:]
+    xs = refs[18]
     me = lax.axis_index("grp")
     k = w.shape[-2]
     n = xs.shape[2]
@@ -113,13 +113,12 @@
 
             @pl.when(which == t)
             def _():
-                pltpu.make_async_copy(bufs[t].at[first & 1], xs.at[i], sems.at[i]).start()
+                xs[i] = bufs[t][first & 1]
 
         return carry
 
     lax.fori_loop(0, count, fetch, 0)
     for i in range(count):
-        pltpu.make_async_copy(bufs[0].at[0], xs.at[i], sems.at[i]).wait()
         p = nt(xs[i].reshape(2 * n, xs.shape[3]), w[0, 0, base + i].reshape(2 * k, w.shape[-1]))
         live = lax.broadcasted_iota(jnp.int32, (n, k), 1) < rank[0, base + i]
         out[i, 0], out[i, 1] = combine(p, n, k, live)
@@ -132,11 +131,7 @@
         functools.partial(level0_body, color, base, count),
         [src, rank], [*bufs, w],
         jax.ShapeDtypeStruct((count, 2, n, k), BF16),
-        [
-            pltpu.VMEM((count, 2, n, rows), BF16),
-            pltpu.SemaphoreType.DMA((count,)),
-        ],
-        space=[pl.ANY] * 16 + [pltpu.VMEM],
+        [pltpu.VMEM((count, 2, n, rows), BF16)],
         room=count * 2 * rows * n * 2,
     )
 

time: 202 us -> 202 us (level)
  waiting for transfers between devices: 101 us -> 110 us
  Pallas kernels: 39.2 us -> 32.8 us
  starting transfers between devices: 58.9 us -> 56 us
    ppermute x30, waiting for transfers between devices: 42 us -> 49.4 us  [swap(): lax.ppermute(value, axis, [(i, i ^ mask) for i in range(lax.axis_size(axi...]
    pallas_call x19, Pallas kernels: 39.2 us -> 32.8 us  [call(): pl.pallas_call(body, in_specs=[SMEM] * len(scalars) + [pl.BlockSpec(memor...]
    ppermute x30, starting transfers between devices: 26.6 us -> 23.9 us  [swap(): lax.ppermute(value, axis, [(i, i ^ mask) for i in range(lax.axis_size(axi...]
  transfers between devices with their start and end apart: 50 -> 50, of which waited for: 21 -> 20; matrix products, arithmetic and copies ran while one was open for 0% -> 0% of each run, Pallas kernels for 19% -> 16%
where the time goes in v3:
time: 202 us; the launch traced here: 201 us
  waiting for transfers between devices  110 us (54%)
  starting transfers between devices  56 us (28%)
  Pallas kernels  32.8 us (16%)
    ppermute x18, waiting for transfers between devices, ring(): return lax.ppermute(value, 'grp', perm)  60.8 us
    ppermute x30, waiting for transfers between devices, swap(): lax.ppermute(value, axis, [(i, i ^ mask) for i in range(lax.axis_size(axi...  49.4 us
    pallas_call x19, Pallas kernels, call(): pl.pallas_call(body, in_specs=[SMEM] * len(scalars) + [pl.BlockSpec(memor...  32.8 us
    ppermute x18, starting transfers between devices, ring(): return lax.ppermute(value, 'grp', perm)  26.3 us
    ppermute x30, starting transfers between devices, swap(): lax.ppermute(value, axis, [(i, i ^ mask) for i in range(lax.axis_size(axi...  23.9 us
  transfers between devices with their start and end apart: 50, of which 20 were waited for; matrix products, arithmetic and copies ran while one was open for 0% of the time, Pallas kernels for 16%

profile of v3, /device:TPU:6, one launch (start us, length us, event | category | flops | bytes accessed | tf_op | source)
XLA Modules:
  0.0 201.4 jit_solution(9977521514741724971)
XLA Ops:
  1.5 3.3 %collective-permute-start.28 = (bf16[1,2,128,512]{3,2,1,0:T(8,128)(2,1)S(1)}, bf16[1,2,128,512]{3,2,1,0:T(8,128)(2,1)S(1)}, u32[]{:S(2)}, u32[]{:S(2)}) collective-permute-start(bf16[1,2,128,512]{3,2,1,0:T(8,128)(2,1)S(1)} %get-tuple-element.31), channel_id=1, source_target_pairs={{0,64},{4,68},{8,72},{12,76},{16,80},{20,84},{24,88},{28,92},{32,9... | collective-permute-start | bytes 786440 | tf_op jit(solution)/shard_map/ppermute | solution.py:27
  10.8 4.5 %collective-permute-start.5 = (bf16[2,2,128,512]{3,2,1,0:T(8,128)(2,1)S(1)}, bf16[2,2,128,512]{3,2,1,0:T(8,128)(2,1)S(1)}, u32[]{:S(2)}, u32[]{:S(2)}) collective-permute-start(bf16[2,2,128,512]{3,2,1,0:T(8,128)(2,1)S(1)} %pad_maximum_fusion.refs_0_), channel_id=1, source_target_pairs={{0,96},{4,100},{8,104},{12,108},{16,112},{20,116},{24,120},{28,124... | collective-permute-start | bytes 1572872 | tf_op jit(solution)/shard_map/ppermute | solution.py:27
  15.3 3.8 %collective-permute-done.1 = bf16[1,2,128,512]{3,2,1,0:T(8,128)(2,1)S(1)} collective-permute-done((bf16[1,2,128,512]{3,2,1,0:T(8,128)(2,1)S(1)}, bf16[1,2,128,512]{3,2,1,0:T(8,128)(2,1)S(1)}, u32[]{:S(2)}, u32[]{:S(2)}) %collective-permute-start.1) | collective-permute-done | bytes 262176 | tf_op jit(solution)/shard_map/ppermute | solution.py:27
  20.0 16.6 %collective-permute-done.26 = bf16[1,2,128,512]{3,2,1,0:T(8,128)(2,1)S(1)} collective-permute-done((bf16[1,2,128,512]{3,2,1,0:T(8,128)(2,1)S(1)}, bf16[1,2,128,512]{3,2,1,0:T(8,128)(2,1)S(1)}, u32[]{:S(2)}, u32[]{:S(2)}) %collective-permute-start.26) | collective-permute-done | bytes 262176 | tf_op jit(solution)/shard_map/ppermute | solution.py:27
  39.0 3.2 %collective-permute-start.29 = (bf16[2,2,128,512]{3,2,1,0:T(8,128)(2,1)S(1)}, bf16[2,2,128,512]{3,2,1,0:T(8,128)(2,1)S(1)}, u32[]{:S(2)}, u32[]{:S(2)}) collective-permute-start(bf16[2,2,128,512]{3,2,1,0:T(8,128)(2,1)S(1)} %pad_maximum_fusion.1.refs_0_), channel_id=1, source_target_pairs={{0,8},{4,12},{8,16},{12,20},{16,24},{20,28},{24,0},{28,4},{32,40},... | collective-permute-start | bytes 1572872 | tf_op jit(solution)/shard_map/ppermute | solution.py:27
  42.2 3.7 %collective-permute-done.6.refs_5_ = bf16[2,2,128,512]{3,2,1,0:T(8,128)(2,1)S(1)} collective-permute-done((bf16[2,2,128,512]{3,2,1,0:T(8,128)(2,1)S(1)}, bf16[2,2,128,512]{3,2,1,0:T(8,128)(2,1)S(1)}, u32[]{:S(2)}, u32[]{:S(2)}) %collective-permute-start.6) | collective-permute-done | bytes 524320 | tf_op jit(solution)/shard_map/ppermute | solution.py:27
  47.9 3.2 %collective-permute-start.30 = (bf16[2,2,128,512]{3,2,1,0:T(8,128)(2,1)S(1)}, bf16[2,2,128,512]{3,2,1,0:T(8,128)(2,1)S(1)}, u32[]{:S(2)}, u32[]{:S(2)}) collective-permute-start(bf16[2,2,128,512]{3,2,1,0:T(8,128)(2,1)S(1)} %constant_dynamic-update-slice_fusion.2.refs_1_), channel_id=1, source_target_pairs={{0,8},{4,12},{8,16},{12,20},{16,24},{20,28},{24,0},{28,4},{32,40},... | collective-permute-start | bytes 1572872 | tf_op jit(solution)/shard_map/ppermute | solution.py:27
  51.1 3.8 %collective-permute-done.31.refs_4_ = bf16[2,2,128,512]{3,2,1,0:T(8,128)(2,1)S(1)} collective-permute-done((bf16[2,2,128,512]{3,2,1,0:T(8,128)(2,1)S(1)}, bf16[2,2,128,512]{3,2,1,0:T(8,128)(2,1)S(1)}, u32[]{:S(2)}, u32[]{:S(2)}) %collective-permute-start.31) | collective-permute-done | bytes 524320 | tf_op jit(solution)/shard_map/ppermute | solution.py:27
  57.1 8.5 %collective-permute-done.32.refs_5_ = bf16[2,2,128,512]{3,2,1,0:T(8,128)(2,1)S(1)} collective-permute-done((bf16[2,2,128,512]{3,2,1,0:T(8,128)(2,1)S(1)}, bf16[2,2,128,512]{3,2,1,0:T(8,128)(2,1)S(1)}, u32[]{:S(2)}, u32[]{:S(2)}) %collective-permute-start.32) | collective-permute-done | bytes 524320 | tf_op jit(solution)/shard_map/ppermute | solution.py:27
  65.8 3.1 %collective-permute-start.8 = (bf16[2,2,128,512]{3,2,1,0:T(8,128)(2,1)S(1)}, bf16[2,2,128,512]{3,2,1,0:T(8,128)(2,1)S(1)}, u32[]{:S(2)}, u32[]{:S(2)}) collective-permute-start(bf16[2,2,128,512]{3,2,1,0:T(8,128)(2,1)S(1)} %collective-permute-done.6.refs_5_), channel_id=1, source_target_pairs={{0,96},{4,100},{8,104},{12,108},{16,112},{20,116},{24,120},{28,124... | collective-permute-start | bytes 1572872 | tf_op jit(solution)/shard_map/ppermute | solution.py:27
  69.4 10.9 %collective-permute-done.7.refs_6_ = bf16[2,2,128,512]{3,2,1,0:T(8,128)(2,1)S(1)} collective-permute-done((bf16[2,2,128,512]{3,2,1,0:T(8,128)(2,1)S(1)}, bf16[2,2,128,512]{3,2,1,0:T(8,128)(2,1)S(1)}, u32[]{:S(2)}, u32[]{:S(2)}) %collective-permute-start.7) | collective-permute-done | bytes 524320 | tf_op jit(solution)/shard_map/ppermute | solution.py:27
  88.5 7.7 %collective-permute-done.33.refs_6_ = bf16[2,2,128,512]{3,2,1,0:T(8,128)(2,1)S(1)} collective-permute-done((bf16[2,2,128,512]{3,2,1,0:T(8,128)(2,1)S(1)}, bf16[2,2,128,512]{3,2,1,0:T(8,128)(2,1)S(1)}, u32[]{:S(2)}, u32[]{:S(2)}) %collective-permute-start.33) | collective-permute-done | bytes 524320 | tf_op jit(solution)/shard_map/ppermute | solution.py:27
  100.9 6.7 %collective-permute-done.17.other = bf16[7,2,128,128]{3,2,1,0:T(8,128)(2,1)S(1)} collective-permute-done((bf16[7,2,128,128]{3,2,1,0:T(8,128)(2,1)S(1)}, bf16[7,2,128,128]{3,2,1,0:T(8,128)(2,1)S(1)}, u32[]{:S(2)}, u32[]{:S(2)}) %collective-permute-start.17) | collective-permute-done | bytes 458784 | tf_op jit(solution)/shard_map/ppermute | solution.py:18
  110.6 9.3 %collective-permute-done.20.other = bf16[7,2,128,128]{3,2,1,0:T(8,128)(2,1)S(1)} collective-permute-done((bf16[7,2,128,128]{3,2,1,0:T(8,128)(2,1)S(1)}, bf16[7,2,128,128]{3,2,1,0:T(8,128)(2,1)S(1)}, u32[]{:S(2)}, u32[]{:S(2)}) %collective-permute-start.20) | collective-permute-done | bytes 458784 | tf_op jit(solution)/shard_map/ppermute | solution.py:18
  119.8 3.7 %collective-permute-start.19 = (bf16[7,2,128,128]{3,2,1,0:T(8,128)(2,1)S(1)}, bf16[7,2,128,128]{3,2,1,0:T(8,128)(2,1)S(1)}, u32[]{:S(2)}, u32[]{:S(2)}) collective-permute-start(bf16[7,2,128,128]{3,2,1,0:T(8,128)(2,1)S(1)} %get-tuple-element.18), channel_id=1, source_target_pairs={{0,3},{1,2},{2,1},{3,0},{4,7},{5,6},{6,5},{7,4},{8,11},{9,10},{10,... | collective-permute-start | bytes 1376264 | tf_op jit(solution)/shard_map/ppermute | solution.py:18
  131.6 3.3 %collective-permute-done.19.other = bf16[7,2,128,128]{3,2,1,0:T(8,128)(2,1)S(1)} collective-permute-done((bf16[7,2,128,128]{3,2,1,0:T(8,128)(2,1)S(1)}, bf16[7,2,128,128]{3,2,1,0:T(8,128)(2,1)S(1)}, u32[]{:S(2)}, u32[]{:S(2)}) %collective-permute-start.19) | collective-permute-done | bytes 458784 | tf_op jit(solution)/shard_map/ppermute | solution.py:18
  135.9 6.9 %collective-permute-done.21.other = bf16[7,2,128,128]{3,2,1,0:T(8,128)(2,1)S(1)} collective-permute-done((bf16[7,2,128,128]{3,2,1,0:T(8,128)(2,1)S(1)}, bf16[7,2,128,128]{3,2,1,0:T(8,128)(2,1)S(1)}, u32[]{:S(2)}, u32[]{:S(2)}) %collective-permute-start.21) | collective-permute-done | bytes 458784 | tf_op jit(solution)/shard_map/ppermute | solution.py:18
  142.9 3.8 %shard_map.96 = (bf16[14,256,256]{2,1,0:T(8,128)(2,1)S(1)}, bf16[2,2,128,512]{3,2,1,0:T(8,128)(2,1)S(1)}) custom-call(s32[1,14]{1,0:T(1,128)S(1)} %copy-done.6, bf16[7,2,128,128]{3,2,1,0:T(8,128)(2,1)S(1)} %shard_map.93.ready, bf16[7,2,128,128]{3,2,1,0:T(8,128)(2,1)S(1)} %get-tuple-element.19.own, ...), custom_call_target="tpu_custom_call" | custom-call | tf_op jit(solution)/shard_map/pallas_call | solution.py:46
  155.0 3.9 %collective-permute-start.23 = (bf16[2,256,256]{2,1,0:T(8,128)(2,1)S(1)}, bf16[2,256,256]{2,1,0:T(8,128)(2,1)S(1)}, u32[]{:S(2)}, u32[]{:S(2)}) collective-permute-start(bf16[2,256,256]{2,1,0:T(8,128)(2,1)S(1)} %get-tuple-element.34), channel_id=1, source_target_pairs={{0,1},{1,2},{2,3},{3,4},{4,5},{5,6},{6,7},{7,8},{8,9},{9,10},{10,1... | collective-permute-start | bytes 786440 | tf_op jit(solution)/shard_map/ppermute | solution.py:290
  159.0 6.6 %collective-permute-done.44.other = bf16[7,2,128,128]{3,2,1,0:T(8,128)(2,1)S(1)} collective-permute-done((bf16[7,2,128,128]{3,2,1,0:T(8,128)(2,1)S(1)}, bf16[7,2,128,128]{3,2,1,0:T(8,128)(2,1)S(1)}, u32[]{:S(2)}, u32[]{:S(2)}) %collective-permute-start.44) | collective-permute-done | bytes 458784 | tf_op jit(solution)/shard_map/ppermute | solution.py:18
  166.5 7.9 %collective-permute-done.46.other = bf16[7,2,128,128]{3,2,1,0:T(8,128)(2,1)S(1)} collective-permute-done((bf16[7,2,128,128]{3,2,1,0:T(8,128)(2,1)S(1)}, bf16[7,2,128,128]{3,2,1,0:T(8,128)(2,1)S(1)}, u32[]{:S(2)}, u32[]{:S(2)}) %collective-permute-start.46) | collective-permute-done | bytes 458784 | tf_op jit(solution)/shard_map/ppermute | solution.py:18
  181.7 3.8 %collective-permute-start.25 = (bf16[2,128,512]{2,1,0:T(8,128)(2,1)S(1)}, bf16[2,128,512]{2,1,0:T(8,128)(2,1)S(1)}, u32[]{:S(2)}, u32[]{:S(2)}) collective-permute-start(bf16[2,128,512]{2,1,0:T(8,128)(2,1)S(1)} %fusion.2), channel_id=1, source_target_pairs={{0,3},{1,2},{2,1},{3,0},{4,7},{5,6},{6,5},{7,4},{8,11},{9,10},{10,... | collective-permute-start | bytes 786440 | tf_op jit(solution)/shard_map/ppermute | solution.py:18
  185.5 3.2 %shard_map.98 = f32[2,256,512]{2,1,0:T(8,128)S(1)} custom-call(s32[2,3]{1,0:T(2,128)S(1)} %copy-done.7, bf16[2,256,512]{2,1,0:T(8,128)(2,1)S(1)} %copy-done.3, bf16[2,256,256]{2,1,0:T(8,128)(2,1)S(1)} %collective-permute-done.23.low, bf16[2,256,256]{2,1,0:T(8,128)(2,1)S(1)} %collective-permute-done.24.high, bf16[2,3,2,256,256]{4,3,2,1,0:T(8,128)(2,1)S(1)} %copy-done.4), custom_call_target="tpu_custom_call" | custom-call | tf_op jit(solution)/shard_map/pallas_call | solution.py:46
  193.3 7.2 %collective-permute-done.49.last = bf16[2,128,512]{2,1,0:T(8,128)(2,1)S(1)} collective-permute-done((bf16[2,128,512]{2,1,0:T(8,128)(2,1)S(1)}, bf16[2,128,512]{2,1,0:T(8,128)(2,1)S(1)}, u32[]{:S(2)}, u32[]{:S(2)}) %collective-permute-start.49) | collective-permute-done | bytes 262176 | tf_op jit(solution)/shard_map/ppermute | solution.py:18
  (131 shorter events, 62.3 us)
Async XLA Ops:
  10.0 27.5 %collective-permute-start.9 = (bf16[2,2,128,512]{3,2,1,0:T(8,128)(2,1)S(1)}, bf16[2,2,128,512]{3,2,1,0:T(8,128)(2,1)S(1)}, u32[]{:S(2)}, u32[]{:S(2)}) collective-permute-start(bf16[2,2,128,512]{3,2,1,0:T(8,128)(2,1)S(1)} %pad_maximum_fusion.refs_0_), channel_id=1, source_target_pairs={{0,4},{4,0},{8,12},{12,8},{16,20},{20,16},{24,28},{28,24},{32,36},... | collective-permute-start | bytes 1572872 | tf_op jit(solution)/shard_map/ppermute | solution.py:18
  10.8 28.0 %collective-permute-start.5 = (bf16[2,2,128,512]{3,2,1,0:T(8,128)(2,1)S(1)}, bf16[2,2,128,512]{3,2,1,0:T(8,128)(2,1)S(1)}, u32[]{:S(2)}, u32[]{:S(2)}) collective-permute-start(bf16[2,2,128,512]{3,2,1,0:T(8,128)(2,1)S(1)} %pad_maximum_fusion.refs_0_), channel_id=1, source_target_pairs={{0,96},{4,100},{8,104},{12,108},{16,112},{20,116},{24,120},{28,124... | collective-permute-start | bytes 1572872 | tf_op jit(solution)/shard_map/ppermute | solution.py:27
  19.1 19.7 %collective-permute-start.3 = (bf16[2,2,128,512]{3,2,1,0:T(8,128)(2,1)S(1)}, bf16[2,2,128,512]{3,2,1,0:T(8,128)(2,1)S(1)}, u32[]{:S(2)}, u32[]{:S(2)}) collective-permute-start(bf16[2,2,128,512]{3,2,1,0:T(8,128)(2,1)S(1)} %pad_maximum_fusion.refs_0_), channel_id=1, source_target_pairs={{0,32},{4,36},{8,40},{12,44},{16,48},{20,52},{24,56},{28,60},{32,6... | collective-permute-start | bytes 1572872 | tf_op jit(solution)/shard_map/ppermute | solution.py:27
  19.8 16.9 %collective-permute-start.26 = (bf16[1,2,128,512]{3,2,1,0:T(8,128)(2,1)S(1)}, bf16[1,2,128,512]{3,2,1,0:T(8,128)(2,1)S(1)}, u32[]{:S(2)}, u32[]{:S(2)}) collective-permute-start(bf16[1,2,128,512]{3,2,1,0:T(8,128)(2,1)S(1)} %get-tuple-element.31), channel_id=1, source_target_pairs={{0,32},{4,36},{8,40},{12,44},{16,48},{20,52},{24,56},{28,60},{32,6... | collective-permute-start | bytes 786440 | tf_op jit(solution)/shard_map/ppermute | solution.py:27
  20.0 19.0 %collective-permute-start.10 = (bf16[2,2,128,512]{3,2,1,0:T(8,128)(2,1)S(1)}, bf16[2,2,128,512]{3,2,1,0:T(8,128)(2,1)S(1)}, u32[]{:S(2)}, u32[]{:S(2)}) collective-permute-start(bf16[2,2,128,512]{3,2,1,0:T(8,128)(2,1)S(1)} %constant_dynamic-update-slice_fusion.refs_1_), channel_id=1, source_target_pairs={{0,4},{4,0},{8,12},{12,8},{16,20},{20,16},{24,28},{28,24},{32,36},... | collective-permute-start | bytes 1572872 | tf_op jit(solution)/shard_map/ppermute | solution.py:18
  38.9 16.1 %collective-permute-start.31 = (bf16[2,2,128,512]{3,2,1,0:T(8,128)(2,1)S(1)}, bf16[2,2,128,512]{3,2,1,0:T(8,128)(2,1)S(1)}, u32[]{:S(2)}, u32[]{:S(2)}) collective-permute-start(bf16[2,2,128,512]{3,2,1,0:T(8,128)(2,1)S(1)} %pad_maximum_fusion.1.refs_0_), channel_id=1, source_target_pairs={{0,24},{4,28},{8,0},{12,4},{16,8},{20,12},{24,16},{28,20},{32,56},... | collective-permute-start | bytes 1572872 | tf_op jit(solution)/shard_map/ppermute | solution.py:27
  39.0 16.0 %collective-permute-start.29 = (bf16[2,2,128,512]{3,2,1,0:T(8,128)(2,1)S(1)}, bf16[2,2,128,512]{3,2,1,0:T(8,128)(2,1)S(1)}, u32[]{:S(2)}, u32[]{:S(2)}) collective-permute-start(bf16[2,2,128,512]{3,2,1,0:T(8,128)(2,1)S(1)} %pad_maximum_fusion.1.refs_0_), channel_id=1, source_target_pairs={{0,8},{4,12},{8,16},{12,20},{16,24},{20,28},{24,0},{28,4},{32,40},... | collective-permute-start | bytes 1572872 | tf_op jit(solution)/shard_map/ppermute | solution.py:27
  47.9 17.8 %collective-permute-start.32 = (bf16[2,2,128,512]{3,2,1,0:T(8,128)(2,1)S(1)}, bf16[2,2,128,512]{3,2,1,0:T(8,128)(2,1)S(1)}, u32[]{:S(2)}, u32[]{:S(2)}) collective-permute-start(bf16[2,2,128,512]{3,2,1,0:T(8,128)(2,1)S(1)} %constant_dynamic-update-slice_fusion.2.refs_1_), channel_id=1, source_target_pairs={{0,24},{4,28},{8,0},{12,4},{16,8},{20,12},{24,16},{28,20},{32,56},... | collective-permute-start | bytes 1572872 | tf_op jit(solution)/shard_map/ppermute | solution.py:27
  47.9 17.9 %collective-permute-start.30 = (bf16[2,2,128,512]{3,2,1,0:T(8,128)(2,1)S(1)}, bf16[2,2,128,512]{3,2,1,0:T(8,128)(2,1)S(1)}, u32[]{:S(2)}, u32[]{:S(2)}) collective-permute-start(bf16[2,2,128,512]{3,2,1,0:T(8,128)(2,1)S(1)} %constant_dynamic-update-slice_fusion.2.refs_1_), channel_id=1, source_target_pairs={{0,8},{4,12},{8,16},{12,20},{16,24},{20,28},{24,0},{28,4},{32,40},... | collective-permute-start | bytes 1572872 | tf_op jit(solution)/shard_map/ppermute | solution.py:27
  55.0 43.2 %collective-permute-start.18 = (bf16[1,1,14,2,128,256]{5,4,3,2,1,0:T(8,128)(2,1)}, bf16[1,1,14,2,128,256]{5,4,3,2,1,0:T(8,128)(2,1)S(1)}, u32[]{:S(2)}, u32[]{:S(2)}) collective-permute-start(bf16[1,1,14,2,128,256]{5,4,3,2,1,0:T(8,128)(2,1)} %refs_0_.11), channel_id=1, source_target_pairs={{0,1},{1,0},{2,3},{3,2},{4,5},{5,4},{6,7},{7,6},{8,9},{9,8},{10,11... | collective-permute-start | bytes 5505032 | tf_op jit(solution)/shard_map/ppermute | solution.py:18
  82.9 15.2 %collective-permute-start.34 = (bf16[2,2,128,512]{3,2,1,0:T(8,128)(2,1)S(1)}, bf16[2,2,128,512]{3,2,1,0:T(8,128)(2,1)S(1)}, u32[]{:S(2)}, u32[]{:S(2)}) collective-permute-start(bf16[2,2,128,512]{3,2,1,0:T(8,128)(2,1)S(1)} %collective-permute-done.32.refs_5_), channel_id=1, source_target_pairs={{0,24},{4,28},{8,0},{12,4},{16,8},{20,12},{24,16},{28,20},{32,56},... | collective-permute-start | bytes 1572872 | tf_op jit(solution)/shard_map/ppermute | solution.py:27
  86.5 21.1 %collective-permute-start.17 = (bf16[7,2,128,128]{3,2,1,0:T(8,128)(2,1)S(1)}, bf16[7,2,128,128]{3,2,1,0:T(8,128)(2,1)S(1)}, u32[]{:S(2)}, u32[]{:S(2)}) collective-permute-start(bf16[7,2,128,128]{3,2,1,0:T(8,128)(2,1)S(1)} %shard_map.91.own), channel_id=1, source_target_pairs={{0,1},{1,0},{2,3},{3,2},{4,5},{5,4},{6,7},{7,6},{8,9},{9,8},{10,11... | collective-permute-start | bytes 1376264 | tf_op jit(solution)/shard_map/ppermute | solution.py:18
  88.5 36.3 %collective-permute-start.40 = (bf16[2,2,128,512]{3,2,1,0:T(8,128)(2,1)S(1)}, bf16[2,2,128,512]{3,2,1,0:T(8,128)(2,1)S(1)}, u32[]{:S(2)}, u32[]{:S(2)}) collective-permute-start(bf16[2,2,128,512]{3,2,1,0:T(8,128)(2,1)S(1)} %collective-permute-done.32.refs_5_), channel_id=1, source_target_pairs={{0,4},{4,0},{8,12},{12,8},{16,20},{20,16},{24,28},{28,24},{32,36},... | collective-permute-start | bytes 1572872 | tf_op jit(solution)/shard_map/ppermute | solution.py:18
  96.1 28.7 %collective-permute-start.38 = (bf16[2,2,128,512]{3,2,1,0:T(8,128)(2,1)S(1)}, bf16[2,2,128,512]{3,2,1,0:T(8,128)(2,1)S(1)}, u32[]{:S(2)}, u32[]{:S(2)}) collective-permute-start(bf16[2,2,128,512]{3,2,1,0:T(8,128)(2,1)S(1)} %collective-permute-done.30.refs_3_), channel_id=1, source_target_pairs={{0,4},{4,0},{8,12},{12,8},{16,20},{20,16},{24,28},{28,24},{32,36},... | collective-permute-start | bytes 1572872 | tf_op jit(solution)/shard_map/ppermute | solution.py:18
  98.1 26.8 %collective-permute-start.41 = (bf16[2,2,128,512]{3,2,1,0:T(8,128)(2,1)S(1)}, bf16[2,2,128,512]{3,2,1,0:T(8,128)(2,1)S(1)}, u32[]{:S(2)}, u32[]{:S(2)}) collective-permute-start(bf16[2,2,128,512]{3,2,1,0:T(8,128)(2,1)S(1)} %collective-permute-done.33.refs_6_), channel_id=1, source_target_pairs={{0,4},{4,0},{8,12},{12,8},{16,20},{20,16},{24,28},{28,24},{32,36},... | collective-permute-start | bytes 1572872 | tf_op jit(solution)/shard_map/ppermute | solution.py:18
  98.1 26.8 %collective-permute-start.42 = (bf16[2,2,128,512]{3,2,1,0:T(8,128)(2,1)S(1)}, bf16[2,2,128,512]{3,2,1,0:T(8,128)(2,1)S(1)}, u32[]{:S(2)}, u32[]{:S(2)}) collective-permute-start(bf16[2,2,128,512]{3,2,1,0:T(8,128)(2,1)S(1)} %collective-permute-done.34.refs_7_), channel_id=1, source_target_pairs={{0,4},{4,0},{8,12},{12,8},{16,20},{20,16},{24,28},{28,24},{32,36},... | collective-permute-start | bytes 1572872 | tf_op jit(solution)/shard_map/ppermute | solution.py:18
  124.8 18.1 %collective-permute-start.21 = (bf16[7,2,128,128]{3,2,1,0:T(8,128)(2,1)S(1)}, bf16[7,2,128,128]{3,2,1,0:T(8,128)(2,1)S(1)}, u32[]{:S(2)}, u32[]{:S(2)}) collective-permute-start(bf16[7,2,128,128]{3,2,1,0:T(8,128)(2,1)S(1)} %get-tuple-element.20), channel_id=1, source_target_pairs={{0,3},{1,2},{2,1},{3,0},{4,7},{5,6},{6,5},{7,4},{8,11},{9,10},{10,... | collective-permute-start | bytes 1376264 | tf_op jit(solution)/shard_map/ppermute | solution.py:18
  127.2 19.6 %collective-permute-start.43 = (bf16[7,2,128,128]{3,2,1,0:T(8,128)(2,1)S(1)}, bf16[7,2,128,128]{3,2,1,0:T(8,128)(2,1)S(1)}, u32[]{:S(2)}, u32[]{:S(2)}) collective-permute-start(bf16[7,2,128,128]{3,2,1,0:T(8,128)(2,1)S(1)} %shard_map.100.own), channel_id=1, source_target_pairs={{0,1},{1,0},{2,3},{3,2},{4,5},{5,4},{6,7},{7,6},{8,9},{9,8},{10,11... | collective-permute-start | bytes 1376264 | tf_op jit(solution)/shard_map/ppermute | solution.py:18
  129.6 21.5 %collective-permute-start.45 = (bf16[7,2,128,128]{3,2,1,0:T(8,128)(2,1)S(1)}, bf16[7,2,128,128]{3,2,1,0:T(8,128)(2,1)S(1)}, u32[]{:S(2)}, u32[]{:S(2)}) collective-permute-start(bf16[7,2,128,128]{3,2,1,0:T(8,128)(2,1)S(1)} %shard_map.103.own), channel_id=1, source_target_pairs={{0,1},{1,0},{2,3},{3,2},{4,5},{5,4},{6,7},{7,6},{8,9},{9,8},{10,11... | collective-permute-start | bytes 1376264 | tf_op jit(solution)/shard_map/ppermute | solution.py:18
  146.7 35.0 %collective-permute-start.22 = (bf16[2,2,128,512]{3,2,1,0:T(8,128)(2,1)S(1)}, bf16[2,2,128,512]{3,2,1,0:T(8,128)(2,1)S(1)}, u32[]{:S(2)}, u32[]{:S(2)}) collective-permute-start(bf16[2,2,128,512]{3,2,1,0:T(8,128)(2,1)S(1)} %get-tuple-element.22), channel_id=1, source_target_pairs={{0,1},{1,0},{2,3},{3,2},{4,5},{5,4},{6,7},{7,6},{8,9},{9,8},{10,11... | collective-permute-start | bytes 1572872 | tf_op jit(solution)/shard_map/ppermute | solution.py:18
  148.0 17.5 %collective-permute-start.44 = (bf16[7,2,128,128]{3,2,1,0:T(8,128)(2,1)S(1)}, bf16[7,2,128,128]{3,2,1,0:T(8,128)(2,1)S(1)}, u32[]{:S(2)}, u32[]{:S(2)}) collective-permute-start(bf16[7,2,128,128]{3,2,1,0:T(8,128)(2,1)S(1)} %get-tuple-element.24), channel_id=1, source_target_pairs={{0,3},{1,2},{2,1},{3,0},{4,7},{5,6},{6,5},{7,4},{8,11},{9,10},{10,... | collective-permute-start | bytes 1376264 | tf_op jit(solution)/shard_map/ppermute | solution.py:18
  152.3 22.1 %collective-permute-start.46 = (bf16[7,2,128,128]{3,2,1,0:T(8,128)(2,1)S(1)}, bf16[7,2,128,128]{3,2,1,0:T(8,128)(2,1)S(1)}, u32[]{:S(2)}, u32[]{:S(2)}) collective-permute-start(bf16[7,2,128,128]{3,2,1,0:T(8,128)(2,1)S(1)} %get-tuple-element.26), channel_id=1, source_target_pairs={{0,3},{1,2},{2,1},{3,0},{4,7},{5,6},{6,5},{7,4},{8,11},{9,10},{10,... | collective-permute-start | bytes 1376264 | tf_op jit(solution)/shard_map/ppermute | solution.py:18
  153.1 32.4 %collective-permute-start.24 = (bf16[2,256,256]{2,1,0:T(8,128)(2,1)S(1)}, bf16[2,256,256]{2,1,0:T(8,128)(2,1)S(1)}, u32[]{:S(2)}, u32[]{:S(2)}) collective-permute-start(bf16[2,256,256]{2,1,0:T(8,128)(2,1)S(1)} %get-tuple-element.33), channel_id=1, source_target_pairs={{1,0},{2,1},{3,2},{4,3},{5,4},{6,5},{7,6},{8,7},{9,8},{10,9},{11,1... | collective-permute-start | bytes 786440 | tf_op jit(solution)/shard_map/ppermute | solution.py:291
  155.0 30.5 %collective-permute-start.23 = (bf16[2,256,256]{2,1,0:T(8,128)(2,1)S(1)}, bf16[2,256,256]{2,1,0:T(8,128)(2,1)S(1)}, u32[]{:S(2)}, u32[]{:S(2)}) collective-permute-start(bf16[2,256,256]{2,1,0:T(8,128)(2,1)S(1)} %get-tuple-element.34), channel_id=1, source_target_pairs={{0,1},{1,2},{2,3},{3,4},{4,5},{5,6},{6,7},{7,8},{8,9},{9,10},{10,1... | collective-permute-start | bytes 786440 | tf_op jit(solution)/shard_map/ppermute | solution.py:290
  (38 other events, 620.3 us)

commit v4 on v3

--- a/solution.py
+++ b/solution.py
@@ -94,7 +94,7 @@
     )
 
 
-def level0_body(color, base, count, src, rank, *refs):
+def level0_body(color, base, count, part, src, rank, *refs):
     bufs, w, out = refs[:16], refs[16], refs[17]
     xs = refs[18]
     me = lax.axis_index("grp")
@@ -113,7 +113,7 @@
 
             @pl.when(which == t)
             def _():
-                xs[i] = bufs[t][first & 1]
+                xs[i] = bufs[t][first & 1, :, part]
 
         return carry
 
@@ -124,11 +124,12 @@
         out[i, 0], out[i, 1] = combine(p, n, k, live)
 
 
-def level0(color, base, count, src, rank, bufs, w):
-    _, _, n, rows = bufs[0].shape
+def level0(color, base, count, part, src, rank, bufs, w):
+    rows = bufs[0].shape[3]
+    n = part.stop - part.start
     k = w.shape[-2]
     return call(
-        functools.partial(level0_body, color, base, count),
+        functools.partial(level0_body, color, base, count, part),
         [src, rank], [*bufs, w],
         jax.ShapeDtypeStruct((count, 2, n, k), BF16),
         [pltpu.VMEM((count, 2, n, rows), BF16)],
@@ -196,9 +197,10 @@
     lax.fori_loop(0, out.shape[0] * per, body, 0)
 
 
-def first_body(base, order, rank, ready, own, other, s2, w, xs, out):
+def first_body(base, order, rank, *refs):
+    ready, (own, other, s2, w, xs, out) = refs[:-6], refs[-6:]
     for i in range(base):
-        fill(xs, i, ready[i, 0], ready[i, 1])
+        fill(xs, i, ready[0][i, 0], ready[0][i, 1])
     count, _, n, k = own.shape
     upper = (lax.axis_index("mem") >> 1) & 1 == 1
     for i in range(count):
@@ -213,11 +215,11 @@
 
 def first_outward(order, rank, ready, own, other, s2, w):
     count, _, n, k = own.shape
-    base = ready.shape[0]
+    base = ready[0].shape[0] if ready else 0
     far = base + count
     return call(
         functools.partial(first_body, base, order),
-        [rank], [ready, own, other, s2, w],
+        [rank], [*ready, own, other, s2, w],
         [
             jax.ShapeDtypeStruct((far, 2 * n, 2 * k), BF16),
             jax.ShapeDtypeStruct((len(order), 2, n, w.shape[4] // 4), BF16),
@@ -233,17 +235,21 @@
     )
 
 
-def final_body(first, base, last, out):
-    n = first.shape[1]
-    out[:, :n] = first[...]
-    out[:, n:] = (base[...] + last[...].astype(F32)).astype(BF16)
-
-
-def final(first, base, last):
-    parts, n, rows = first.shape
-    return call(
-        final_body, [], [first, base, last],
-        jax.ShapeDtypeStruct((parts, 2 * n, rows), BF16),
+def final_body(*refs):
+    done, (base, last, out) = refs[:-3], refs[-3:]
+    at = 0
+    for v in done:
+        out[:, at : at + v.shape[1]] = v[...]
+        at += v.shape[1]
+    out[:, at:] = (base[...] + last[...].astype(F32)).astype(BF16)
+
+
+def final(done, base, last):
+    parts, n, rows = base.shape
+    n += sum(v.shape[1] for v in done)
+    return call(
+        final_body, [], [*done, base, last],
+        jax.ShapeDtypeStruct((parts, n, rows), BF16),
     )
 
 
@@ -291,38 +297,37 @@
     high = lax.ppermute(incident[:, :, :leaf], axes, backward)
     near = near_field(near_mask, incident, low, high, near_blocks)
 
-    cut = far // 2
-    spans = ((0, cut), (cut, far - cut))
-
-    pieces = []
-    for h in range(2):
-        at = slice(2 * h * q, 2 * (h + 1) * q)
-        level1 = []
-        for base, count in spans:
-            lev0 = level0(h, base, count, far_source.T, far_rank, bufs[h], basis_in)
-            lev0_pair = swap(lev0, "mem", 1)
-            lev1, lev1_pair = section(
-                base, 0, far_rank, lev0, lev0_pair, [section_one, section_pair]
-            )
-            level1.append((lev1, swap(lev1_pair, "mem", 3)))
-        (ready,) = section(0, 1, far_rank, *level1[0], [section_two])
-        early = 2 - h
+    def pair_levels(color, base, count, part):
+        lev0 = level0(color, base, count, part, far_source.T, far_rank, bufs[color], basis_in)
+        lev0_pair = swap(lev0, "mem", 1)
+        lev1, lev1_pair = section(base, 0, far_rank, lev0, lev0_pair, [section_one, section_pair])
+        return lev1, swap(lev1_pair, "mem", 3)
+
+    def outgoing(at, split, ready, level1):
         xs, sent = first_outward(
-            (2, 1)[:early], far_rank, ready, *level1[1],
+            (2,) if split else (2, 1), far_rank, ready, *level1,
             section_two, basis_out,
         )
         sent = swap(sent, "mem", 1)
-        if h == 0:
-            sent = (sent[0], sent[1])
-        else:
+        if split:
             part = outward(BF16, (1,), xs, basis_out)
             sent = (sent[0], swap(part, "mem", 1)[0])
+        else:
+            sent = (sent[0], sent[1])
         other = outward(F32, (3,), xs, basis_out)[0]
         last = swap((other + sent[0].astype(F32)).astype(BF16), "mem", 3)
         kept = outward(F32, (0,), xs, basis_out)[0]
-        pieces.append((kept + sent[1].astype(F32) + near[:, at], last))
-    base, last = pieces[0]
-    return final((base + last.astype(F32)).astype(BF16), *pieces[1])
+        return kept + sent[1].astype(F32) + near[:, at], last
+
+    cut = far * 3 // 7
+    half, first, second = slice(0, 2 * q), slice(0, q), slice(q, 2 * q)
+    done = []
+    level1 = pair_levels(0, 0, cut, half)
+    (ready,) = section(0, 1, far_rank, *level1, [section_two])
+    done.append(outgoing(half, False, [ready], pair_levels(0, cut, far - cut, half)))
+    done.append(outgoing(slice(2 * q, 3 * q), False, [], pair_levels(1, 0, far, first)))
+    base, last = outgoing(slice(3 * q, 4 * q), True, [], pair_levels(1, 0, far, second))
+    return final([(b + v.astype(F32)).astype(BF16) for b, v in done], base, last)
 
 
 def solution(mesh):

time: 202 us -> 221 us (1.094)
  the two profiles are of different devices: /device:TPU:6 before, /device:TPU:24 now
where the time goes in v4:
time: 221 us
  waiting for transfers between devices  116 us (52%)
  starting transfers between devices  59.7 us (27%)
  Pallas kernels  43.6 us (20%)
    ppermute x32, waiting for transfers between devices, swap(): lax.ppermute(value, axis, [(i, i ^ mask) for i in range(lax.axis_size(axi...  57.9 us
    ppermute x18, waiting for transfers between devices, ring(): return lax.ppermute(value, 'grp', perm)  57.8 us
    pallas_call x21, Pallas kernels, call(): pl.pallas_call(body, in_specs=[SMEM] * len(scalars) + [pl.BlockSpec(memor...  43.6 us
    ppermute x32, starting transfers between devices, swap(): lax.ppermute(value, axis, [(i, i ^ mask) for i in range(lax.axis_size(axi...  32.2 us
    ppermute x18, starting transfers between devices, ring(): return lax.ppermute(value, 'grp', perm)  21.6 us
  transfers between devices with their start and end apart: 52, of which 25 were waited for; matrix products, arithmetic and copies ran while one was open for 0% of the time, Pallas kernels for 19%

profile of v4, /device:TPU:24, one launch (start us, length us, event | category | flops | bytes accessed | tf_op | source)
XLA Modules:
  0.0 221.2 jit_solution(2141658264596327901)
XLA Ops:
  4.4 6.0 %collective-permute-done = bf16[1,2,128,512]{3,2,1,0:T(8,128)(2,1)S(1)} collective-permute-done((bf16[1,2,128,512]{3,2,1,0:T(8,128)(2,1)S(1)}, bf16[1,2,128,512]{3,2,1,0:T(8,128)(2,1)S(1)}, u32[]{:S(2)}, u32[]{:S(2)}) %collective-permute-start) | collective-permute-done | bytes 262176 | tf_op jit(solution)/shard_map/ppermute | solution.py:27
  13.7 3.2 %collective-permute-start.26 = (bf16[1,2,128,512]{3,2,1,0:T(8,128)(2,1)S(1)}, bf16[1,2,128,512]{3,2,1,0:T(8,128)(2,1)S(1)}, u32[]{:S(2)}, u32[]{:S(2)}) collective-permute-start(bf16[1,2,128,512]{3,2,1,0:T(8,128)(2,1)S(1)} %get-tuple-element.35), channel_id=1, source_target_pairs={{0,32},{4,36},{8,40},{12,44},{16,48},{20,52},{24,56},{28,60},{32,6... | collective-permute-start | bytes 786440 | tf_op jit(solution)/shard_map/ppermute | solution.py:27
  17.0 3.8 %collective-permute-done.2 = bf16[1,2,128,512]{3,2,1,0:T(8,128)(2,1)S(1)} collective-permute-done((bf16[1,2,128,512]{3,2,1,0:T(8,128)(2,1)S(1)}, bf16[1,2,128,512]{3,2,1,0:T(8,128)(2,1)S(1)}, u32[]{:S(2)}, u32[]{:S(2)}) %collective-permute-start.2) | collective-permute-done | bytes 262176 | tf_op jit(solution)/shard_map/ppermute | solution.py:27
  24.1 3.9 %collective-permute-done.27 = bf16[1,2,128,512]{3,2,1,0:T(8,128)(2,1)S(1)} collective-permute-done((bf16[1,2,128,512]{3,2,1,0:T(8,128)(2,1)S(1)}, bf16[1,2,128,512]{3,2,1,0:T(8,128)(2,1)S(1)}, u32[]{:S(2)}, u32[]{:S(2)}) %collective-permute-start.27) | collective-permute-done | bytes 262176 | tf_op jit(solution)/shard_map/ppermute | solution.py:27
  31.4 7.9 %collective-permute-done.5.refs_4_ = bf16[2,2,128,512]{3,2,1,0:T(8,128)(2,1)S(1)} collective-permute-done((bf16[2,2,128,512]{3,2,1,0:T(8,128)(2,1)S(1)}, bf16[2,2,128,512]{3,2,1,0:T(8,128)(2,1)S(1)}, u32[]{:S(2)}, u32[]{:S(2)}) %collective-permute-start.5) | collective-permute-done | bytes 524320 | tf_op jit(solution)/shard_map/ppermute | solution.py:27
  41.4 9.0 %collective-permute-done.6.refs_5_ = bf16[2,2,128,512]{3,2,1,0:T(8,128)(2,1)S(1)} collective-permute-done((bf16[2,2,128,512]{3,2,1,0:T(8,128)(2,1)S(1)}, bf16[2,2,128,512]{3,2,1,0:T(8,128)(2,1)S(1)}, u32[]{:S(2)}, u32[]{:S(2)}) %collective-permute-start.6) | collective-permute-done | bytes 524320 | tf_op jit(solution)/shard_map/ppermute | solution.py:27
  57.9 7.1 %collective-permute-done.32.refs_5_ = bf16[2,2,128,512]{3,2,1,0:T(8,128)(2,1)S(1)} collective-permute-done((bf16[2,2,128,512]{3,2,1,0:T(8,128)(2,1)S(1)}, bf16[2,2,128,512]{3,2,1,0:T(8,128)(2,1)S(1)}, u32[]{:S(2)}, u32[]{:S(2)}) %collective-permute-start.32) | collective-permute-done | bytes 524320 | tf_op jit(solution)/shard_map/ppermute | solution.py:27
  67.5 2.8 %collective-permute-done.7.refs_6_ = bf16[2,2,128,512]{3,2,1,0:T(8,128)(2,1)S(1)} collective-permute-done((bf16[2,2,128,512]{3,2,1,0:T(8,128)(2,1)S(1)}, bf16[2,2,128,512]{3,2,1,0:T(8,128)(2,1)S(1)}, u32[]{:S(2)}, u32[]{:S(2)}) %collective-permute-start.7) | collective-permute-done | bytes 524320 | tf_op jit(solution)/shard_map/ppermute | solution.py:27
  70.8 9.0 %collective-permute-done.8.refs_7_ = bf16[2,2,128,512]{3,2,1,0:T(8,128)(2,1)S(1)} collective-permute-done((bf16[2,2,128,512]{3,2,1,0:T(8,128)(2,1)S(1)}, bf16[2,2,128,512]{3,2,1,0:T(8,128)(2,1)S(1)}, u32[]{:S(2)}, u32[]{:S(2)}) %collective-permute-start.8) | collective-permute-done | bytes 524320 | tf_op jit(solution)/shard_map/ppermute | solution.py:27
  86.0 3.6 %shard_map.105.own = bf16[14,2,64,128]{3,2,1,0:T(8,128)(2,1)S(1)} custom-call(s32[14,32]{1,0:T(8,128)S(1)} %bitcast.19, s32[1,14]{1,0:T(1,128)S(1)} %copy-done.6, bf16[2,2,128,512]{3,2,1,0:T(8,128)(2,1)S(1)} %pad_maximum_fusion.1.refs_0_, bf16[2,2,128,512]{3,2,1,0:T(8,128)(2,1)S(1)} %constant_dynamic-update-slice_fusion.2.refs_1_, ...), custom_call_target="tpu_custom_call" | custom-call | tf_op jit(solution)/shard_map/pallas_call | solution.py:46
  94.3 3.6 %shard_map.100.own = bf16[14,2,64,128]{3,2,1,0:T(8,128)(2,1)S(1)} custom-call(s32[14,32]{1,0:T(8,128)S(1)} %bitcast.21, s32[1,14]{1,0:T(1,128)S(1)} %copy-done.6, bf16[2,2,128,512]{3,2,1,0:T(8,128)(2,1)S(1)} %pad_maximum_fusion.1.refs_0_, bf16[2,2,128,512]{3,2,1,0:T(8,128)(2,1)S(1)} %constant_dynamic-update-slice_fusion.2.refs_1_, ...), custom_call_target="tpu_custom_call" | custom-call | tf_op jit(solution)/shard_map/pallas_call | solution.py:46
  102.1 20.8 %collective-permute-done.18.refs_1_ = bf16[1,1,14,2,128,256]{5,4,3,2,1,0:T(8,128)(2,1)S(1)} collective-permute-done((bf16[1,1,14,2,128,256]{5,4,3,2,1,0:T(8,128)(2,1)}, bf16[1,1,14,2,128,256]{5,4,3,2,1,0:T(8,128)(2,1)S(1)}, u32[]{:S(2)}, u32[]{:S(2)}) %collective-permute-start.18) | collective-permute-done | bytes 1835040 | tf_op jit(solution)/shard_map/ppermute | solution.py:18
  122.9 9.8 %collective-permute-done.47.other = bf16[14,2,64,128]{3,2,1,0:T(8,128)(2,1)S(1)} collective-permute-done((bf16[14,2,64,128]{3,2,1,0:T(8,128)(2,1)S(1)}, bf16[14,2,64,128]{3,2,1,0:T(8,128)(2,1)S(1)}, u32[]{:S(2)}, u32[]{:S(2)}) %collective-permute-start.47) | collective-permute-done | bytes 458784 | tf_op jit(solution)/shard_map/ppermute | solution.py:18
  134.6 4.1 %collective-permute-start.48 = (bf16[14,2,64,128]{3,2,1,0:T(8,128)(2,1)S(1)}, bf16[14,2,64,128]{3,2,1,0:T(8,128)(2,1)S(1)}, u32[]{:S(2)}, u32[]{:S(2)}) collective-permute-start(bf16[14,2,64,128]{3,2,1,0:T(8,128)(2,1)S(1)} %get-tuple-element.30), channel_id=1, source_target_pairs={{0,3},{1,2},{2,1},{3,0},{4,7},{5,6},{6,5},{7,4},{8,11},{9,10},{10,... | collective-permute-start | bytes 1376264 | tf_op jit(solution)/shard_map/ppermute | solution.py:18
  138.7 5.2 %collective-permute-done.20.other = bf16[8,2,128,128]{3,2,1,0:T(8,128)(2,1)S(1)} collective-permute-done((bf16[8,2,128,128]{3,2,1,0:T(8,128)(2,1)S(1)}, bf16[8,2,128,128]{3,2,1,0:T(8,128)(2,1)S(1)}, u32[]{:S(2)}, u32[]{:S(2)}) %collective-permute-start.20) | collective-permute-done | bytes 524320 | tf_op jit(solution)/shard_map/ppermute | solution.py:18
  145.3 4.1 %collective-permute-start.21 = (bf16[8,2,128,128]{3,2,1,0:T(8,128)(2,1)S(1)}, bf16[8,2,128,128]{3,2,1,0:T(8,128)(2,1)S(1)}, u32[]{:S(2)}, u32[]{:S(2)}) collective-permute-start(bf16[8,2,128,128]{3,2,1,0:T(8,128)(2,1)S(1)} %get-tuple-element.22), channel_id=1, source_target_pairs={{0,3},{1,2},{2,1},{3,0},{4,7},{5,6},{6,5},{7,4},{8,11},{9,10},{10,... | collective-permute-start | bytes 1572872 | tf_op jit(solution)/shard_map/ppermute | solution.py:18
  149.4 11.0 %collective-permute-done.17.other = bf16[6,2,128,128]{3,2,1,0:T(8,128)(2,1)S(1)} collective-permute-done((bf16[6,2,128,128]{3,2,1,0:T(8,128)(2,1)S(1)}, bf16[6,2,128,128]{3,2,1,0:T(8,128)(2,1)S(1)}, u32[]{:S(2)}, u32[]{:S(2)}) %collective-permute-start.17) | collective-permute-done | bytes 393248 | tf_op jit(solution)/shard_map/ppermute | solution.py:18
  161.6 3.9 %collective-permute-start.19 = (bf16[6,2,128,128]{3,2,1,0:T(8,128)(2,1)S(1)}, bf16[6,2,128,128]{3,2,1,0:T(8,128)(2,1)S(1)}, u32[]{:S(2)}, u32[]{:S(2)}) collective-permute-start(bf16[6,2,128,128]{3,2,1,0:T(8,128)(2,1)S(1)} %get-tuple-element.20), channel_id=1, source_target_pairs={{0,3},{1,2},{2,1},{3,0},{4,7},{5,6},{6,5},{7,4},{8,11},{9,10},{10,... | collective-permute-start | bytes 1179656 | tf_op jit(solution)/shard_map/ppermute | solution.py:18
  169.8 3.7 %collective-permute-start.23 = (bf16[2,256,256]{2,1,0:T(8,128)(2,1)S(1)}, bf16[2,256,256]{2,1,0:T(8,128)(2,1)S(1)}, u32[]{:S(2)}, u32[]{:S(2)}) collective-permute-start(bf16[2,256,256]{2,1,0:T(8,128)(2,1)S(1)} %get-tuple-element.38), channel_id=1, source_target_pairs={{0,1},{1,2},{2,3},{3,4},{4,5},{5,6},{6,7},{7,8},{8,9},{9,10},{10,1... | collective-permute-start | bytes 786440 | tf_op jit(solution)/shard_map/ppermute | solution.py:296
  178.8 3.8 %shard_map.96 = (bf16[14,256,256]{2,1,0:T(8,128)(2,1)S(1)}, bf16[2,2,128,512]{3,2,1,0:T(8,128)(2,1)S(1)}) custom-call(s32[1,14]{1,0:T(1,128)S(1)} %copy-done.6, bf16[6,2,128,128]{3,2,1,0:T(8,128)(2,1)S(1)} %shard_map.93.refs_0_, bf16[8,2,128,128]{3,2,1,0:T(8,128)(2,1)S(1)} %get-tuple-element.21.refs_1_, ...), custom_call_target="tpu_custom_call" | custom-call | tf_op jit(solution)/shard_map/pallas_call | solution.py:46
  187.7 4.2 %shard_map.102 = (bf16[14,128,256]{2,1,0:T(8,128)(2,1)S(1)}, bf16[2,2,64,512]{3,2,1,0:T(8,128)(2,1)S(1)}) custom-call(s32[1,14]{1,0:T(1,128)S(1)} %copy-done.6, bf16[14,2,64,128]{3,2,1,0:T(8,128)(2,1)S(1)} %get-tuple-element.25.refs_0_, bf16[14,2,64,128]{3,2,1,0:T(8,128)(2,1)S(1)} %collective-permute-done.44.refs_1_, ...), custom_call_target="tpu_custom_call" | custom-call | tf_op jit(solution)/shard_map/pallas_call | solution.py:46
  192.0 3.2 %shard_map.98 = f32[2,256,512]{2,1,0:T(8,128)S(1)} custom-call(s32[2,3]{1,0:T(2,128)S(1)} %copy-done.7, bf16[2,256,512]{2,1,0:T(8,128)(2,1)S(1)} %copy-done.3, bf16[2,256,256]{2,1,0:T(8,128)(2,1)S(1)} %collective-permute-done.23.low, bf16[2,256,256]{2,1,0:T(8,128)(2,1)S(1)} %collective-permute-done.24.high, bf16[2,3,2,256,256]{4,3,2,1,0:T(8,128)(2,1)S(1)} %copy-done.4), custom_call_target="tpu_custom_call" | custom-call | tf_op jit(solution)/shard_map/pallas_call | solution.py:46
  207.4 3.7 %collective-permute-start.51 = (bf16[2,64,512]{2,1,0:T(8,128)(2,1)S(1)}, bf16[2,64,512]{2,1,0:T(8,128)(2,1)S(1)}, u32[]{:S(2)}, u32[]{:S(2)}) collective-permute-start(bf16[2,64,512]{2,1,0:T(8,128)(2,1)S(1)} %fusion.6), channel_id=1, source_target_pairs={{0,3},{1,2},{2,1},{3,0},{4,7},{5,6},{6,5},{7,4},{8,11},{9,10},{10,... | collective-permute-start | bytes 393224 | tf_op jit(solution)/shard_map/ppermute | solution.py:18
  211.3 3.3 %collective-permute-start.25 = (bf16[2,128,512]{2,1,0:T(8,128)(2,1)S(1)}, bf16[2,128,512]{2,1,0:T(8,128)(2,1)S(1)}, u32[]{:S(2)}, u32[]{:S(2)}) collective-permute-start(bf16[2,128,512]{2,1,0:T(8,128)(2,1)S(1)} %fusion.2), channel_id=1, source_target_pairs={{0,3},{1,2},{2,1},{3,0},{4,7},{5,6},{6,5},{7,4},{8,11},{9,10},{10,... | collective-permute-start | bytes 786440 | tf_op jit(solution)/shard_map/ppermute | solution.py:18
  (139 shorter events, 79.9 us)
Async XLA Ops:
  10.5 18.3 %collective-permute-start.9 = (bf16[2,2,128,512]{3,2,1,0:T(8,128)(2,1)S(1)}, bf16[2,2,128,512]{3,2,1,0:T(8,128)(2,1)S(1)}, u32[]{:S(2)}, u32[]{:S(2)}) collective-permute-start(bf16[2,2,128,512]{3,2,1,0:T(8,128)(2,1)S(1)} %pad_maximum_fusion.refs_0_), channel_id=1, source_target_pairs={{0,4},{4,0},{8,12},{12,8},{16,20},{20,16},{24,28},{28,24},{32,36},... | collective-permute-start | bytes 1572872 | tf_op jit(solution)/shard_map/ppermute | solution.py:18
  20.8 18.5 %collective-permute-start.5 = (bf16[2,2,128,512]{3,2,1,0:T(8,128)(2,1)S(1)}, bf16[2,2,128,512]{3,2,1,0:T(8,128)(2,1)S(1)}, u32[]{:S(2)}, u32[]{:S(2)}) collective-permute-start(bf16[2,2,128,512]{3,2,1,0:T(8,128)(2,1)S(1)} %pad_maximum_fusion.refs_0_), channel_id=1, source_target_pairs={{0,96},{4,100},{8,104},{12,108},{16,112},{20,116},{24,120},{28,124... | collective-permute-start | bytes 1572872 | tf_op jit(solution)/shard_map/ppermute | solution.py:27
  23.2 16.1 %collective-permute-start.3 = (bf16[2,2,128,512]{3,2,1,0:T(8,128)(2,1)S(1)}, bf16[2,2,128,512]{3,2,1,0:T(8,128)(2,1)S(1)}, u32[]{:S(2)}, u32[]{:S(2)}) collective-permute-start(bf16[2,2,128,512]{3,2,1,0:T(8,128)(2,1)S(1)} %pad_maximum_fusion.refs_0_), channel_id=1, source_target_pairs={{0,32},{4,36},{8,40},{12,44},{16,48},{20,52},{24,56},{28,60},{32,6... | collective-permute-start | bytes 1572872 | tf_op jit(solution)/shard_map/ppermute | solution.py:27
  28.0 22.4 %collective-permute-start.6 = (bf16[2,2,128,512]{3,2,1,0:T(8,128)(2,1)S(1)}, bf16[2,2,128,512]{3,2,1,0:T(8,128)(2,1)S(1)}, u32[]{:S(2)}, u32[]{:S(2)}) collective-permute-start(bf16[2,2,128,512]{3,2,1,0:T(8,128)(2,1)S(1)} %constant_dynamic-update-slice_fusion.refs_1_), channel_id=1, source_target_pairs={{0,96},{4,100},{8,104},{12,108},{16,112},{20,116},{24,120},{28,124... | collective-permute-start | bytes 1572872 | tf_op jit(solution)/shard_map/ppermute | solution.py:27
  28.8 21.7 %collective-permute-start.4 = (bf16[2,2,128,512]{3,2,1,0:T(8,128)(2,1)S(1)}, bf16[2,2,128,512]{3,2,1,0:T(8,128)(2,1)S(1)}, u32[]{:S(2)}, u32[]{:S(2)}) collective-permute-start(bf16[2,2,128,512]{3,2,1,0:T(8,128)(2,1)S(1)} %constant_dynamic-update-slice_fusion.refs_1_), channel_id=1, source_target_pairs={{0,32},{4,36},{8,40},{12,44},{16,48},{20,52},{24,56},{28,60},{32,6... | collective-permute-start | bytes 1572872 | tf_op jit(solution)/shard_map/ppermute | solution.py:27
  40.5 15.5 %collective-permute-start.29 = (bf16[2,2,128,512]{3,2,1,0:T(8,128)(2,1)S(1)}, bf16[2,2,128,512]{3,2,1,0:T(8,128)(2,1)S(1)}, u32[]{:S(2)}, u32[]{:S(2)}) collective-permute-start(bf16[2,2,128,512]{3,2,1,0:T(8,128)(2,1)S(1)} %pad_maximum_fusion.1.refs_0_), channel_id=1, source_target_pairs={{0,8},{4,12},{8,16},{12,20},{16,24},{20,28},{24,0},{28,4},{32,40},... | collective-permute-start | bytes 1572872 | tf_op jit(solution)/shard_map/ppermute | solution.py:27
  51.6 15.4 %collective-permute-start.30 = (bf16[2,2,128,512]{3,2,1,0:T(8,128)(2,1)S(1)}, bf16[2,2,128,512]{3,2,1,0:T(8,128)(2,1)S(1)}, u32[]{:S(2)}, u32[]{:S(2)}) collective-permute-start(bf16[2,2,128,512]{3,2,1,0:T(8,128)(2,1)S(1)} %constant_dynamic-update-slice_fusion.2.refs_1_), channel_id=1, source_target_pairs={{0,8},{4,12},{8,16},{12,20},{16,24},{20,28},{24,0},{28,4},{32,40},... | collective-permute-start | bytes 1572872 | tf_op jit(solution)/shard_map/ppermute | solution.py:27
  64.9 14.9 %collective-permute-start.8 = (bf16[2,2,128,512]{3,2,1,0:T(8,128)(2,1)S(1)}, bf16[2,2,128,512]{3,2,1,0:T(8,128)(2,1)S(1)}, u32[]{:S(2)}, u32[]{:S(2)}) collective-permute-start(bf16[2,2,128,512]{3,2,1,0:T(8,128)(2,1)S(1)} %collective-permute-done.6.refs_5_), channel_id=1, source_target_pairs={{0,96},{4,100},{8,104},{12,108},{16,112},{20,116},{24,120},{28,124... | collective-permute-start | bytes 1572872 | tf_op jit(solution)/shard_map/ppermute | solution.py:27
  67.0 14.7 %collective-permute-start.39 = (bf16[2,2,128,512]{3,2,1,0:T(8,128)(2,1)S(1)}, bf16[2,2,128,512]{3,2,1,0:T(8,128)(2,1)S(1)}, u32[]{:S(2)}, u32[]{:S(2)}) collective-permute-start(bf16[2,2,128,512]{3,2,1,0:T(8,128)(2,1)S(1)} %collective-permute-done.31.refs_4_), channel_id=1, source_target_pairs={{0,4},{4,0},{8,12},{12,8},{16,20},{20,16},{24,28},{28,24},{32,36},... | collective-permute-start | bytes 1572872 | tf_op jit(solution)/shard_map/ppermute | solution.py:18
  67.5 15.1 %collective-permute-start.33 = (bf16[2,2,128,512]{3,2,1,0:T(8,128)(2,1)S(1)}, bf16[2,2,128,512]{3,2,1,0:T(8,128)(2,1)S(1)}, u32[]{:S(2)}, u32[]{:S(2)}) collective-permute-start(bf16[2,2,128,512]{3,2,1,0:T(8,128)(2,1)S(1)} %collective-permute-done.29.refs_2_), channel_id=1, source_target_pairs={{0,8},{4,12},{8,16},{12,20},{16,24},{20,28},{24,0},{28,4},{32,40},... | collective-permute-start | bytes 1572872 | tf_op jit(solution)/shard_map/ppermute | solution.py:27
  79.8 43.1 %collective-permute-start.18 = (bf16[1,1,14,2,128,256]{5,4,3,2,1,0:T(8,128)(2,1)}, bf16[1,1,14,2,128,256]{5,4,3,2,1,0:T(8,128)(2,1)S(1)}, u32[]{:S(2)}, u32[]{:S(2)}) collective-permute-start(bf16[1,1,14,2,128,256]{5,4,3,2,1,0:T(8,128)(2,1)} %refs_0_.9), channel_id=1, source_target_pairs={{0,1},{1,0},{2,3},{3,2},{4,5},{5,4},{6,7},{7,6},{8,9},{9,8},{10,11... | collective-permute-start | bytes 5505032 | tf_op jit(solution)/shard_map/ppermute | solution.py:18
  89.6 43.1 %collective-permute-start.47 = (bf16[14,2,64,128]{3,2,1,0:T(8,128)(2,1)S(1)}, bf16[14,2,64,128]{3,2,1,0:T(8,128)(2,1)S(1)}, u32[]{:S(2)}, u32[]{:S(2)}) collective-permute-start(bf16[14,2,64,128]{3,2,1,0:T(8,128)(2,1)S(1)} %shard_map.105.own), channel_id=1, source_target_pairs={{0,1},{1,0},{2,3},{3,2},{4,5},{5,4},{6,7},{7,6},{8,9},{9,8},{10,11... | collective-permute-start | bytes 1376264 | tf_op jit(solution)/shard_map/ppermute | solution.py:18
  93.9 50.1 %collective-permute-start.20 = (bf16[8,2,128,128]{3,2,1,0:T(8,128)(2,1)S(1)}, bf16[8,2,128,128]{3,2,1,0:T(8,128)(2,1)S(1)}, u32[]{:S(2)}, u32[]{:S(2)}) collective-permute-start(bf16[8,2,128,128]{3,2,1,0:T(8,128)(2,1)S(1)} %shard_map.94.own), channel_id=1, source_target_pairs={{0,1},{1,0},{2,3},{3,2},{4,5},{5,4},{6,7},{7,6},{8,9},{9,8},{10,11... | collective-permute-start | bytes 1572872 | tf_op jit(solution)/shard_map/ppermute | solution.py:18
  97.9 67.7 %collective-permute-start.43 = (bf16[14,2,64,128]{3,2,1,0:T(8,128)(2,1)S(1)}, bf16[14,2,64,128]{3,2,1,0:T(8,128)(2,1)S(1)}, u32[]{:S(2)}, u32[]{:S(2)}) collective-permute-start(bf16[14,2,64,128]{3,2,1,0:T(8,128)(2,1)S(1)} %shard_map.100.own), channel_id=1, source_target_pairs={{0,1},{1,0},{2,3},{3,2},{4,5},{5,4},{6,7},{7,6},{8,9},{9,8},{10,11... | collective-permute-start | bytes 1376264 | tf_op jit(solution)/shard_map/ppermute | solution.py:18
  101.7 58.7 %collective-permute-start.17 = (bf16[6,2,128,128]{3,2,1,0:T(8,128)(2,1)S(1)}, bf16[6,2,128,128]{3,2,1,0:T(8,128)(2,1)S(1)}, u32[]{:S(2)}, u32[]{:S(2)}) collective-permute-start(bf16[6,2,128,128]{3,2,1,0:T(8,128)(2,1)S(1)} %shard_map.91.own), channel_id=1, source_target_pairs={{0,1},{1,0},{2,3},{3,2},{4,5},{5,4},{6,7},{7,6},{8,9},{9,8},{10,11... | collective-permute-start | bytes 1179656 | tf_op jit(solution)/shard_map/ppermute | solution.py:18
  134.6 35.1 %collective-permute-start.48 = (bf16[14,2,64,128]{3,2,1,0:T(8,128)(2,1)S(1)}, bf16[14,2,64,128]{3,2,1,0:T(8,128)(2,1)S(1)}, u32[]{:S(2)}, u32[]{:S(2)}) collective-permute-start(bf16[14,2,64,128]{3,2,1,0:T(8,128)(2,1)S(1)} %get-tuple-element.30), channel_id=1, source_target_pairs={{0,3},{1,2},{2,1},{3,0},{4,7},{5,6},{6,5},{7,4},{8,11},{9,10},{10,... | collective-permute-start | bytes 1376264 | tf_op jit(solution)/shard_map/ppermute | solution.py:18
  145.3 33.5 %collective-permute-start.21 = (bf16[8,2,128,128]{3,2,1,0:T(8,128)(2,1)S(1)}, bf16[8,2,128,128]{3,2,1,0:T(8,128)(2,1)S(1)}, u32[]{:S(2)}, u32[]{:S(2)}) collective-permute-start(bf16[8,2,128,128]{3,2,1,0:T(8,128)(2,1)S(1)} %get-tuple-element.22), channel_id=1, source_target_pairs={{0,3},{1,2},{2,1},{3,0},{4,7},{5,6},{6,5},{7,4},{8,11},{9,10},{10,... | collective-permute-start | bytes 1572872 | tf_op jit(solution)/shard_map/ppermute | solution.py:18
  161.6 16.3 %collective-permute-start.19 = (bf16[6,2,128,128]{3,2,1,0:T(8,128)(2,1)S(1)}, bf16[6,2,128,128]{3,2,1,0:T(8,128)(2,1)S(1)}, u32[]{:S(2)}, u32[]{:S(2)}) collective-permute-start(bf16[6,2,128,128]{3,2,1,0:T(8,128)(2,1)S(1)} %get-tuple-element.20), channel_id=1, source_target_pairs={{0,3},{1,2},{2,1},{3,0},{4,7},{5,6},{6,5},{7,4},{8,11},{9,10},{10,... | collective-permute-start | bytes 1179656 | tf_op jit(solution)/shard_map/ppermute | solution.py:18
  167.4 20.2 %collective-permute-start.44 = (bf16[14,2,64,128]{3,2,1,0:T(8,128)(2,1)S(1)}, bf16[14,2,64,128]{3,2,1,0:T(8,128)(2,1)S(1)}, u32[]{:S(2)}, u32[]{:S(2)}) collective-permute-start(bf16[14,2,64,128]{3,2,1,0:T(8,128)(2,1)S(1)} %get-tuple-element.26), channel_id=1, source_target_pairs={{0,3},{1,2},{2,1},{3,0},{4,7},{5,6},{6,5},{7,4},{8,11},{9,10},{10,... | collective-permute-start | bytes 1376264 | tf_op jit(solution)/shard_map/ppermute | solution.py:18
  167.6 24.4 %collective-permute-start.24 = (bf16[2,256,256]{2,1,0:T(8,128)(2,1)S(1)}, bf16[2,256,256]{2,1,0:T(8,128)(2,1)S(1)}, u32[]{:S(2)}, u32[]{:S(2)}) collective-permute-start(bf16[2,256,256]{2,1,0:T(8,128)(2,1)S(1)} %get-tuple-element.37), channel_id=1, source_target_pairs={{1,0},{2,1},{3,2},{4,3},{5,4},{6,5},{7,6},{8,7},{9,8},{10,9},{11,1... | collective-permute-start | bytes 786440 | tf_op jit(solution)/shard_map/ppermute | solution.py:297
  169.8 22.2 %collective-permute-start.23 = (bf16[2,256,256]{2,1,0:T(8,128)(2,1)S(1)}, bf16[2,256,256]{2,1,0:T(8,128)(2,1)S(1)}, u32[]{:S(2)}, u32[]{:S(2)}) collective-permute-start(bf16[2,256,256]{2,1,0:T(8,128)(2,1)S(1)} %get-tuple-element.38), channel_id=1, source_target_pairs={{0,1},{1,2},{2,3},{3,4},{4,5},{5,6},{6,7},{7,8},{8,9},{9,10},{10,1... | collective-permute-start | bytes 786440 | tf_op jit(solution)/shard_map/ppermute | solution.py:296
  177.8 29.5 %collective-permute-start.50 = (bf16[1,2,64,512]{3,2,1,0:T(8,128)(2,1)S(1)}, bf16[1,2,64,512]{3,2,1,0:T(8,128)(2,1)S(1)}, u32[]{:S(2)}, u32[]{:S(2)}) collective-permute-start(bf16[1,2,64,512]{3,2,1,0:T(8,128)(2,1)S(1)} %get-tuple-element.32), channel_id=1, source_target_pairs={{0,1},{1,0},{2,3},{3,2},{4,5},{5,4},{6,7},{7,6},{8,9},{9,8},{10,11... | collective-permute-start | bytes 393224 | tf_op jit(solution)/shard_map/ppermute | solution.py:18
  182.6 28.6 %collective-permute-start.22 = (bf16[2,2,128,512]{3,2,1,0:T(8,128)(2,1)S(1)}, bf16[2,2,128,512]{3,2,1,0:T(8,128)(2,1)S(1)}, u32[]{:S(2)}, u32[]{:S(2)}) collective-permute-start(bf16[2,2,128,512]{3,2,1,0:T(8,128)(2,1)S(1)} %get-tuple-element.24), channel_id=1, source_target_pairs={{0,1},{1,0},{2,3},{3,2},{4,5},{5,4},{6,7},{7,6},{8,9},{9,8},{10,11... | collective-permute-start | bytes 1572872 | tf_op jit(solution)/shard_map/ppermute | solution.py:18
  191.9 19.2 %collective-permute-start.45 = (bf16[2,2,64,512]{3,2,1,0:T(8,128)(2,1)S(1)}, bf16[2,2,64,512]{3,2,1,0:T(8,128)(2,1)S(1)}, u32[]{:S(2)}, u32[]{:S(2)}) collective-permute-start(bf16[2,2,64,512]{3,2,1,0:T(8,128)(2,1)S(1)} %get-tuple-element.28), channel_id=1, source_target_pairs={{0,1},{1,0},{2,3},{3,2},{4,5},{5,4},{6,7},{7,6},{8,9},{9,8},{10,11... | collective-permute-start | bytes 786440 | tf_op jit(solution)/shard_map/ppermute | solution.py:18
  (40 other events, 806.8 us)

commit v5 on v4

--- a/solution.py
+++ b/solution.py
@@ -300,7 +300,8 @@
     def pair_levels(color, base, count, part):
         lev0 = level0(color, base, count, part, far_source.T, far_rank, bufs[color], basis_in)
         lev0_pair = swap(lev0, "mem", 1)
-        lev1, lev1_pair = section(base, 0, far_rank, lev0, lev0_pair, [section_one, section_pair])
+        (lev1_pair,) = section(base, 0, far_rank, lev0, lev0_pair, [section_pair])
+        (lev1,) = section(base, 0, far_rank, lev0, lev0_pair, [section_one])
         return lev1, swap(lev1_pair, "mem", 3)
 
     def outgoing(at, split, ready, level1):
@@ -319,7 +320,7 @@
         kept = outward(F32, (0,), xs, basis_out)[0]
         return kept + sent[1].astype(F32) + near[:, at], last
 
-    cut = far * 3 // 7
+    cut = far // 2
     half, first, second = slice(0, 2 * q), slice(0, q), slice(q, 2 * q)
     done = []
     level1 = pair_levels(0, 0, cut, half)

time: 221 us -> 221 us (level)
  the two profiles are of different devices: /device:TPU:24 before, /device:TPU:7 now
where the time goes in v5:
time: 221 us; the launch traced here: 219 us
  waiting for transfers between devices  98.7 us (45%)
  starting transfers between devices  71.3 us (32%)
  Pallas kernels  46.5 us (21%)
    ppermute x32, waiting for transfers between devices, swap(): lax.ppermute(value, axis, [(i, i ^ mask) for i in range(lax.axis_size(axi...  50.9 us
    ppermute x18, waiting for transfers between devices, ring(): return lax.ppermute(value, 'grp', perm)  47.7 us
    pallas_call x25, Pallas kernels, call(): pl.pallas_call(body, in_specs=[SMEM] * len(scalars) + [pl.BlockSpec(memor...  46.5 us
    ppermute x32, starting transfers between devices, swap(): lax.ppermute(value, axis, [(i, i ^ mask) for i in range(lax.axis_size(axi...  43.7 us
    ppermute x18, starting transfers between devices, ring(): return lax.ppermute(value, 'grp', perm)  21.2 us
    ppermute x1, starting transfers between devices, on_device(): high = lax.ppermute(incident[:, :, :leaf], axes, backward)  4.5 us
  transfers between devices with their start and end apart: 52, of which 19 were waited for; matrix products, arithmetic and copies ran while one was open for 0% of the time, Pallas kernels for 21%

profile of v5, /device:TPU:7, one launch (start us, length us, event | category | flops | bytes accessed | tf_op | source)
XLA Modules:
  0.0 218.9 jit_solution(16980813744547337677)
XLA Ops:
  3.5 4.8 %collective-permute-done = bf16[1,2,128,512]{3,2,1,0:T(8,128)(2,1)S(1)} collective-permute-done((bf16[1,2,128,512]{3,2,1,0:T(8,128)(2,1)S(1)}, bf16[1,2,128,512]{3,2,1,0:T(8,128)(2,1)S(1)}, u32[]{:S(2)}, u32[]{:S(2)}) %collective-permute-start) | collective-permute-done | bytes 262176 | tf_op jit(solution)/shard_map/ppermute | solution.py:27
  21.8 4.7 %collective-permute-done.27 = bf16[1,2,128,512]{3,2,1,0:T(8,128)(2,1)S(1)} collective-permute-done((bf16[1,2,128,512]{3,2,1,0:T(8,128)(2,1)S(1)}, bf16[1,2,128,512]{3,2,1,0:T(8,128)(2,1)S(1)}, u32[]{:S(2)}, u32[]{:S(2)}) %collective-permute-start.27) | collective-permute-done | bytes 262176 | tf_op jit(solution)/shard_map/ppermute | solution.py:27
  29.9 7.8 %collective-permute-done.5.refs_4_ = bf16[2,2,128,512]{3,2,1,0:T(8,128)(2,1)S(1)} collective-permute-done((bf16[2,2,128,512]{3,2,1,0:T(8,128)(2,1)S(1)}, bf16[2,2,128,512]{3,2,1,0:T(8,128)(2,1)S(1)}, u32[]{:S(2)}, u32[]{:S(2)}) %collective-permute-start.5) | collective-permute-done | bytes 524320 | tf_op jit(solution)/shard_map/ppermute | solution.py:27
  42.0 6.9 %collective-permute-done.6.refs_5_ = bf16[2,2,128,512]{3,2,1,0:T(8,128)(2,1)S(1)} collective-permute-done((bf16[2,2,128,512]{3,2,1,0:T(8,128)(2,1)S(1)}, bf16[2,2,128,512]{3,2,1,0:T(8,128)(2,1)S(1)}, u32[]{:S(2)}, u32[]{:S(2)}) %collective-permute-start.6) | collective-permute-done | bytes 524320 | tf_op jit(solution)/shard_map/ppermute | solution.py:27
  55.6 9.7 %collective-permute-done.32.refs_5_ = bf16[2,2,128,512]{3,2,1,0:T(8,128)(2,1)S(1)} collective-permute-done((bf16[2,2,128,512]{3,2,1,0:T(8,128)(2,1)S(1)}, bf16[2,2,128,512]{3,2,1,0:T(8,128)(2,1)S(1)}, u32[]{:S(2)}, u32[]{:S(2)}) %collective-permute-start.32) | collective-permute-done | bytes 524320 | tf_op jit(solution)/shard_map/ppermute | solution.py:27
  69.8 8.1 %collective-permute-done.8.refs_7_ = bf16[2,2,128,512]{3,2,1,0:T(8,128)(2,1)S(1)} collective-permute-done((bf16[2,2,128,512]{3,2,1,0:T(8,128)(2,1)S(1)}, bf16[2,2,128,512]{3,2,1,0:T(8,128)(2,1)S(1)}, u32[]{:S(2)}, u32[]{:S(2)}) %collective-permute-start.8) | collective-permute-done | bytes 524320 | tf_op jit(solution)/shard_map/ppermute | solution.py:27
  87.7 3.6 %shard_map.108.own = bf16[14,2,64,128]{3,2,1,0:T(8,128)(2,1)S(1)} custom-call(s32[14,32]{1,0:T(8,128)S(1)} %bitcast.19, s32[1,14]{1,0:T(1,128)S(1)} %copy-done.5, bf16[2,2,128,512]{3,2,1,0:T(8,128)(2,1)S(1)} %pad_maximum_fusion.1.refs_0_, bf16[2,2,128,512]{3,2,1,0:T(8,128)(2,1)S(1)} %constant_dynamic-update-slice_fusion.2.refs_1_, ...), custom_call_target="tpu_custom_call" | custom-call | tf_op jit(solution)/shard_map/pallas_call | solution.py:46
  99.1 3.6 %shard_map.102.own = bf16[14,2,64,128]{3,2,1,0:T(8,128)(2,1)S(1)} custom-call(s32[14,32]{1,0:T(8,128)S(1)} %bitcast.22, s32[1,14]{1,0:T(1,128)S(1)} %copy-done.5, bf16[2,2,128,512]{3,2,1,0:T(8,128)(2,1)S(1)} %pad_maximum_fusion.1.refs_0_, bf16[2,2,128,512]{3,2,1,0:T(8,128)(2,1)S(1)} %constant_dynamic-update-slice_fusion.2.refs_1_, ...), custom_call_target="tpu_custom_call" | custom-call | tf_op jit(solution)/shard_map/pallas_call | solution.py:46
  102.9 15.4 %collective-permute-done.18.refs_0_ = bf16[1,1,14,2,128,256]{5,4,3,2,1,0:T(8,128)(2,1)S(1)} collective-permute-done((bf16[1,1,14,2,128,256]{5,4,3,2,1,0:T(8,128)(2,1)}, bf16[1,1,14,2,128,256]{5,4,3,2,1,0:T(8,128)(2,1)S(1)}, u32[]{:S(2)}, u32[]{:S(2)}) %collective-permute-start.18) | collective-permute-done | bytes 1835040 | tf_op jit(solution)/shard_map/ppermute | solution.py:18
  118.3 9.8 %collective-permute-done.47.other = bf16[14,2,64,128]{3,2,1,0:T(8,128)(2,1)S(1)} collective-permute-done((bf16[14,2,64,128]{3,2,1,0:T(8,128)(2,1)S(1)}, bf16[14,2,64,128]{3,2,1,0:T(8,128)(2,1)S(1)}, u32[]{:S(2)}, u32[]{:S(2)}) %collective-permute-start.47) | collective-permute-done | bytes 458784 | tf_op jit(solution)/shard_map/ppermute | solution.py:18
  129.4 3.5 %collective-permute-start.48 = (bf16[14,2,64,128]{3,2,1,0:T(8,128)(2,1)S(1)}, bf16[14,2,64,128]{3,2,1,0:T(8,128)(2,1)S(1)}, u32[]{:S(2)}, u32[]{:S(2)}) collective-permute-start(bf16[14,2,64,128]{3,2,1,0:T(8,128)(2,1)S(1)} %shard_map.110), channel_id=1, source_target_pairs={{0,3},{1,2},{2,1},{3,0},{4,7},{5,6},{6,5},{7,4},{8,11},{9,10},{10,... | collective-permute-start | bytes 1376264 | tf_op jit(solution)/shard_map/ppermute | solution.py:18
  132.9 5.0 %collective-permute-done.17.other = bf16[7,2,128,128]{3,2,1,0:T(8,128)(2,1)S(1)} collective-permute-done((bf16[7,2,128,128]{3,2,1,0:T(8,128)(2,1)S(1)}, bf16[7,2,128,128]{3,2,1,0:T(8,128)(2,1)S(1)}, u32[]{:S(2)}, u32[]{:S(2)}) %collective-permute-start.17) | collective-permute-done | bytes 458784 | tf_op jit(solution)/shard_map/ppermute | solution.py:18
  139.0 3.5 %collective-permute-start.19 = (bf16[7,2,128,128]{3,2,1,0:T(8,128)(2,1)S(1)}, bf16[7,2,128,128]{3,2,1,0:T(8,128)(2,1)S(1)}, u32[]{:S(2)}, u32[]{:S(2)}) collective-permute-start(bf16[7,2,128,128]{3,2,1,0:T(8,128)(2,1)S(1)} %shard_map.93), channel_id=1, source_target_pairs={{0,3},{1,2},{2,1},{3,0},{4,7},{5,6},{6,5},{7,4},{8,11},{9,10},{10,... | collective-permute-start | bytes 1376264 | tf_op jit(solution)/shard_map/ppermute | solution.py:18
  142.4 5.3 %collective-permute-done.20.other = bf16[7,2,128,128]{3,2,1,0:T(8,128)(2,1)S(1)} collective-permute-done((bf16[7,2,128,128]{3,2,1,0:T(8,128)(2,1)S(1)}, bf16[7,2,128,128]{3,2,1,0:T(8,128)(2,1)S(1)}, u32[]{:S(2)}, u32[]{:S(2)}) %collective-permute-start.20) | collective-permute-done | bytes 458784 | tf_op jit(solution)/shard_map/ppermute | solution.py:18
  148.8 3.5 %collective-permute-start.21 = (bf16[7,2,128,128]{3,2,1,0:T(8,128)(2,1)S(1)}, bf16[7,2,128,128]{3,2,1,0:T(8,128)(2,1)S(1)}, u32[]{:S(2)}, u32[]{:S(2)}) collective-permute-start(bf16[7,2,128,128]{3,2,1,0:T(8,128)(2,1)S(1)} %shard_map.97), channel_id=1, source_target_pairs={{0,3},{1,2},{2,1},{3,0},{4,7},{5,6},{6,5},{7,4},{8,11},{9,10},{10,... | collective-permute-start | bytes 1376264 | tf_op jit(solution)/shard_map/ppermute | solution.py:18
  152.3 5.3 %collective-permute-done.43.other = bf16[14,2,64,128]{3,2,1,0:T(8,128)(2,1)S(1)} collective-permute-done((bf16[14,2,64,128]{3,2,1,0:T(8,128)(2,1)S(1)}, bf16[14,2,64,128]{3,2,1,0:T(8,128)(2,1)S(1)}, u32[]{:S(2)}, u32[]{:S(2)}) %collective-permute-start.43) | collective-permute-done | bytes 458784 | tf_op jit(solution)/shard_map/ppermute | solution.py:18
  158.9 3.5 %collective-permute-start.44 = (bf16[14,2,64,128]{3,2,1,0:T(8,128)(2,1)S(1)}, bf16[14,2,64,128]{3,2,1,0:T(8,128)(2,1)S(1)}, u32[]{:S(2)}, u32[]{:S(2)}) collective-permute-start(bf16[14,2,64,128]{3,2,1,0:T(8,128)(2,1)S(1)} %shard_map.104), channel_id=1, source_target_pairs={{0,3},{1,2},{2,1},{3,0},{4,7},{5,6},{6,5},{7,4},{8,11},{9,10},{10,... | collective-permute-start | bytes 1376264 | tf_op jit(solution)/shard_map/ppermute | solution.py:18
  162.4 4.5 %collective-permute-start.24 = (bf16[2,256,256]{2,1,0:T(8,128)(2,1)S(1)}, bf16[2,256,256]{2,1,0:T(8,128)(2,1)S(1)}, u32[]{:S(2)}, u32[]{:S(2)}) collective-permute-start(bf16[2,256,256]{2,1,0:T(8,128)(2,1)S(1)} %get-tuple-element.21), channel_id=1, source_target_pairs={{1,0},{2,1},{3,2},{4,3},{5,4},{6,5},{7,6},{8,7},{9,8},{10,9},{11,1... | collective-permute-start | bytes 786440 | tf_op jit(solution)/shard_map/ppermute | solution.py:297
  176.1 3.8 %shard_map.98 = (bf16[14,256,256]{2,1,0:T(8,128)(2,1)S(1)}, bf16[2,2,128,512]{3,2,1,0:T(8,128)(2,1)S(1)}) custom-call(s32[1,14]{1,0:T(1,128)S(1)} %copy-done.5, bf16[7,2,128,128]{3,2,1,0:T(8,128)(2,1)S(1)} %shard_map.94.refs_0_, bf16[7,2,128,128]{3,2,1,0:T(8,128)(2,1)S(1)} %shard_map.96.refs_1_, ...), custom_call_target="tpu_custom_call" | custom-call | tf_op jit(solution)/shard_map/pallas_call | solution.py:46
  183.0 4.2 %shard_map.105 = (bf16[14,128,256]{2,1,0:T(8,128)(2,1)S(1)}, bf16[2,2,64,512]{3,2,1,0:T(8,128)(2,1)S(1)}) custom-call(s32[1,14]{1,0:T(1,128)S(1)} %copy-done.5, bf16[14,2,64,128]{3,2,1,0:T(8,128)(2,1)S(1)} %shard_map.103.refs_0_, bf16[14,2,64,128]{3,2,1,0:T(8,128)(2,1)S(1)} %collective-permute-done.44.refs_1_, ...), custom_call_target="tpu_custom_call" | custom-call | tf_op jit(solution)/shard_map/pallas_call | solution.py:46
  187.3 3.2 %shard_map.100 = f32[2,256,512]{2,1,0:T(8,128)S(1)} custom-call(s32[2,3]{1,0:T(2,128)S(1)} %copy-done.7, bf16[2,256,512]{2,1,0:T(8,128)(2,1)S(1)} %copy-done.3, bf16[2,256,256]{2,1,0:T(8,128)(2,1)S(1)} %collective-permute-done.23.low, bf16[2,256,256]{2,1,0:T(8,128)(2,1)S(1)} %collective-permute-done.24.high, bf16[2,3,2,256,256]{4,3,2,1,0:T(8,128)(2,1)S(1)} %copy-done.4), custom_call_target="tpu_custom_call" | custom-call | tf_op jit(solution)/shard_map/pallas_call | solution.py:46
  202.2 3.6 %collective-permute-start.51 = (bf16[2,64,512]{2,1,0:T(8,128)(2,1)S(1)}, bf16[2,64,512]{2,1,0:T(8,128)(2,1)S(1)}, u32[]{:S(2)}, u32[]{:S(2)}) collective-permute-start(bf16[2,64,512]{2,1,0:T(8,128)(2,1)S(1)} %fusion.6), channel_id=1, source_target_pairs={{0,3},{1,2},{2,1},{3,0},{4,7},{5,6},{6,5},{7,4},{8,11},{9,10},{10,... | collective-permute-start | bytes 393224 | tf_op jit(solution)/shard_map/ppermute | solution.py:18
  208.7 3.5 %collective-permute-done.46 = bf16[2,64,512]{2,1,0:T(8,128)(2,1)S(1)} collective-permute-done((bf16[2,64,512]{2,1,0:T(8,128)(2,1)S(1)}, bf16[2,64,512]{2,1,0:T(8,128)(2,1)S(1)}, u32[]{:S(2)}, u32[]{:S(2)}) %collective-permute-start.46) | collective-permute-done | bytes 131104 | tf_op jit(solution)/shard_map/ppermute | solution.py:18
  212.4 5.5 %collective-permute-done.25 = bf16[2,128,512]{2,1,0:T(8,128)(2,1)S(1)} collective-permute-done((bf16[2,128,512]{2,1,0:T(8,128)(2,1)S(1)}, bf16[2,128,512]{2,1,0:T(8,128)(2,1)S(1)}, u32[]{:S(2)}, u32[]{:S(2)}) %collective-permute-start.25) | collective-permute-done | bytes 262176 | tf_op jit(solution)/shard_map/ppermute | solution.py:18
  (143 shorter events, 86.1 us)
Async XLA Ops:
  8.4 21.4 %collective-permute-start.9 = (bf16[2,2,128,512]{3,2,1,0:T(8,128)(2,1)S(1)}, bf16[2,2,128,512]{3,2,1,0:T(8,128)(2,1)S(1)}, u32[]{:S(2)}, u32[]{:S(2)}) collective-permute-start(bf16[2,2,128,512]{3,2,1,0:T(8,128)(2,1)S(1)} %pad_maximum_fusion.refs_0_), channel_id=1, source_target_pairs={{0,4},{4,0},{8,12},{12,8},{16,20},{20,16},{24,28},{28,24},{32,36},... | collective-permute-start | bytes 1572872 | tf_op jit(solution)/shard_map/ppermute | solution.py:18
  16.6 21.1 %collective-permute-start.5 = (bf16[2,2,128,512]{3,2,1,0:T(8,128)(2,1)S(1)}, bf16[2,2,128,512]{3,2,1,0:T(8,128)(2,1)S(1)}, u32[]{:S(2)}, u32[]{:S(2)}) collective-permute-start(bf16[2,2,128,512]{3,2,1,0:T(8,128)(2,1)S(1)} %pad_maximum_fusion.refs_0_), channel_id=1, source_target_pairs={{0,96},{4,100},{8,104},{12,108},{16,112},{20,116},{24,120},{28,124... | collective-permute-start | bytes 1572872 | tf_op jit(solution)/shard_map/ppermute | solution.py:27
  20.4 18.8 %collective-permute-start.3 = (bf16[2,2,128,512]{3,2,1,0:T(8,128)(2,1)S(1)}, bf16[2,2,128,512]{3,2,1,0:T(8,128)(2,1)S(1)}, u32[]{:S(2)}, u32[]{:S(2)}) collective-permute-start(bf16[2,2,128,512]{3,2,1,0:T(8,128)(2,1)S(1)} %pad_maximum_fusion.refs_0_), channel_id=1, source_target_pairs={{0,32},{4,36},{8,40},{12,44},{16,48},{20,52},{24,56},{28,60},{32,6... | collective-permute-start | bytes 1572872 | tf_op jit(solution)/shard_map/ppermute | solution.py:27
  27.9 21.0 %collective-permute-start.6 = (bf16[2,2,128,512]{3,2,1,0:T(8,128)(2,1)S(1)}, bf16[2,2,128,512]{3,2,1,0:T(8,128)(2,1)S(1)}, u32[]{:S(2)}, u32[]{:S(2)}) collective-permute-start(bf16[2,2,128,512]{3,2,1,0:T(8,128)(2,1)S(1)} %constant_dynamic-update-slice_fusion.refs_1_), channel_id=1, source_target_pairs={{0,96},{4,100},{8,104},{12,108},{16,112},{20,116},{24,120},{28,124... | collective-permute-start | bytes 1572872 | tf_op jit(solution)/shard_map/ppermute | solution.py:27
  29.8 20.0 %collective-permute-start.4 = (bf16[2,2,128,512]{3,2,1,0:T(8,128)(2,1)S(1)}, bf16[2,2,128,512]{3,2,1,0:T(8,128)(2,1)S(1)}, u32[]{:S(2)}, u32[]{:S(2)}) collective-permute-start(bf16[2,2,128,512]{3,2,1,0:T(8,128)(2,1)S(1)} %constant_dynamic-update-slice_fusion.refs_1_), channel_id=1, source_target_pairs={{0,32},{4,36},{8,40},{12,44},{16,48},{20,52},{24,56},{28,60},{32,6... | collective-permute-start | bytes 1572872 | tf_op jit(solution)/shard_map/ppermute | solution.py:27
  39.2 14.8 %collective-permute-start.31 = (bf16[2,2,128,512]{3,2,1,0:T(8,128)(2,1)S(1)}, bf16[2,2,128,512]{3,2,1,0:T(8,128)(2,1)S(1)}, u32[]{:S(2)}, u32[]{:S(2)}) collective-permute-start(bf16[2,2,128,512]{3,2,1,0:T(8,128)(2,1)S(1)} %pad_maximum_fusion.1.refs_0_), channel_id=1, source_target_pairs={{0,24},{4,28},{8,0},{12,4},{16,8},{20,12},{24,16},{28,20},{32,56},... | collective-permute-start | bytes 1572872 | tf_op jit(solution)/shard_map/ppermute | solution.py:27
  39.9 15.5 %collective-permute-start.29 = (bf16[2,2,128,512]{3,2,1,0:T(8,128)(2,1)S(1)}, bf16[2,2,128,512]{3,2,1,0:T(8,128)(2,1)S(1)}, u32[]{:S(2)}, u32[]{:S(2)}) collective-permute-start(bf16[2,2,128,512]{3,2,1,0:T(8,128)(2,1)S(1)} %pad_maximum_fusion.1.refs_0_), channel_id=1, source_target_pairs={{0,8},{4,12},{8,16},{12,20},{16,24},{20,28},{24,0},{28,4},{32,40},... | collective-permute-start | bytes 1572872 | tf_op jit(solution)/shard_map/ppermute | solution.py:27
  49.9 15.4 %collective-permute-start.32 = (bf16[2,2,128,512]{3,2,1,0:T(8,128)(2,1)S(1)}, bf16[2,2,128,512]{3,2,1,0:T(8,128)(2,1)S(1)}, u32[]{:S(2)}, u32[]{:S(2)}) collective-permute-start(bf16[2,2,128,512]{3,2,1,0:T(8,128)(2,1)S(1)} %constant_dynamic-update-slice_fusion.2.refs_1_), channel_id=1, source_target_pairs={{0,24},{4,28},{8,0},{12,4},{16,8},{20,12},{24,16},{28,20},{32,56},... | collective-permute-start | bytes 1572872 | tf_op jit(solution)/shard_map/ppermute | solution.py:27
  50.4 16.8 %collective-permute-start.30 = (bf16[2,2,128,512]{3,2,1,0:T(8,128)(2,1)S(1)}, bf16[2,2,128,512]{3,2,1,0:T(8,128)(2,1)S(1)}, u32[]{:S(2)}, u32[]{:S(2)}) collective-permute-start(bf16[2,2,128,512]{3,2,1,0:T(8,128)(2,1)S(1)} %constant_dynamic-update-slice_fusion.2.refs_1_), channel_id=1, source_target_pairs={{0,8},{4,12},{8,16},{12,20},{16,24},{20,28},{24,0},{28,4},{32,40},... | collective-permute-start | bytes 1572872 | tf_op jit(solution)/shard_map/ppermute | solution.py:27
  77.9 40.4 %collective-permute-start.18 = (bf16[1,1,14,2,128,256]{5,4,3,2,1,0:T(8,128)(2,1)}, bf16[1,1,14,2,128,256]{5,4,3,2,1,0:T(8,128)(2,1)S(1)}, u32[]{:S(2)}, u32[]{:S(2)}) collective-permute-start(bf16[1,1,14,2,128,256]{5,4,3,2,1,0:T(8,128)(2,1)} %refs_0_.9), channel_id=1, source_target_pairs={{0,1},{1,0},{2,3},{3,2},{4,5},{5,4},{6,7},{7,6},{8,9},{9,8},{10,11... | collective-permute-start | bytes 5505032 | tf_op jit(solution)/shard_map/ppermute | solution.py:18
  91.3 36.8 %collective-permute-start.47 = (bf16[14,2,64,128]{3,2,1,0:T(8,128)(2,1)S(1)}, bf16[14,2,64,128]{3,2,1,0:T(8,128)(2,1)S(1)}, u32[]{:S(2)}, u32[]{:S(2)}) collective-permute-start(bf16[14,2,64,128]{3,2,1,0:T(8,128)(2,1)S(1)} %shard_map.108.own), channel_id=1, source_target_pairs={{0,1},{1,0},{2,3},{3,2},{4,5},{5,4},{6,7},{7,6},{8,9},{9,8},{10,11... | collective-permute-start | bytes 1376264 | tf_op jit(solution)/shard_map/ppermute | solution.py:18
  95.3 42.7 %collective-permute-start.17 = (bf16[7,2,128,128]{3,2,1,0:T(8,128)(2,1)S(1)}, bf16[7,2,128,128]{3,2,1,0:T(8,128)(2,1)S(1)}, u32[]{:S(2)}, u32[]{:S(2)}) collective-permute-start(bf16[7,2,128,128]{3,2,1,0:T(8,128)(2,1)S(1)} %shard_map.91.own), channel_id=1, source_target_pairs={{0,1},{1,0},{2,3},{3,2},{4,5},{5,4},{6,7},{7,6},{8,9},{9,8},{10,11... | collective-permute-start | bytes 1376264 | tf_op jit(solution)/shard_map/ppermute | solution.py:18
  97.6 50.1 %collective-permute-start.20 = (bf16[7,2,128,128]{3,2,1,0:T(8,128)(2,1)S(1)}, bf16[7,2,128,128]{3,2,1,0:T(8,128)(2,1)S(1)}, u32[]{:S(2)}, u32[]{:S(2)}) collective-permute-start(bf16[7,2,128,128]{3,2,1,0:T(8,128)(2,1)S(1)} %shard_map.95.own), channel_id=1, source_target_pairs={{0,1},{1,0},{2,3},{3,2},{4,5},{5,4},{6,7},{7,6},{8,9},{9,8},{10,11... | collective-permute-start | bytes 1376264 | tf_op jit(solution)/shard_map/ppermute | solution.py:18
  102.7 54.9 %collective-permute-start.43 = (bf16[14,2,64,128]{3,2,1,0:T(8,128)(2,1)S(1)}, bf16[14,2,64,128]{3,2,1,0:T(8,128)(2,1)S(1)}, u32[]{:S(2)}, u32[]{:S(2)}) collective-permute-start(bf16[14,2,64,128]{3,2,1,0:T(8,128)(2,1)S(1)} %shard_map.102.own), channel_id=1, source_target_pairs={{0,1},{1,0},{2,3},{3,2},{4,5},{5,4},{6,7},{7,6},{8,9},{9,8},{10,11... | collective-permute-start | bytes 1376264 | tf_op jit(solution)/shard_map/ppermute | solution.py:18
  129.4 37.5 %collective-permute-start.48 = (bf16[14,2,64,128]{3,2,1,0:T(8,128)(2,1)S(1)}, bf16[14,2,64,128]{3,2,1,0:T(8,128)(2,1)S(1)}, u32[]{:S(2)}, u32[]{:S(2)}) collective-permute-start(bf16[14,2,64,128]{3,2,1,0:T(8,128)(2,1)S(1)} %shard_map.110), channel_id=1, source_target_pairs={{0,3},{1,2},{2,1},{3,0},{4,7},{5,6},{6,5},{7,4},{8,11},{9,10},{10,... | collective-permute-start | bytes 1376264 | tf_op jit(solution)/shard_map/ppermute | solution.py:18
  139.0 34.1 %collective-permute-start.19 = (bf16[7,2,128,128]{3,2,1,0:T(8,128)(2,1)S(1)}, bf16[7,2,128,128]{3,2,1,0:T(8,128)(2,1)S(1)}, u32[]{:S(2)}, u32[]{:S(2)}) collective-permute-start(bf16[7,2,128,128]{3,2,1,0:T(8,128)(2,1)S(1)} %shard_map.93), channel_id=1, source_target_pairs={{0,3},{1,2},{2,1},{3,0},{4,7},{5,6},{6,5},{7,4},{8,11},{9,10},{10,... | collective-permute-start | bytes 1376264 | tf_op jit(solution)/shard_map/ppermute | solution.py:18
  148.8 27.3 %collective-permute-start.21 = (bf16[7,2,128,128]{3,2,1,0:T(8,128)(2,1)S(1)}, bf16[7,2,128,128]{3,2,1,0:T(8,128)(2,1)S(1)}, u32[]{:S(2)}, u32[]{:S(2)}) collective-permute-start(bf16[7,2,128,128]{3,2,1,0:T(8,128)(2,1)S(1)} %shard_map.97), channel_id=1, source_target_pairs={{0,3},{1,2},{2,1},{3,0},{4,7},{5,6},{6,5},{7,4},{8,11},{9,10},{10,... | collective-permute-start | bytes 1376264 | tf_op jit(solution)/shard_map/ppermute | solution.py:18
  158.9 24.1 %collective-permute-start.44 = (bf16[14,2,64,128]{3,2,1,0:T(8,128)(2,1)S(1)}, bf16[14,2,64,128]{3,2,1,0:T(8,128)(2,1)S(1)}, u32[]{:S(2)}, u32[]{:S(2)}) collective-permute-start(bf16[14,2,64,128]{3,2,1,0:T(8,128)(2,1)S(1)} %shard_map.104), channel_id=1, source_target_pairs={{0,3},{1,2},{2,1},{3,0},{4,7},{5,6},{6,5},{7,4},{8,11},{9,10},{10,... | collective-permute-start | bytes 1376264 | tf_op jit(solution)/shard_map/ppermute | solution.py:18
  162.4 24.9 %collective-permute-start.24 = (bf16[2,256,256]{2,1,0:T(8,128)(2,1)S(1)}, bf16[2,256,256]{2,1,0:T(8,128)(2,1)S(1)}, u32[]{:S(2)}, u32[]{:S(2)}) collective-permute-start(bf16[2,256,256]{2,1,0:T(8,128)(2,1)S(1)} %get-tuple-element.21), channel_id=1, source_target_pairs={{1,0},{2,1},{3,2},{4,3},{5,4},{6,5},{7,6},{8,7},{9,8},{10,9},{11,1... | collective-permute-start | bytes 786440 | tf_op jit(solution)/shard_map/ppermute | solution.py:297
  167.0 20.3 %collective-permute-start.23 = (bf16[2,256,256]{2,1,0:T(8,128)(2,1)S(1)}, bf16[2,256,256]{2,1,0:T(8,128)(2,1)S(1)}, u32[]{:S(2)}, u32[]{:S(2)}) collective-permute-start(bf16[2,256,256]{2,1,0:T(8,128)(2,1)S(1)} %get-tuple-element.22), channel_id=1, source_target_pairs={{0,1},{1,2},{2,3},{3,4},{4,5},{5,6},{6,7},{7,8},{8,9},{9,10},{10,1... | collective-permute-start | bytes 786440 | tf_op jit(solution)/shard_map/ppermute | solution.py:296
  173.0 29.1 %collective-permute-start.50 = (bf16[1,2,64,512]{3,2,1,0:T(8,128)(2,1)S(1)}, bf16[1,2,64,512]{3,2,1,0:T(8,128)(2,1)S(1)}, u32[]{:S(2)}, u32[]{:S(2)}) collective-permute-start(bf16[1,2,64,512]{3,2,1,0:T(8,128)(2,1)S(1)} %get-tuple-element.16), channel_id=1, source_target_pairs={{0,1},{1,0},{2,3},{3,2},{4,5},{5,4},{6,7},{7,6},{8,9},{9,8},{10,11... | collective-permute-start | bytes 393224 | tf_op jit(solution)/shard_map/ppermute | solution.py:18
  179.9 26.0 %collective-permute-start.22 = (bf16[2,2,128,512]{3,2,1,0:T(8,128)(2,1)S(1)}, bf16[2,2,128,512]{3,2,1,0:T(8,128)(2,1)S(1)}, u32[]{:S(2)}, u32[]{:S(2)}) collective-permute-start(bf16[2,2,128,512]{3,2,1,0:T(8,128)(2,1)S(1)} %get-tuple-element.12), channel_id=1, source_target_pairs={{0,1},{1,0},{2,3},{3,2},{4,5},{5,4},{6,7},{7,6},{8,9},{9,8},{10,11... | collective-permute-start | bytes 1572872 | tf_op jit(solution)/shard_map/ppermute | solution.py:18
  187.2 18.6 %collective-permute-start.45 = (bf16[2,2,64,512]{3,2,1,0:T(8,128)(2,1)S(1)}, bf16[2,2,64,512]{3,2,1,0:T(8,128)(2,1)S(1)}, u32[]{:S(2)}, u32[]{:S(2)}) collective-permute-start(bf16[2,2,64,512]{3,2,1,0:T(8,128)(2,1)S(1)} %get-tuple-element.14), channel_id=1, source_target_pairs={{0,1},{1,0},{2,3},{3,2},{4,5},{5,4},{6,7},{7,6},{8,9},{9,8},{10,11... | collective-permute-start | bytes 786440 | tf_op jit(solution)/shard_map/ppermute | solution.py:18
  202.2 15.9 %collective-permute-start.51 = (bf16[2,64,512]{2,1,0:T(8,128)(2,1)S(1)}, bf16[2,64,512]{2,1,0:T(8,128)(2,1)S(1)}, u32[]{:S(2)}, u32[]{:S(2)}) collective-permute-start(bf16[2,64,512]{2,1,0:T(8,128)(2,1)S(1)} %fusion.6), channel_id=1, source_target_pairs={{0,3},{1,2},{2,1},{3,0},{4,7},{5,6},{6,5},{7,4},{8,11},{9,10},{10,... | collective-permute-start | bytes 393224 | tf_op jit(solution)/shard_map/ppermute | solution.py:18
  (40 other events, 820.7 us)
